TPU v7x, 32 devices: a whole 2x2x4 slice. The times are simulated.
32 devices in a mesh: dp: 4 (over y, core), seq: 8 (over z, x).
Axes of the slice: x: 2, y: 2, z: 4, core: 2. Of those that a mesh axis runs over, the one named last changes fastest.
Arguments:
- tokens: bfloat16 [8, 4096, 768], P('dp', 'seq'), may hold values from -6 to 6
- encoder_states: bfloat16 [8, 256, 768], P('dp', 'seq'), may hold values from -6 to 6
- out_grad: bfloat16 [8, 4096, 768], P('dp', 'seq'), may hold values from -6 to 6
- block_map: int32 [8, 32], P('dp'), may hold values from 0 to 31, each once within a row
- branch_fork: int32 [8, 8], P('dp'), may hold values from 512 to 2048
- norm_gain: bfloat16 [3, 768], P(None, ('dp', 'seq')), may hold values from 0.5 to 1.5
- norm_bias: bfloat16 [3, 768], P(None, ('dp', 'seq')), may hold values from -1.75 to 1.75
- self_in: bfloat16 [3, 768, 768], P(None, ('dp', 'seq')), may hold values from -0.21875 to 0.21875
- self_out: bfloat16 [768, 768], P(('dp', 'seq')), may hold values from -1.75 to 1.75
- self_bias: bfloat16 [3, 768], P(None, ('dp', 'seq')), may hold values from -0.3125 to 0.3125
- cross_in: bfloat16 [3, 768, 768], P(None, ('dp', 'seq')), may hold values from -0.21875 to 0.21875
- cross_out: bfloat16 [768, 768], P(('dp', 'seq')), may hold values from -1.75 to 1.75
- cross_bias: bfloat16 [3, 768], P(None, ('dp', 'seq')), may hold values from -0.3125 to 0.3125
- up_weight: bfloat16 [768, 3072], P(('dp', 'seq')), may hold values from -0.21875 to 0.21875
- up_bias: bfloat16 [3072], P(('dp', 'seq')), may hold values from -3 to 3
- down_weight: bfloat16 [3072, 768], P(('dp', 'seq')), may hold values from -0.109375 to 0.109375
- down_bias: bfloat16 [768], P(('dp', 'seq')), may hold values from -1.25 to 1.25
Outputs:
- activations: bfloat16 [8, 4096, 768], P('dp', 'seq')
- tokens_grad: float32 [8, 4096, 768], P('dp', 'seq')
- encoder_grad: float32 [8, 256, 768], P('dp', 'seq')
- norm_gain_grad: float32 [3, 768], P(None, ('dp', 'seq'))
- norm_bias_grad: float32 [3, 768], P(None, ('dp', 'seq'))
- self_in_grad: float32 [3, 768, 768], P(None, ('dp', 'seq'))
- self_out_grad: float32 [768, 768], P(('dp', 'seq'))
- self_bias_grad: float32 [3, 768], P(None, ('dp', 'seq'))
- cross_in_grad: float32 [3, 768, 768], P(None, ('dp', 'seq'))
- cross_out_grad: float32 [768, 768], P(('dp', 'seq'))
- cross_bias_grad: float32 [3, 768], P(None, ('dp', 'seq'))
- up_weight_grad: float32 [768, 3072], P(('dp', 'seq'))
- up_bias_grad: float32 [3072], P(('dp', 'seq'))
- down_weight_grad: float32 [3072, 768], P(('dp', 'seq'))
- down_bias_grad: float32 [768], P(('dp', 'seq'))
Inputs may be any that keep to these rules, and one draw needn't show every extreme that they name: Each row of block_map is a permutation of the group's 32 logical blocks.
All inputs are finite; a program needn't handle non-finite values.
Results may differ from a plain program's by a relative error of at most 0.02.
Values may be sent and summed in bfloat16 or wider, within the bound.
No kernel may reach another device: no remote copies, remote signals or barrier semaphores. Data moves between devices by JAX's collectives and lax.ppermute only.
A program may use at most 576 MiB of HBM per device.

v0:
```python
import jax
import jax.numpy as jnp
from jax import lax
from jax.sharding import PartitionSpec as P

HEADS = 12
HEAD = 64
PROMPT = 2048
BRANCHES = 8
BLEN = 256
BLOCK = 128


def product(former, latter):
    return jnp.dot(former, latter, preferred_element_type=jnp.float32)


def product_left(former, latter):
    return lax.dot_general(
        former, latter, (((0,), (0,)), ((), ())), preferred_element_type=jnp.float32
    )


def product_right(former, latter):
    return lax.dot_general(
        former, latter, (((1,), (1,)), ((), ())), preferred_element_type=jnp.float32
    )


def column_sum(matrix):
    return jnp.sum(matrix.astype(jnp.float32), axis=0)


def norm_layer(stream, norm_gain, norm_shift):
    center = jnp.mean(stream, axis=-1, keepdims=True)
    centered = stream - center
    spread = jnp.mean(centered * centered, axis=-1, keepdims=True)
    return centered * lax.rsqrt(spread + 1e-05) * norm_gain + norm_shift


def gelu_exact(before):
    return jax.nn.gelu(before, approximate=False)


def token_info(blocks, branch_forks):
    offsets = jnp.arange(BLOCK, dtype=jnp.int32)
    logical = (blocks[:, None] * BLOCK + offsets[None, :]).reshape(-1)
    relative = logical - PROMPT
    in_branch = relative >= 0
    segment = jnp.where(in_branch, relative // BLEN + 1, 0)
    position = jnp.where(in_branch, relative % BLEN, logical)
    labels = jnp.arange(1, BRANCHES + 1, dtype=jnp.int32)
    fork_reach = jnp.sum(
        jnp.where(segment[:, None] == labels[None, :], branch_forks[None, :], 0), axis=1
    )
    return (segment, position, fork_reach)


def allowed(query_info, key_info):
    same = (query_info[0][:, None] == key_info[0][None, :]) & (
        key_info[1][None, :] <= query_info[1][:, None]
    )
    shared = (
        (query_info[0][:, None] > 0)
        & (key_info[0][None, :] == 0)
        & (key_info[1][None, :] < query_info[2][:, None])
    )
    return same | shared


def head_split(matrix):
    return matrix.reshape(matrix.shape[0], HEADS, HEAD)


def score_block(queries, key_rows, key_mask):
    scores = jnp.einsum(
        "rhd,khd->hrk",
        head_split(queries),
        head_split(key_rows),
        preferred_element_type=jnp.float32,
    ) * HEAD ** (-0.5)
    if key_mask is None:
        return scores
    return jnp.where(key_mask[None], scores, -1e30)


def attend_forward(queries, key_rows, value_rows, key_mask):
    scores = score_block(queries, key_rows, key_mask)
    row_max = jnp.max(scores, axis=2, keepdims=True)
    weights = jnp.exp(scores - row_max)
    row_total = jnp.sum(weights, axis=2, keepdims=True)
    shares = (weights / row_total).astype(jnp.bfloat16)
    attended = jnp.einsum(
        "hrk,khd->rhd", shares, head_split(value_rows), preferred_element_type=jnp.float32
    )
    return (attended.reshape(queries.shape[0], -1).astype(jnp.bfloat16), row_max, row_total)


def attend_backward(queries, key_rows, value_rows, key_mask, row_max, row_total, incoming):
    scores = score_block(queries, key_rows, key_mask)
    shares_full = jnp.exp(scores - row_max) / row_total
    shares_low = shares_full.astype(jnp.bfloat16)
    grad_heads = head_split(incoming)
    grad_values = jnp.einsum(
        "hrk,rhd->khd", shares_low, grad_heads, preferred_element_type=jnp.float32
    )
    grad_shares = jnp.einsum(
        "rhd,khd->hrk", grad_heads, head_split(value_rows), preferred_element_type=jnp.float32
    )
    inner_sum = jnp.sum(grad_shares * shares_full, axis=2, keepdims=True)
    grad_scores = (shares_full * (grad_shares - inner_sum)).astype(jnp.bfloat16)
    grad_queries = jnp.einsum(
        "hrk,khd->rhd", grad_scores, head_split(key_rows), preferred_element_type=jnp.float32
    ) * HEAD ** (-0.5)
    grad_keys = jnp.einsum(
        "hrk,rhd->khd", grad_scores, head_split(queries), preferred_element_type=jnp.float32
    ) * HEAD ** (-0.5)
    row_count = queries.shape[0]
    key_count = key_rows.shape[0]
    return (
        grad_queries.reshape(row_count, -1),
        grad_keys.reshape(key_count, -1),
        grad_values.reshape(key_count, -1),
    )


def fetch_self(shards):
    return (
        lax.all_gather(shards[0][0], ("dp", "seq"), axis=0, tiled=True),
        lax.all_gather(shards[1][0], ("dp", "seq"), axis=0, tiled=True),
        lax.all_gather(shards[2], ("dp", "seq"), axis=1, tiled=True),
        lax.all_gather(shards[3], ("dp", "seq"), axis=0, tiled=True),
        lax.all_gather(shards[4], ("dp", "seq"), axis=1, tiled=True),
    )


def fetch_cross(shards):
    return (
        lax.all_gather(shards[0][1], ("dp", "seq"), axis=0, tiled=True),
        lax.all_gather(shards[1][1], ("dp", "seq"), axis=0, tiled=True),
        lax.all_gather(shards[5], ("dp", "seq"), axis=1, tiled=True),
        lax.all_gather(shards[6], ("dp", "seq"), axis=0, tiled=True),
        lax.all_gather(shards[7], ("dp", "seq"), axis=1, tiled=True),
    )


def fetch_feed(shards):
    return (
        lax.all_gather(shards[0][2], ("dp", "seq"), axis=0, tiled=True),
        lax.all_gather(shards[1][2], ("dp", "seq"), axis=0, tiled=True),
        lax.all_gather(shards[8], ("dp", "seq"), axis=0, tiled=True),
        lax.all_gather(shards[9], ("dp", "seq"), axis=0, tiled=True),
        lax.all_gather(shards[10], ("dp", "seq"), axis=0, tiled=True),
        lax.all_gather(shards[11], ("dp", "seq"), axis=0, tiled=True),
    )


def body(
    tokens,
    encoder_states,
    out_grad,
    block_map,
    branch_fork,
    norm_gain,
    norm_bias,
    self_in,
    self_out,
    self_bias,
    cross_in,
    cross_out,
    cross_bias,
    up_weight,
    up_bias,
    down_weight,
    down_bias,
):
    shards = (
        norm_gain,
        norm_bias,
        self_in,
        self_out,
        self_bias,
        cross_in,
        cross_out,
        cross_bias,
        up_weight,
        up_bias,
        down_weight,
        down_bias,
    )
    model_width = tokens.shape[2]
    hidden_width = up_weight.shape[1]
    seq_count = lax.axis_size("seq")
    seq_place = lax.axis_index("seq")

    def micro_step(grad_sums, inputs):
        tokens_in, encoded, cotangent, blocks, branch_forks = inputs
        slot_count = blocks.shape[0] // seq_count
        own_blocks = lax.dynamic_slice_in_dim(blocks, seq_place * slot_count, slot_count)
        query_info = token_info(own_blocks, branch_forks)
        full_info = token_info(blocks, branch_forks)
        key_mask = allowed(query_info, full_info)
        gain_first, shift_first, attend_in, attend_out, attend_bias = fetch_self(shards)
        stream = tokens_in.astype(jnp.float32)
        norm_full, pull_first = jax.vjp(
            norm_layer, stream, gain_first.astype(jnp.float32), shift_first.astype(jnp.float32)
        )
        norm_first = norm_full.astype(jnp.bfloat16)
        queries = (product(norm_first, attend_in[0]) + attend_bias[0].astype(jnp.float32)).astype(
            jnp.bfloat16
        )
        key_local = product(norm_first, attend_in[1]).astype(jnp.bfloat16)
        value_local = (
            product(norm_first, attend_in[2]) + attend_bias[1].astype(jnp.float32)
        ).astype(jnp.bfloat16)
        key_rows, value_rows = (
            lax.all_gather(key_local, "seq", axis=0, tiled=True),
            lax.all_gather(value_local, "seq", axis=0, tiled=True),
        )
        attended, self_max, self_total = attend_forward(queries, key_rows, value_rows, key_mask)
        middle = stream + product(attended, attend_out) + attend_bias[2].astype(jnp.float32)
        gain_second, shift_second, cross_proj, cross_back, cross_shift = fetch_cross(shards)
        cross_key_local = product(encoded, cross_proj[1]).astype(jnp.bfloat16)
        cross_value_local = (
            product(encoded, cross_proj[2]) + cross_shift[1].astype(jnp.float32)
        ).astype(jnp.bfloat16)
        cross_keys, cross_values = (
            lax.all_gather(cross_key_local, "seq", axis=0, tiled=True),
            lax.all_gather(cross_value_local, "seq", axis=0, tiled=True),
        )
        norm_full_second, pull_second = jax.vjp(
            norm_layer, middle, gain_second.astype(jnp.float32), shift_second.astype(jnp.float32)
        )
        norm_second = norm_full_second.astype(jnp.bfloat16)
        cross_queries = (
            product(norm_second, cross_proj[0]) + cross_shift[0].astype(jnp.float32)
        ).astype(jnp.bfloat16)
        cross_attended, cross_max, cross_total = attend_forward(
            cross_queries, cross_keys, cross_values, None
        )
        after_cross = (
            middle + product(cross_attended, cross_back) + cross_shift[2].astype(jnp.float32)
        )
        gain_third, shift_third, feed_up, feed_up_bias, feed_down, feed_down_bias = fetch_feed(
            shards
        )
        norm_full_third, pull_third = jax.vjp(
            norm_layer, after_cross, gain_third.astype(jnp.float32), shift_third.astype(jnp.float32)
        )
        norm_third = norm_full_third.astype(jnp.bfloat16)
        before = product(norm_third, feed_up) + feed_up_bias.astype(jnp.float32)
        activated_full, gelu_pull = jax.vjp(gelu_exact, before)
        activated = activated_full.astype(jnp.bfloat16)
        result = after_cross + product(activated, feed_down) + feed_down_bias.astype(jnp.float32)
        gain_third, shift_third, feed_up, feed_up_bias, feed_down, feed_down_bias = fetch_feed(
            shards
        )
        cot_float = cotangent.astype(jnp.float32)
        grad_act = product_right(cotangent, feed_down)
        grad_down = product_left(activated, cotangent)
        grad_down_bias = jnp.sum(cot_float, axis=0)
        grad_before = gelu_pull(grad_act)[0].astype(jnp.bfloat16)
        grad_up = product_left(norm_third, grad_before)
        grad_up_bias = column_sum(grad_before)
        grad_third = product_right(grad_before, feed_up)
        grad_after_norm, grad_gain_third, grad_shift_third = pull_third(grad_third)
        grad_after = cot_float + grad_after_norm
        gain_second, shift_second, cross_proj, cross_back, cross_shift = fetch_cross(shards)
        grad_after_low = grad_after.astype(jnp.bfloat16)
        grad_cross_back = product_left(cross_attended, grad_after_low)
        grad_cross_out_bias = column_sum(grad_after_low)
        grad_cross_attended = product_right(grad_after_low, cross_back).astype(jnp.bfloat16)
        grad_cross_queries, grad_cross_keys, grad_cross_values = attend_backward(
            cross_queries,
            cross_keys,
            cross_values,
            None,
            cross_max,
            cross_total,
            grad_cross_attended,
        )
        cross_key_part, cross_value_part = (
            lax.psum_scatter(
                grad_cross_keys.astype(jnp.bfloat16), "seq", scatter_dimension=0, tiled=True
            ).astype(jnp.float32),
            lax.psum_scatter(
                grad_cross_values.astype(jnp.bfloat16), "seq", scatter_dimension=0, tiled=True
            ).astype(jnp.float32),
        )
        cross_key_low = cross_key_part.astype(jnp.bfloat16)
        cross_value_low = cross_value_part.astype(jnp.bfloat16)
        cross_query_low = grad_cross_queries.astype(jnp.bfloat16)
        grad_cross_proj = jnp.stack(
            [
                product_left(norm_second, cross_query_low),
                product_left(encoded, cross_key_low),
                product_left(encoded, cross_value_low),
            ]
        )
        grad_cross_shift = jnp.stack(
            [column_sum(cross_query_low), column_sum(cross_value_low), grad_cross_out_bias]
        )
        encoder_grad = product_right(cross_key_low, cross_proj[1]) + product_right(
            cross_value_low, cross_proj[2]
        )
        grad_second = product_right(cross_query_low, cross_proj[0])
        grad_middle_norm, grad_gain_second, grad_shift_second = pull_second(grad_second)
        grad_middle = grad_after + grad_middle_norm
        gain_first, shift_first, attend_in, attend_out, attend_bias = fetch_self(shards)
        grad_middle_low = grad_middle.astype(jnp.bfloat16)
        grad_attend_out = product_left(attended, grad_middle_low)
        grad_out_bias = column_sum(grad_middle_low)
        grad_attended = product_right(grad_middle_low, attend_out).astype(jnp.bfloat16)
        grad_queries, grad_keys, grad_values = attend_backward(
            queries, key_rows, value_rows, key_mask, self_max, self_total, grad_attended
        )
        key_part, value_part = (
            lax.psum_scatter(
                grad_keys.astype(jnp.bfloat16), "seq", scatter_dimension=0, tiled=True
            ).astype(jnp.float32),
            lax.psum_scatter(
                grad_values.astype(jnp.bfloat16), "seq", scatter_dimension=0, tiled=True
            ).astype(jnp.float32),
        )
        key_low = key_part.astype(jnp.bfloat16)
        value_low = value_part.astype(jnp.bfloat16)
        query_low = grad_queries.astype(jnp.bfloat16)
        grad_attend_in = jnp.stack(
            [
                product_left(norm_first, query_low),
                product_left(norm_first, key_low),
                product_left(norm_first, value_low),
            ]
        )
        grad_attend_bias = jnp.stack([column_sum(query_low), column_sum(value_low), grad_out_bias])
        grad_first = (
            product_right(query_low, attend_in[0])
            + product_right(key_low, attend_in[1])
            + product_right(value_low, attend_in[2])
        )
        grad_stream_norm, grad_gain_first, grad_shift_first = pull_first(grad_first)
        tokens_grad = grad_middle + grad_stream_norm
        updates = (
            jnp.stack([grad_gain_first, grad_gain_second, grad_gain_third]),
            jnp.stack([grad_shift_first, grad_shift_second, grad_shift_third]),
            grad_attend_in,
            grad_attend_out,
            grad_attend_bias,
            grad_cross_proj,
            grad_cross_back,
            grad_cross_shift,
            grad_up,
            grad_up_bias,
            grad_down,
            grad_down_bias,
        )
        grad_sums = tuple((former + latter for former, latter in zip(grad_sums, updates)))
        return (grad_sums, (result.astype(jnp.bfloat16), tokens_grad, encoder_grad))

    starting = (
        jnp.zeros((3, model_width), jnp.float32),
        jnp.zeros((3, model_width), jnp.float32),
        jnp.zeros((3, model_width, model_width), jnp.float32),
        jnp.zeros((model_width, model_width), jnp.float32),
        jnp.zeros((3, model_width), jnp.float32),
        jnp.zeros((3, model_width, model_width), jnp.float32),
        jnp.zeros((model_width, model_width), jnp.float32),
        jnp.zeros((3, model_width), jnp.float32),
        jnp.zeros((model_width, hidden_width), jnp.float32),
        jnp.zeros((hidden_width,), jnp.float32),
        jnp.zeros((hidden_width, model_width), jnp.float32),
        jnp.zeros((model_width,), jnp.float32),
    )
    grad_sums, outputs = lax.scan(
        micro_step, starting, (tokens, encoder_states, out_grad, block_map, branch_fork)
    )
    feed_part = (
        lax.psum_scatter(grad_sums[8], ("dp", "seq"), scatter_dimension=0, tiled=True),
        lax.psum_scatter(grad_sums[9], ("dp", "seq"), scatter_dimension=0, tiled=True),
        lax.psum_scatter(grad_sums[10], ("dp", "seq"), scatter_dimension=0, tiled=True),
        lax.psum_scatter(grad_sums[11], ("dp", "seq"), scatter_dimension=0, tiled=True),
    )
    cross_part = (
        lax.psum_scatter(grad_sums[5], ("dp", "seq"), scatter_dimension=1, tiled=True),
        lax.psum_scatter(grad_sums[6], ("dp", "seq"), scatter_dimension=0, tiled=True),
        lax.psum_scatter(grad_sums[7], ("dp", "seq"), scatter_dimension=1, tiled=True),
    )
    self_part = (
        lax.psum_scatter(grad_sums[0], ("dp", "seq"), scatter_dimension=1, tiled=True),
        lax.psum_scatter(grad_sums[1], ("dp", "seq"), scatter_dimension=1, tiled=True),
        lax.psum_scatter(grad_sums[2], ("dp", "seq"), scatter_dimension=1, tiled=True),
        lax.psum_scatter(grad_sums[3], ("dp", "seq"), scatter_dimension=0, tiled=True),
        lax.psum_scatter(grad_sums[4], ("dp", "seq"), scatter_dimension=1, tiled=True),
    )
    return (
        outputs[0],
        outputs[1],
        outputs[2],
        self_part[0],
        self_part[1],
        self_part[2],
        self_part[3],
        self_part[4],
        cross_part[0],
        cross_part[1],
        cross_part[2],
        feed_part[0],
        feed_part[1],
        feed_part[2],
        feed_part[3],
    )


def solution(mesh):
    in_specs = (
        P("dp", "seq", None),
        P("dp", "seq", None),
        P("dp", "seq", None),
        P("dp", None),
        P("dp", None),
        P(None, ("dp", "seq")),
        P(None, ("dp", "seq")),
        P(None, ("dp", "seq"), None),
        P(("dp", "seq"), None),
        P(None, ("dp", "seq")),
        P(None, ("dp", "seq"), None),
        P(("dp", "seq"), None),
        P(None, ("dp", "seq")),
        P(("dp", "seq"), None),
        P(("dp", "seq")),
        P(("dp", "seq"), None),
        P(("dp", "seq")),
    )
    out_specs = (
        P("dp", "seq", None),
        P("dp", "seq", None),
        P("dp", "seq", None),
        P(None, ("dp", "seq")),
        P(None, ("dp", "seq")),
        P(None, ("dp", "seq"), None),
        P(("dp", "seq"), None),
        P(None, ("dp", "seq")),
        P(None, ("dp", "seq"), None),
        P(("dp", "seq"), None),
        P(None, ("dp", "seq")),
        P(("dp", "seq"), None),
        P(("dp", "seq")),
        P(("dp", "seq"), None),
        P(("dp", "seq")),
    )
    return jax.shard_map(body, mesh=mesh, in_specs=in_specs, out_specs=out_specs, check_vma=False)
```

profile of v0, /device:TPU:20, one launch (start us, length us, event | category | flops | bytes accessed | tf_op | source)
XLA Modules:
  0.0 2783.0 jit_solution(18066528006122591567)
XLA Ops:
  8.2 2025.1 %while.42 = (s32[]{:T(128)}, f32[3,768]{1,0:T(4,128)}, f32[3,768]{1,0:T(4,128)}, f32[3,768,768]{2,1,0:T(8,128)}, f32[768,768]{1,0:T(8,128)}, /*index=5*/f32[3,76...) while((s32[]{:T(128)}, f32[3,768]{1,0:T(4,128)}, ...), condition=%wide.region_38.39_spmd.clone, body=%wide.region_0.38_spmd.clone.sunk | while | flops 46778474496 | bytes 1825830656 | solution.py:374
  14.6 41.5 %all-reduce.25 = (bf16[768]{0:T(1024)(128)(2,1)S(1)}, bf16[768]{0:T(1024)(128)(2,1)S(1)}, bf16[768]{0:T(1024)(128)(2,1)S(1)}, bf16[768]{0:T(1024)(128)(2,1)S(1)}...) all-reduce(bf16[768]{0:T(1024)(128)(2,1)S(1)} %dynamic-update-slice, ...), channel_id=3, replica_groups=mesh['dp'=4,'seq'=8] {'dp','seq'}, use_global_device_ids=true, to_apply=%add.1 | all-reduce | flops 8448 | bytes 33792 | tf_op jit(solution)/shard_map/while
  75.5 62.4 %all-gather.13 = bf16[32,24,3]{1,2,0:T(4,128)(2,1)S(1)} all-gather(bf16[1,24,3]{1,2,0:T(4,128)(2,1)S(1)} %bitcast.585), channel_id=1, replica_groups=mesh['dp'=4,'seq'=8] {'dp','seq'}, dimensions={0}, use_global_device_ids=true | all-gather | bytes 4752 | tf_op jit(solution)/shard_map/while/body/eval_jaxpr/all_gather | solution.py:133
  148.0 66.6 %all-gather.12 = bf16[32,24,3]{1,2,0:T(4,128)(2,1)S(1)} all-gather(bf16[1,24,3]{1,2,0:T(4,128)(2,1)S(1)} %bitcast.586), channel_id=1, replica_groups=mesh['dp'=4,'seq'=8] {'dp','seq'}, dimensions={0}, use_global_device_ids=true | all-gather | bytes 4752 | tf_op jit(solution)/shard_map/while/body/eval_jaxpr/all_gather | solution.py:143
  304.4 44.6 %fusion.365 = (f32[12,512]{1,0:T(8,128)S(1)}, f32[12,512,4096]{2,1,0:T(8,128)}) fusion(pred[512,4096]{1,0:T(8,128)(4,1)S(1)} %copy-done.32, bf16[512,12,64]{0,2,1:T(8,128)(2,1)S(1)} %bitcast.561, bf16[4096,12,64]{0,2,1:T(8,128)(2,1)} %bitcast.552), kind=kOutput, calls=%fused_computation.250.clone.1 | convolution fusion | flops 3321892864 | bytes 109862912 | tf_op jit(solution)/shard_map/while/body/eval_jaxpr/sub | solution.py:101
  453.7 62.6 %all-gather.35.cloned.1.call-done = bf16[768,3072]{1,0:T(8,128)(2,1)} async-done(((bf16[24,3072]{1,0:T(8,128)(2,1)}), bf16[768,3072]{1,0:T(8,128)(2,1)}) %all-gather.35.cloned.1.call-update) | async-done | bytes 4718608 | tf_op jit(solution)/shard_map/while/body/eval_jaxpr/all_gather | solution.py:151
  536.0 45.2 %all-gather.37.cloned.1.call-done = bf16[3072,768]{1,0:T(8,128)(2,1)} async-done(((bf16[96,768]{1,0:T(8,128)(2,1)}), bf16[3072,768]{1,0:T(8,128)(2,1)}) %all-gather.37.cloned.1.call-update) | async-done | bytes 4718608 | tf_op jit(solution)/shard_map/while/body/eval_jaxpr/all_gather | solution.py:153
  631.3 66.9 %multiply_reduce_fusion.20 = (f32[12,512]{1,0:T(8,128)}, f32[12,512,4096]{2,1,0:T(8,128)}) fusion(f32[12,512,4096]{2,1,0:T(8,128)} %get-tuple-element.1113, f32[12,512]{1,0:T(8,128)S(1)} %copy-done.55, bf16[512,12,64]{0,2,1:T(8,128)(2,1)} %bitcast.574, bf16[4096,12,64]{0,2,1:T(8,128)(2,1)} %bitcast.557), kind=kOutput, calls=%fused_computation.3.clone.1 | convolution fusion | flops 3296716800 | bytes 208453632 | tf_op jit(solution)/shard_map/while/body/eval_jaxpr/rhd,khd->hrk/dot_general | solution.py:107
  737.3 80.1 %multiply_convert_fusion.12 = bf16[12,512,4096]{2,1,0:T(8,128)(2,1)} fusion(f32[12,512,4096]{2,1,0:T(8,128)} %get-tuple-element.1146, f32[12,512]{1,0:T(8,128)S(1)} %copy-done.59, f32[12,512,4096]{2,1,0:T(8,128)} %get-tuple-element.1113, f32[12,512]{1,0:T(8,128)S(1)} %copy-done.56), kind=kLoop, calls=%fused_computation.2.clone.1 | loop fusion | flops 100663296 | bytes 251707392 | tf_op jit(solution)/shard_map/while/body/eval_jaxpr/convert_element_type | solution.py:111
  908.3 96.1 %reduce-scatter.37.cloned.1.call-done = bf16[512,768]{0,1:T(8,128)(2,1)} async-done(((bf16[4096,768]{0,1:T(8,128)(2,1)}), bf16[512,768]{0,1:T(8,128)(2,1)}) %reduce-scatter.37.cloned.1.call-update) | async-done | bytes 786448 | tf_op jit(solution)/shard_map/while/body/eval_jaxpr/reduce_scatter | solution.py:318
  1086.7 62.4 %all-gather.13 = bf16[32,24,3]{1,2,0:T(4,128)(2,1)S(1)} all-gather(bf16[1,24,3]{1,2,0:T(4,128)(2,1)S(1)} %bitcast.585), channel_id=1, replica_groups=mesh['dp'=4,'seq'=8] {'dp','seq'}, dimensions={0}, use_global_device_ids=true | all-gather | bytes 4752 | tf_op jit(solution)/shard_map/while/body/eval_jaxpr/all_gather | solution.py:133
  1158.9 66.4 %all-gather.12 = bf16[32,24,3]{1,2,0:T(4,128)(2,1)S(1)} all-gather(bf16[1,24,3]{1,2,0:T(4,128)(2,1)S(1)} %bitcast.586), channel_id=1, replica_groups=mesh['dp'=4,'seq'=8] {'dp','seq'}, dimensions={0}, use_global_device_ids=true | all-gather | bytes 4752 | tf_op jit(solution)/shard_map/while/body/eval_jaxpr/all_gather | solution.py:143
  1315.0 44.6 %fusion.365 = (f32[12,512]{1,0:T(8,128)S(1)}, f32[12,512,4096]{2,1,0:T(8,128)}) fusion(pred[512,4096]{1,0:T(8,128)(4,1)S(1)} %copy-done.32, bf16[512,12,64]{0,2,1:T(8,128)(2,1)S(1)} %bitcast.561, bf16[4096,12,64]{0,2,1:T(8,128)(2,1)} %bitcast.552), kind=kOutput, calls=%fused_computation.250.clone.1 | convolution fusion | flops 3321892864 | bytes 109862912 | tf_op jit(solution)/shard_map/while/body/eval_jaxpr/sub | solution.py:101
  1464.5 62.6 %all-gather.35.cloned.1.call-done = bf16[768,3072]{1,0:T(8,128)(2,1)} async-done(((bf16[24,3072]{1,0:T(8,128)(2,1)}), bf16[768,3072]{1,0:T(8,128)(2,1)}) %all-gather.35.cloned.1.call-update) | async-done | bytes 4718608 | tf_op jit(solution)/shard_map/while/body/eval_jaxpr/all_gather | solution.py:151
  1546.8 45.2 %all-gather.37.cloned.1.call-done = bf16[3072,768]{1,0:T(8,128)(2,1)} async-done(((bf16[96,768]{1,0:T(8,128)(2,1)}), bf16[3072,768]{1,0:T(8,128)(2,1)}) %all-gather.37.cloned.1.call-update) | async-done | bytes 4718608 | tf_op jit(solution)/shard_map/while/body/eval_jaxpr/all_gather | solution.py:153
  1642.2 66.7 %multiply_reduce_fusion.20 = (f32[12,512]{1,0:T(8,128)}, f32[12,512,4096]{2,1,0:T(8,128)}) fusion(f32[12,512,4096]{2,1,0:T(8,128)} %get-tuple-element.1113, f32[12,512]{1,0:T(8,128)S(1)} %copy-done.55, bf16[512,12,64]{0,2,1:T(8,128)(2,1)} %bitcast.574, bf16[4096,12,64]{0,2,1:T(8,128)(2,1)} %bitcast.557), kind=kOutput, calls=%fused_computation.3.clone.1 | convolution fusion | flops 3296716800 | bytes 208453632 | tf_op jit(solution)/shard_map/while/body/eval_jaxpr/rhd,khd->hrk/dot_general | solution.py:107
  1748.0 80.1 %multiply_convert_fusion.12 = bf16[12,512,4096]{2,1,0:T(8,128)(2,1)} fusion(f32[12,512,4096]{2,1,0:T(8,128)} %get-tuple-element.1146, f32[12,512]{1,0:T(8,128)S(1)} %copy-done.59, f32[12,512,4096]{2,1,0:T(8,128)} %get-tuple-element.1113, f32[12,512]{1,0:T(8,128)S(1)} %copy-done.56), kind=kLoop, calls=%fused_computation.2.clone.1 | loop fusion | flops 100663296 | bytes 251707392 | tf_op jit(solution)/shard_map/while/body/eval_jaxpr/convert_element_type | solution.py:111
  1926.0 89.2 %reduce-scatter.37.cloned.1.call-done = bf16[512,768]{0,1:T(8,128)(2,1)} async-done(((bf16[4096,768]{0,1:T(8,128)(2,1)}), bf16[512,768]{0,1:T(8,128)(2,1)}) %reduce-scatter.37.cloned.1.call-update) | async-done | bytes 786448 | tf_op jit(solution)/shard_map/while/body/eval_jaxpr/reduce_scatter | solution.py:318
  2080.9 57.3 %reduce-scatter.25.cloned.1.call-done = f32[24,768]{1,0:T(8,128)} async-done(((f32[768,768]{1,0:T(8,128)}), f32[24,768]{1,0:T(8,128)}) %reduce-scatter.25.cloned.1.call-update) | async-done | bytes 73744 | tf_op jit(solution)/shard_map/reduce_scatter | solution.py:392
  2138.2 104.3 %reduce-scatter.29.cloned.1.call-done = f32[24,768]{1,0:T(8,128)} async-done(((f32[768,768]{1,0:T(8,128)}), f32[24,768]{1,0:T(8,128)}) %reduce-scatter.29.cloned.1.call-update) | async-done | bytes 73744 | tf_op jit(solution)/shard_map/reduce_scatter | solution.py:385
  2242.6 124.6 %reduce-scatter.23.cloned.1.call-done = f32[3,24,768]{2,1,0:T(8,128)} async-done(((f32[3,768,768]{2,1,0:T(8,128)}), f32[3,24,768]{2,1,0:T(8,128)}) %reduce-scatter.23.cloned.1.call-update) | async-done | bytes 221200 | tf_op jit(solution)/shard_map/reduce_scatter | solution.py:391
  2367.2 124.8 %reduce-scatter.27.cloned.1.call-done = f32[3,24,768]{2,1,0:T(8,128)} async-done(((f32[3,768,768]{2,1,0:T(8,128)}), f32[3,24,768]{2,1,0:T(8,128)}) %reduce-scatter.27.cloned.1.call-update) | async-done | bytes 221200 | tf_op jit(solution)/shard_map/reduce_scatter | solution.py:384
  2492.0 141.7 %reduce-scatter.31.cloned.1.call-done = f32[24,3072]{1,0:T(8,128)} async-done(((f32[768,3072]{1,0:T(8,128)}), f32[24,3072]{1,0:T(8,128)}) %reduce-scatter.31.cloned.1.call-update) | async-done | bytes 294928 | tf_op jit(solution)/shard_map/reduce_scatter | solution.py:378
  2633.7 141.7 %reduce-scatter.33.cloned.1.call-done = f32[96,768]{1,0:T(8,128)} async-done(((f32[3072,768]{1,0:T(8,128)}), f32[96,768]{1,0:T(8,128)}) %reduce-scatter.33.cloned.1.call-update) | async-done | bytes 294928 | tf_op jit(solution)/shard_map/reduce_scatter | solution.py:380
  (893 shorter events, 983.5 us)
Async XLA Ops:
  9.2 210.9 %all-gather.31.cloned.1.call-start = ((), (), s32[]{:S(2)}) async-start(), calls=%async_computation.20 | async-start | bytes 3649536 | tf_op jit(solution)/shard_map/while/body/eval_jaxpr/all_gather | solution.py:141
  9.9 285.4 %all-gather.27.cloned.1.call-start = ((), (), s32[]{:S(2)}) async-start(), calls=%async_computation.18 | async-start | bytes 7077888 | tf_op jit(solution)/shard_map/while/body/eval_jaxpr/all_gather | solution.py:217
  75.4 273.6 %all-gather.25.cloned.1.call-start = ((), (), s32[]{:S(2)}) async-start(), calls=%async_computation.17 | async-start | bytes 7077888 | tf_op jit(solution)/shard_map/while/body/eval_jaxpr/all_gather | solution.py:218
  141.8 252.5 %all-gather.29.cloned.1.call-start = ((), (), s32[]{:S(2)}) async-start(), calls=%async_computation.19 | async-start | bytes 1216512 | tf_op jit(solution)/shard_map/while/body/eval_jaxpr/all_gather | solution.py:132
  142.4 307.8 %all-gather.33.cloned.1.call-start = ((), (), s32[]{:S(2)}) async-start(), calls=%async_computation.21 | async-start | bytes 1216512 | tf_op jit(solution)/shard_map/while/body/eval_jaxpr/all_gather | solution.py:142
  142.9 373.3 %all-gather.35.cloned.1.call-start = ((), (), s32[]{:S(2)}) async-start(), calls=%async_computation.22 | async-start | bytes 4866048 | tf_op jit(solution)/shard_map/while/body/eval_jaxpr/all_gather | solution.py:151
  143.7 437.5 %all-gather.37.cloned.1.call-start = ((), (), s32[]{:S(2)}) async-start(), calls=%async_computation.23 | async-start | bytes 4866048 | tf_op jit(solution)/shard_map/while/body/eval_jaxpr/all_gather | solution.py:153
  144.4 749.3 %reduce-scatter.39.cloned.1.call-start = ((), (), s32[]{:S(2)}) async-start(), calls=%async_computation.26 | async-start | bytes 442368 | tf_op jit(solution)/shard_map/while
  611.9 285.7 %reduce-scatter.41.cloned.1.call-start = ((), (), s32[]{:S(2)}) async-start(), calls=%async_computation.27 | async-start | bytes 442368 | tf_op jit(solution)/shard_map/while
  736.5 267.9 %reduce-scatter.37.cloned.1.call-start = ((), (), s32[]{:S(2)}) async-start(), calls=%async_computation.25 | async-start | bytes 7077888 | tf_op jit(solution)/shard_map/while/body/eval_jaxpr/reduce_scatter | solution.py:318
  1022.0 284.0 %all-gather.27.cloned.1.call-start = ((), (), s32[]{:S(2)}) async-start(), calls=%async_computation.18 | async-start | bytes 7077888 | tf_op jit(solution)/shard_map/while/body/eval_jaxpr/all_gather | solution.py:217
  1086.6 273.0 %all-gather.25.cloned.1.call-start = ((), (), s32[]{:S(2)}) async-start(), calls=%async_computation.17 | async-start | bytes 7077888 | tf_op jit(solution)/shard_map/while/body/eval_jaxpr/all_gather | solution.py:218
  1152.9 252.2 %all-gather.29.cloned.1.call-start = ((), (), s32[]{:S(2)}) async-start(), calls=%async_computation.19 | async-start | bytes 1216512 | tf_op jit(solution)/shard_map/while/body/eval_jaxpr/all_gather | solution.py:132
  1153.5 307.5 %all-gather.33.cloned.1.call-start = ((), (), s32[]{:S(2)}) async-start(), calls=%async_computation.21 | async-start | bytes 1216512 | tf_op jit(solution)/shard_map/while/body/eval_jaxpr/all_gather | solution.py:142
  1154.1 373.0 %all-gather.35.cloned.1.call-start = ((), (), s32[]{:S(2)}) async-start(), calls=%async_computation.22 | async-start | bytes 4866048 | tf_op jit(solution)/shard_map/while/body/eval_jaxpr/all_gather | solution.py:151
  1154.8 437.1 %all-gather.37.cloned.1.call-start = ((), (), s32[]{:S(2)}) async-start(), calls=%async_computation.23 | async-start | bytes 4866048 | tf_op jit(solution)/shard_map/while/body/eval_jaxpr/all_gather | solution.py:153
  1155.4 753.8 %reduce-scatter.39.cloned.1.call-start = ((), (), s32[]{:S(2)}) async-start(), calls=%async_computation.26 | async-start | bytes 442368 | tf_op jit(solution)/shard_map/while
  1622.8 290.3 %reduce-scatter.41.cloned.1.call-start = ((), (), s32[]{:S(2)}) async-start(), calls=%async_computation.27 | async-start | bytes 442368 | tf_op jit(solution)/shard_map/while
  1712.1 212.6 %reduce-scatter.35.cloned.1.call-start = ((), (), s32[]{:S(2)}) async-start(), calls=%async_computation.24 | async-start | bytes 7077888 | tf_op jit(solution)/shard_map/while/body/eval_jaxpr/reduce_scatter | solution.py:321
  1747.2 267.9 %reduce-scatter.37.cloned.1.call-start = ((), (), s32[]{:S(2)}) async-start(), calls=%async_computation.25 | async-start | bytes 7077888 | tf_op jit(solution)/shard_map/while/body/eval_jaxpr/reduce_scatter | solution.py:318
  2034.4 332.7 %reduce-scatter.23.cloned.1.call-start = ((), (), s32[]{:S(2)}) async-start(), calls=%async_computation.10 | async-start | bytes 7299072 | tf_op jit(solution)/shard_map/reduce_scatter | solution.py:391
  2035.0 457.0 %reduce-scatter.27.cloned.1.call-start = ((), (), s32[]{:S(2)}) async-start(), calls=%async_computation.12 | async-start | bytes 7299072 | tf_op jit(solution)/shard_map/reduce_scatter | solution.py:384
  2035.8 597.9 %reduce-scatter.31.cloned.1.call-start = ((), (), s32[]{:S(2)}) async-start(), calls=%async_computation.14 | async-start | bytes 9732096 | tf_op jit(solution)/shard_map/reduce_scatter | solution.py:378
  2036.5 738.9 %reduce-scatter.33.cloned.1.call-start = ((), (), s32[]{:S(2)}) async-start(), calls=%async_computation.15 | async-start | bytes 9732096 | tf_op jit(solution)/shard_map/reduce_scatter | solution.py:380
  (262 other events, 6050.2 us)
Sparse Core Ops, SparseCore 0:
  12.3 59.7 all-gather.22
  75.2 59.0 all-gather.30
  136.5 99.7 all-gather.26
  238.3 101.1 all-gather.24
  342.4 51.8 all-gather.28
  397.1 52.9 all-gather.32
  453.2 63.0 all-gather.34
  519.3 61.9 all-gather.36
  612.0 60.3 reduce-scatter.38
  701.5 60.2 reduce-scatter.40
  765.5 117.7 reduce-scatter.34
  886.7 117.7 reduce-scatter.36
  1024.5 58.6 all-gather.22
  1086.2 58.9 all-gather.30
  1147.3 99.8 all-gather.26
  1249.2 101.0 all-gather.24
  1353.1 51.9 all-gather.28
  1407.9 53.0 all-gather.32
  1464.0 63.0 all-gather.34
  1529.9 61.9 all-gather.36
  1622.9 60.3 reduce-scatter.38
  1712.2 60.3 reduce-scatter.40
  1776.2 117.6 reduce-scatter.34
  1897.4 117.6 reduce-scatter.36
Sparse Core Ops, SparseCore 1:
  2039.6 98.6 reduce-scatter.24
  2143.9 98.5 reduce-scatter.28
  2248.7 118.5 reduce-scatter.22
  2373.5 118.5 reduce-scatter.26
  2498.5 135.1 reduce-scatter.30
  2640.2 135.1 reduce-scatter.32
where the time goes:
time: 2790 us; the launch traced here: 2780 us
  waiting for transfers between devices  1210 us (43%)
  matrix products  701 us (25%)
  blocking collectives  516 us (18%)
  other arithmetic  224 us (8%)
  local copies, waits for them, and re-layouts  106 us (4%)
    reduce_scatter x2, waiting for transfers between devices, micro_step(): lax.psum_scatter(grad_keys.astype(jnp.bfloat16), 'seq', scatter_dimension...  185 us
    convert_element_type x4, other arithmetic, attend_backward(): grad_scores = (shares_full * (grad_shares - inner_sum)).astype(jnp.bfloat16)  173 us
    dot_general x4, matrix products, attend_backward(): jnp.einsum('rhd,khd->hrk', grad_heads, head_split(value_rows), preferred_...  142 us
    reduce_scatter x1, waiting for transfers between devices, body(): lax.psum_scatter(grad_sums[10], ('dp', 'seq'), scatter_dimension=0, tiled...  142 us
    reduce_scatter x1, waiting for transfers between devices, body(): lax.psum_scatter(grad_sums[8], ('dp', 'seq'), scatter_dimension=0, tiled=...  142 us
    all_gather x2, blocking collectives, fetch_cross(): lax.all_gather(shards[7], ('dp', 'seq'), axis=1, tiled=True)  133 us
    all_gather x2, waiting for transfers between devices, fetch_feed(): lax.all_gather(shards[8], ('dp', 'seq'), axis=0, tiled=True)  125 us
    reduce_scatter x1, waiting for transfers between devices, body(): lax.psum_scatter(grad_sums[5], ('dp', 'seq'), scatter_dimension=1, tiled=...  125 us
  transfers between devices with their start and end apart: 30, of which 18 were waited for; matrix products, arithmetic and copies ran while one was open for 33% of the time, Pallas kernels for 0%

commit v1 on v0

--- a/solution.py
+++ b/solution.py
@@ -1,6 +1,10 @@
+import functools
+
 import jax
 import jax.numpy as jnp
 from jax import lax
+from jax.experimental import pallas as pl
+from jax.experimental.pallas import tpu as pltpu
 from jax.sharding import PartitionSpec as P
 
 HEADS = 12
@@ -411,6 +415,925 @@
     )
 
 
+LOG2E = 1.4426950408889634
+LN2 = 0.6931471805599453
+QSCALE = HEAD ** (-0.5) * LOG2E
+AXES = ("dp", "seq")
+F32 = jnp.float32
+BF16 = jnp.bfloat16
+ANY = pl.BlockSpec(memory_space=pl.ANY)
+SMEM = pl.BlockSpec(memory_space=pltpu.SMEM)
+
+
+def nn(a, b):
+    return lax.dot_general(a, b, (((1,), (0,)), ((), ())), preferred_element_type=F32)
+
+
+def nt(a, b):
+    return lax.dot_general(a, b, (((1,), (1,)), ((), ())), preferred_element_type=F32)
+
+
+def tn(a, b):
+    return lax.dot_general(a, b, (((0,), (0,)), ((), ())), preferred_element_type=F32)
+
+
+def whole(shape):
+    zeros = (0,) * len(shape)
+    return pl.BlockSpec(shape, lambda *_: zeros)
+
+
+def params(**kw):
+    return pltpu.CompilerParams(vmem_limit_bytes=60 * 1024 * 1024, **kw)
+
+
+def cost(flops, nbytes, trans=0):
+    return pl.CostEstimate(flops=int(flops), bytes_accessed=int(nbytes), transcendentals=int(trans))
+
+
+def stats(v):
+    mean = jnp.mean(v, axis=-1, keepdims=True)
+    centered = v - mean
+    var = jnp.mean(centered * centered, axis=-1, keepdims=True)
+    rstd = lax.rsqrt(var + 1e-05)
+    return centered * rstd, rstd
+
+
+def norm_back(v, e, gain):
+    z, rstd = stats(v)
+    f = e * gain
+    grad = rstd * (
+        f - jnp.mean(f, axis=-1, keepdims=True) - z * jnp.mean(f * z, axis=-1, keepdims=True)
+    )
+    return grad, jnp.sum(e * z, axis=0, keepdims=True), jnp.sum(e, axis=0, keepdims=True)
+
+
+def qkv_kernel(meta, *refs):
+    pieces = refs[:8]
+    w_ref, vec_ref, bias_ref, q_ref, kv_ref, tr_ref, n1_ref, buf, sem = refs[8:]
+    rows = buf.shape[0] // 8
+    step = pl.program_id(0)
+
+    @pl.when(step == 0)
+    def _():
+        copies = [
+            pltpu.make_async_copy(pieces[i], buf.at[pl.ds(i * rows, rows), :], sem.at[i])
+            for i in range(8)
+        ]
+        for c in copies:
+            c.start()
+        for c in copies:
+            c.wait()
+
+    gain, shift = vec_ref[0:1, :], vec_ref[3:4, :]
+    w = w_ref[...]
+    bias = bias_ref[0:1, :]
+    for u in range(4):
+        b = meta[32 + step * 4 + u]
+        off = pl.multiple_of((b // 4) * rows + (b % 4) * 128, 32)
+        x = buf[pl.ds(off, 128), :].astype(F32)
+        z, _ = stats(x)
+        n1 = (z * gain + shift).astype(BF16)
+        r = slice(u * 128, (u + 1) * 128)
+        n1_ref[r, :] = n1
+        y = nn(n1, w) + bias
+        kvt = jnp.transpose(y[:, 192:576]).astype(BF16)
+        for t in range(2):
+            for h in range(3):
+                o = (t * 3 + h) * 64
+                tr_ref[t * 3 + h, :, r] = kvt[o : o + 64, :]
+        yq = (y[:, 0:192] * QSCALE).astype(BF16)
+        yk = y[:, 192:576].astype(BF16)
+        zero = jnp.zeros((128, 64), BF16)
+        for h in range(3):
+            q_ref[h, r, :] = jnp.concatenate([yq[:, h * 64 : h * 64 + 64], zero], axis=1)
+            kv_ref[h, r, :] = jnp.concatenate(
+                [yk[:, h * 64 : h * 64 + 64], yk[:, 192 + h * 64 : 256 + h * 64]], axis=1
+            )
+
+
+def qkv_call(meta, pieces, w2, vecs, bias):
+    rows = pieces[0].shape[0]
+    grid = (8,)
+    return pl.pallas_call(
+        qkv_kernel,
+        grid_spec=pltpu.PrefetchScalarGridSpec(
+            num_scalar_prefetch=1,
+            grid=grid,
+            in_specs=[ANY] * 8 + [whole(w2.shape), whole(vecs.shape), whole(bias.shape)],
+            out_specs=[
+                pl.BlockSpec((3, 512, 128), lambda i, m: (0, i, 0)),
+                pl.BlockSpec((3, 512, 128), lambda i, m: (0, i, 0)),
+                pl.BlockSpec((6, 64, 512), lambda i, m: (0, 0, i)),
+                pl.BlockSpec((512, 768), lambda i, m: (i, 0)),
+            ],
+            scratch_shapes=[pltpu.VMEM((8 * rows, 768), BF16), pltpu.SemaphoreType.DMA((8,))],
+        ),
+        out_shape=[
+            jax.ShapeDtypeStruct((3, 4096, 128), BF16),
+            jax.ShapeDtypeStruct((3, 4096, 128), BF16),
+            jax.ShapeDtypeStruct((6, 64, 4096), BF16),
+            jax.ShapeDtypeStruct((4096, 768), BF16),
+        ],
+        compiler_params=params(dimension_semantics=("arbitrary",)),
+        cost_estimate=cost(2 * 4096 * 768 * 576, 20e6),
+        name="qkv",
+    )(meta, *pieces, w2, vecs, bias)
+
+
+def tile_mask(diag, kt, limit):
+    key = lax.broadcasted_iota(jnp.int32, (256, 256), 0)
+    if diag:
+        return key <= lax.broadcasted_iota(jnp.int32, (256, 256), 1)
+    return key + kt * 256 < limit
+
+
+def attend_kernel(meta, q_ref, kv_ref, tr_ref, o_ref, lse_ref, m_ref, l_ref, acc_ref):
+    def q_tile(qi, carry):
+        branch = qi >= 8
+        fork = meta[64 + jnp.maximum(qi - 8, 0)]
+        full = jnp.where(branch, fork // 256, qi)
+        qs = pl.ds(pl.multiple_of(qi * 256, 256), 256)
+        m_ref[...] = jnp.full_like(m_ref, -1e30)
+        l_ref[...] = jnp.zeros_like(l_ref)
+        acc_ref[...] = jnp.zeros_like(acc_ref)
+
+        def k_tile(kt, mask):
+            ks = pl.ds(pl.multiple_of(kt * 256, 256), 256)
+            for h in range(3):
+                s = nt(kv_ref[h, ks, :], q_ref[h, qs, :])
+                if mask is not None:
+                    s = jnp.where(mask, s, -1e30)
+                old = m_ref[h : h + 1, :]
+                new = jnp.maximum(old, jnp.max(s, axis=0, keepdims=True))
+                p = jnp.exp2(s - new)
+                alpha = jnp.exp2(old - new)
+                m_ref[h : h + 1, :] = new
+                l_ref[h : h + 1, :] = l_ref[h : h + 1, :] * alpha + jnp.sum(p, axis=0, keepdims=True)
+                hs = slice(h * 64, h * 64 + 64)
+                acc_ref[hs, :] = acc_ref[hs, :] * alpha + nn(tr_ref[3 + h, :, ks], p.astype(BF16))
+
+        def full_tile(kt, c):
+            k_tile(kt, None)
+            return c
+
+        lax.fori_loop(0, full, full_tile, 0)
+
+        @pl.when(branch & (fork % 256 != 0))
+        def _():
+            k_tile(full, tile_mask(False, full, fork))
+
+        k_tile(qi, tile_mask(True, 0, 0))
+        for h in range(3):
+            hs = slice(h * 64, h * 64 + 64)
+            l = l_ref[h : h + 1, :]
+            acc_ref[hs, :] = acc_ref[hs, :] * (1.0 / l)
+            lse_ref[h : h + 1, qs] = m_ref[h : h + 1, :] + jnp.log2(l)
+        out = jnp.transpose(acc_ref[...]).astype(BF16)
+        for u in range(2):
+            o_ref[meta[32 + qi * 2 + u]] = out[u * 128 : (u + 1) * 128, :]
+        return carry
+
+    lax.fori_loop(0, 16, q_tile, 0)
+
+
+def attend_call(meta, q, kv, tr):
+    return pl.pallas_call(
+        attend_kernel,
+        grid_spec=pltpu.PrefetchScalarGridSpec(
+            num_scalar_prefetch=1,
+            grid=(1,),
+            in_specs=[whole(q.shape), whole(kv.shape), whole(tr.shape)],
+            out_specs=[whole((32, 128, 192)), whole((8, 4096))],
+            scratch_shapes=[
+                pltpu.VMEM((8, 256), F32),
+                pltpu.VMEM((8, 256), F32),
+                pltpu.VMEM((192, 256), F32),
+            ],
+        ),
+        out_shape=[
+            jax.ShapeDtypeStruct((32, 128, 192), BF16),
+            jax.ShapeDtypeStruct((8, 4096), F32),
+        ],
+        compiler_params=params(dimension_semantics=("arbitrary",)),
+        cost_estimate=cost(20e9, 10e6, 20e6),
+        name="attend",
+    )(meta, q, kv, tr)
+
+
+def attend_back_kernel(
+    meta, q_ref, kv_ref, tr_ref, o_ref, lse_ref, d0, d1, d2, d3, out_ref, do_ref, di_ref, dq_ref, acc_ref
+):
+    pieces = (d0, d1, d2, d3)
+    zero = jnp.zeros((128, 64), BF16)
+    for k in range(4):
+        for kk in range(8):
+            b = k * 8 + kk
+            at = pl.ds(pl.multiple_of(meta[b] * 128, 128), 128)
+            do = pieces[k][kk * 128 : (kk + 1) * 128, :]
+            prod = jnp.transpose(do.astype(F32) * o_ref[b].astype(F32))
+            for h in range(3):
+                di_ref[h : h + 1, at] = jnp.sum(prod[h * 64 : h * 64 + 64, :], axis=0, keepdims=True)
+                do_ref[h, at, :] = jnp.concatenate([zero, do[:, h * 64 : h * 64 + 64]], axis=1)
+    acc_ref[...] = jnp.zeros_like(acc_ref)
+
+    def q_tile(qi, carry):
+        branch = qi >= 8
+        fork = meta[64 + jnp.maximum(qi - 8, 0)]
+        full = jnp.where(branch, fork // 256, qi)
+        qs = pl.ds(pl.multiple_of(qi * 256, 256), 256)
+        dq_ref[...] = jnp.zeros_like(dq_ref)
+
+        def k_tile(kt, mask):
+            ks = pl.ds(pl.multiple_of(kt * 256, 256), 256)
+            for h in range(3):
+                kv = kv_ref[h, ks, :]
+                q, do = q_ref[h, qs, :], do_ref[h, qs, :]
+                p = jnp.exp2(nt(kv, q) - lse_ref[h : h + 1, qs])
+                if mask is not None:
+                    p = jnp.where(mask, p, 0.0)
+                ds = (p * (nt(kv, do) - di_ref[h : h + 1, qs])).astype(BF16)
+                acc_ref[h, ks, :] += nn(ds, q) + nn(p.astype(BF16), do)
+                hs = slice(h * 64, h * 64 + 64)
+                dq_ref[hs, :] += nn(tr_ref[h, :, ks], ds)
+
+        def full_tile(kt, c):
+            k_tile(kt, None)
+            return c
+
+        lax.fori_loop(0, full, full_tile, 0)
+
+        @pl.when(branch & (fork % 256 != 0))
+        def _():
+            k_tile(full, tile_mask(False, full, fork))
+
+        k_tile(qi, tile_mask(True, 0, 0))
+        out_ref[qs, 0:192] = (jnp.transpose(dq_ref[...]) * HEAD ** (-0.5)).astype(BF16)
+        return carry
+
+    lax.fori_loop(0, 16, q_tile, 0)
+
+    def finish(t, carry):
+        rs = pl.ds(pl.multiple_of(t * 256, 256), 256)
+        a = [acc_ref[h, rs, :] for h in range(3)]
+        dk = jnp.concatenate([v[:, 0:64] for v in a], axis=1) * LN2
+        dv = jnp.concatenate([v[:, 64:128] for v in a], axis=1)
+        out_ref[rs, 192:576] = jnp.concatenate([dk, dv], axis=1).astype(BF16)
+        return carry
+
+    lax.fori_loop(0, 16, finish, 0)
+
+
+def attend_back_call(meta, q, kv, tr, o, lse, pieces):
+    ins = [q, kv, tr, o, lse, *pieces]
+    return pl.pallas_call(
+        attend_back_kernel,
+        grid_spec=pltpu.PrefetchScalarGridSpec(
+            num_scalar_prefetch=1,
+            grid=(1,),
+            in_specs=[whole(v.shape) for v in ins],
+            out_specs=whole((4096, 576)),
+            scratch_shapes=[
+                pltpu.VMEM((3, 4096, 128), BF16),
+                pltpu.VMEM((8, 4096), F32),
+                pltpu.VMEM((192, 256), F32),
+                pltpu.VMEM((3, 4096, 128), F32),
+            ],
+        ),
+        out_shape=jax.ShapeDtypeStruct((4096, 576), BF16),
+        compiler_params=params(dimension_semantics=("arbitrary",)),
+        cost_estimate=cost(50e9, 15e6, 20e6),
+        name="attend_back",
+    )(meta, *ins)
+
+
+def dx_kernel(meta, d_ref, w_ref, out_ref, *, piece):
+    kk = pl.program_id(0)
+    at = pl.ds(pl.multiple_of(meta[piece * 8 + kk] * 128, 128), 128)
+    out_ref[...] = nt(d_ref[at, :], w_ref[...]).astype(BF16)
+
+
+def dx_call(meta, dqkv, w2, piece):
+    return pl.pallas_call(
+        functools.partial(dx_kernel, piece=piece),
+        grid_spec=pltpu.PrefetchScalarGridSpec(
+            num_scalar_prefetch=1,
+            grid=(8,),
+            in_specs=[whole(dqkv.shape), whole(w2.shape)],
+            out_specs=pl.BlockSpec((128, 768), lambda i, m: (i, 0)),
+        ),
+        out_shape=jax.ShapeDtypeStruct((1024, 768), BF16),
+        compiler_params=params(dimension_semantics=("arbitrary",)),
+        cost_estimate=cost(2 * 1024 * 768 * 576, 6e6),
+        name="dx%d" % piece,
+    )(meta, dqkv, w2)
+
+
+def win_kernel(n_ref, d_ref, g_ref, s_ref, acc_ref):
+    step = pl.program_id(0)
+
+    @pl.when(step == 0)
+    def _():
+        acc_ref[...] = jnp.zeros_like(acc_ref)
+        s_ref[...] = jnp.zeros_like(s_ref)
+
+    d = d_ref[...]
+    acc_ref[...] += tn(n_ref[...], d)
+    s_ref[0:1, :] += jnp.sum(d.astype(F32), axis=0, keepdims=True)
+
+    @pl.when(step == pl.num_programs(0) - 1)
+    def _():
+        g_ref[...] = acc_ref[...].astype(BF16)
+
+
+def win_call(n1, dqkv):
+    return pl.pallas_call(
+        win_kernel,
+        grid=(4,),
+        in_specs=[
+            pl.BlockSpec((1024, 768), lambda i: (i, 0)),
+            pl.BlockSpec((1024, 576), lambda i: (i, 0)),
+        ],
+        out_specs=[whole((768, 576)), whole((8, 576))],
+        out_shape=[
+            jax.ShapeDtypeStruct((768, 576), BF16),
+            jax.ShapeDtypeStruct((8, 576), F32),
+        ],
+        scratch_shapes=[pltpu.VMEM((768, 576), F32)],
+        compiler_params=params(dimension_semantics=("arbitrary",)),
+        cost_estimate=cost(2 * 4096 * 768 * 576, 12e6),
+        name="win",
+    )(n1, dqkv)
+
+
+def head_masks(frames):
+    lane = lax.broadcasted_iota(jnp.int32, (frames, 128), 1) < 64
+    return lane, jnp.logical_not(lane)
+
+
+def mid_kernel(
+    meta, tok_ref, o0, o1, o2, o3, so_ref, ci_ref, co_ref, fr_ref, vec_ref,
+    mid_ref, ac_ref, n2_ref, n3_ref, cq_ref, ca_ref, lse_ref, kc_ref, vc_ref,
+    km_ref, vmt_ref,
+):
+    frames = fr_ref.shape[0]
+    hset = meta[72]
+
+    @pl.when(pl.program_id(0) == 0)
+    def _():
+        fr = fr_ref[...]
+        kc = nn(fr, ci_ref[1]).astype(BF16)
+        vc = (nn(fr, ci_ref[2]) + vec_ref[10:11, :]).astype(BF16)
+        kc_ref[...] = kc
+        vc_ref[...] = vc
+        zero = jnp.zeros((frames, 128), BF16)
+        masks = head_masks(frames)
+        for hp in range(6):
+            ls = slice(hp * 128, hp * 128 + 128)
+            for e in range(2):
+                km_ref[hp * 2 + e] = jnp.where(masks[e], kc[:, ls], zero)
+                vmt_ref[hp * 2 + e] = jnp.transpose(
+                    jnp.where(masks[e], vc[:, ls].astype(F32), 0.0)
+                ).astype(BF16)
+
+    acc = tok_ref[...].astype(F32) + vec_ref[8:9, :]
+    for k, o in enumerate((o0, o1, o2, o3)):
+        at = pl.ds(pl.multiple_of((hset ^ k) * 192, 64), 192)
+        acc = acc + nn(o[...], so_ref[at, :])
+    mid_ref[...] = acc
+    z, _ = stats(acc)
+    n2 = (z * vec_ref[1:2, :] + vec_ref[4:5, :]).astype(BF16)
+    n2_ref[...] = n2
+    cq = ((nn(n2, ci_ref[0]) + vec_ref[9:10, :]) * QSCALE).astype(BF16)
+    cq_ref[...] = cq
+    ca = []
+    for hp in range(6):
+        qp = cq[:, hp * 128 : hp * 128 + 128]
+        out = None
+        for e in range(2):
+            h = hp * 2 + e
+            s = nt(km_ref[h], qp)
+            m = jnp.max(s, axis=0, keepdims=True)
+            p = jnp.exp2(s - m)
+            l = jnp.sum(p, axis=0, keepdims=True)
+            lse_ref[h : h + 1, :] = m + jnp.log2(l)
+            part = nn(vmt_ref[h], p.astype(BF16)) * (1.0 / l)
+            out = part if out is None else out + part
+        ca.append(jnp.transpose(out).astype(BF16))
+    ca = jnp.concatenate(ca, axis=1)
+    ca_ref[...] = ca
+    ac = acc + nn(ca, co_ref[...]) + vec_ref[11:12, :]
+    ac_ref[...] = ac
+    z, _ = stats(ac)
+    n3_ref[...] = (z * vec_ref[2:3, :] + vec_ref[5:6, :]).astype(BF16)
+
+
+def mid_call(meta, tok, pieces, so, ci, co, frames, vecs):
+    rows, width = tok.shape
+    tile = 256
+    nf = frames.shape[0]
+    row = pl.BlockSpec((tile, width), lambda i, m: (i, 0))
+    row4 = pl.BlockSpec((tile, 192), lambda i, m: (i, 0))
+    sds = jax.ShapeDtypeStruct
+    return pl.pallas_call(
+        mid_kernel,
+        grid_spec=pltpu.PrefetchScalarGridSpec(
+            num_scalar_prefetch=1,
+            grid=(rows // tile,),
+            in_specs=[row] + [row4] * 4
+            + [whole(so.shape), whole(ci.shape), whole(co.shape), whole(frames.shape), whole(vecs.shape)],
+            out_specs=[row] * 6
+            + [pl.BlockSpec((16, tile), lambda i, m: (0, i)), whole((nf, width)), whole((nf, width))],
+            scratch_shapes=[pltpu.VMEM((12, nf, 128), BF16), pltpu.VMEM((12, 128, nf), BF16)],
+        ),
+        out_shape=[
+            sds((rows, width), F32), sds((rows, width), F32), sds((rows, width), BF16),
+            sds((rows, width), BF16), sds((rows, width), BF16), sds((rows, width), BF16),
+            sds((16, rows), F32), sds((nf, width), BF16), sds((nf, width), BF16),
+        ],
+        compiler_params=params(dimension_semantics=("arbitrary",)),
+        cost_estimate=cost(8e9, 25e6, 3e6),
+        name="middle",
+    )(meta, tok, *pieces, so, ci, co, frames, vecs)
+
+
+def normal_parts(b):
+    e = jnp.exp2(b * b * (-0.5 * LOG2E))
+    a = jnp.abs(b) * 0.7071067811865476
+    t = 1.0 / (1.0 + 0.3275911 * a)
+    poly = t * (
+        0.254829592 + t * (-0.284496736 + t * (1.421413741 + t * (-1.453152027 + t * 1.061405429)))
+    )
+    tail = 0.5 * poly * e
+    return jnp.where(b < 0.0, tail, 1.0 - tail), e * 0.3989422804014327
+
+
+def feed_kernel(
+    n3_ref, og_ref, ac_ref, up_ref, dn_ref, ub_ref, vec_ref,
+    res_ref, gt_ref, ug_ref, dg_ref, ubg_ref, dbg_ref,
+    acc_ref, n3t_ref, act_ref, gb_ref,
+):
+    step = pl.program_id(0)
+    rows, width = n3_ref.shape
+
+    @pl.when(step == 0)
+    def _():
+        acc_ref[...] = ac_ref[...] + vec_ref[12:13, :]
+        gt_ref[...] = jnp.zeros_like(gt_ref)
+        dbg_ref[...] = jnp.zeros_like(dbg_ref)
+        dbg_ref[0:1, :] = jnp.sum(og_ref[...].astype(F32), axis=0, keepdims=True)
+        n3t_ref[...] = jnp.transpose(n3_ref[...])
+
+    up = up_ref[...].reshape(width, width)
+    dn = dn_ref[...].reshape(width, width)
+    ub = ub_ref[pl.ds(step, 1), :]
+    total = jnp.zeros((1, width), F32)
+    for r in range(rows // 256):
+        rs = slice(r * 256, (r + 1) * 256)
+        n3 = n3_ref[rs, :]
+        og = og_ref[rs, :]
+        b = nn(n3, up) + ub
+        cdf, pdf = normal_parts(b)
+        act = (b * cdf).astype(BF16)
+        gb = (nt(og, dn) * (cdf + b * pdf)).astype(BF16)
+        act_ref[rs, :] = act
+        gb_ref[rs, :] = gb
+        total = total + jnp.sum(gb.astype(F32), axis=0, keepdims=True)
+        acc_ref[rs, :] += nn(act, dn)
+        gt_ref[rs, :] += nt(gb, up)
+    ubg_ref[...] = jnp.broadcast_to(total, (8, width))
+    ug_ref[...] = nn(n3t_ref[...], gb_ref[...]).astype(BF16).reshape(ug_ref.shape)
+    dg_ref[...] = tn(act_ref[...], og_ref[...]).astype(BF16).reshape(dg_ref.shape)
+
+    @pl.when(step == pl.num_programs(0) - 1)
+    def _():
+        res_ref[...] = acc_ref[...].astype(BF16)
+
+
+def feed_call(n3, og, ac, up4, dn4, ub4, vecs):
+    rows, width = n3.shape
+    sds = jax.ShapeDtypeStruct
+    tiles = up4.shape[0]
+    tile = pl.BlockSpec((1, width, width), lambda i: (i, 0, 0))
+    return pl.pallas_call(
+        feed_kernel,
+        grid=(tiles,),
+        in_specs=[whole(n3.shape), whole(og.shape), whole(ac.shape), tile, tile, whole(ub4.shape), whole(vecs.shape)],
+        out_specs=[
+            whole((rows, width)), whole((rows, width)), tile, tile,
+            pl.BlockSpec((8, width), lambda i: (i, 0)), whole((8, width)),
+        ],
+        out_shape=[
+            sds((rows, width), BF16), sds((rows, width), F32),
+            sds((tiles, width, width), BF16), sds((tiles, width, width), BF16),
+            sds((tiles * 8, width), F32), sds((8, width), F32),
+        ],
+        scratch_shapes=[
+            pltpu.VMEM((rows, width), F32), pltpu.VMEM((width, rows), BF16),
+            pltpu.VMEM((rows, width), BF16), pltpu.VMEM((rows, width), BF16),
+        ],
+        compiler_params=params(dimension_semantics=("arbitrary",)),
+        cost_estimate=cost(2 * 6 * rows * width * width * tiles, 35e6, 6e6),
+        name="feed",
+    )(n3, og, ac, up4, dn4, ub4, vecs)
+
+
+def mid_back_kernel(
+    meta, gt_ref, og_ref, ac_ref, mid_ref, n2_ref, cq_ref, ca_ref, lse_ref, kc_ref, vc_ref,
+    fr_ref, so_ref, ci_ref, co_ref, vec_ref, o0, o1, o2, o3,
+    gm_ref, do0, do1, do2, do3, sog_ref, cig_ref, cog_ref, eg_ref, sums_ref,
+    km_ref, kmt_ref, vm_ref, dk_ref, dv_ref, so_acc, cq_acc, co_acc,
+):
+    frames = fr_ref.shape[0]
+    hset = meta[72]
+    step = pl.program_id(0)
+    last = pl.num_programs(0) - 1
+    masks = head_masks(frames)
+
+    @pl.when(step == 0)
+    def _():
+        zero = jnp.zeros((frames, 128), BF16)
+        for hp in range(6):
+            ls = slice(hp * 128, hp * 128 + 128)
+            k, v = kc_ref[:, ls], vc_ref[:, ls]
+            for e in range(2):
+                km_ref[hp * 2 + e] = jnp.where(masks[e], k, zero)
+                vm_ref[hp * 2 + e] = jnp.where(masks[e], v, zero)
+                kmt_ref[hp * 2 + e] = jnp.transpose(
+                    jnp.where(masks[e], k.astype(F32), 0.0)
+                ).astype(BF16)
+        for ref in (dk_ref, dv_ref, so_acc, cq_acc, co_acc, sums_ref):
+            ref[...] = jnp.zeros_like(ref)
+
+    def count(row, value):
+        sums_ref[row : row + 1, :] += value
+
+    gt = gt_ref[...]
+    back, gain, shift = norm_back(ac_ref[...], gt, vec_ref[2:3, :])
+    count(2, gain)
+    count(5, shift)
+    ga = og_ref[...].astype(F32) + back
+    gal = ga.astype(BF16)
+    count(11, jnp.sum(gal.astype(F32), axis=0, keepdims=True))
+    ca = ca_ref[...]
+    co_acc[...] += tn(ca, gal)
+    dca = nt(gal, co_ref[...]).astype(BF16)
+    cq = cq_ref[...]
+    dq = []
+    for hp in range(6):
+        ls = slice(hp * 128, hp * 128 + 128)
+        qp, dp_ = cq[:, ls], dca[:, ls]
+        dqt = None
+        parts = []
+        for e in range(2):
+            h = hp * 2 + e
+            p = jnp.exp2(nt(km_ref[h], qp) - lse_ref[h : h + 1, :])
+            dp = nt(vm_ref[h], dp_)
+            inner = jnp.sum(dp * p, axis=0, keepdims=True)
+            ds = (p * (dp - inner)).astype(BF16)
+            part = nn(kmt_ref[h], ds)
+            dqt = part if dqt is None else dqt + part
+            parts.append((nn(ds, qp), nn(p.astype(BF16), dp_)))
+        dq.append(jnp.transpose(dqt))
+        dk_ref[:, ls] += jnp.where(masks[0], parts[0][0], parts[1][0])
+        dv_ref[:, ls] += jnp.where(masks[0], parts[0][1], parts[1][1])
+    dcq = (jnp.concatenate(dq, axis=1) * HEAD ** (-0.5)).astype(BF16)
+    count(9, jnp.sum(dcq.astype(F32), axis=0, keepdims=True))
+    cq_acc[...] += tn(n2_ref[...], dcq)
+    gs = nt(dcq, ci_ref[0])
+    back, gain, shift = norm_back(mid_ref[...], gs, vec_ref[1:2, :])
+    count(1, gain)
+    count(4, shift)
+    gm = ga + back
+    gm_ref[...] = gm
+    gml = gm.astype(BF16)
+    count(8, jnp.sum(gml.astype(F32), axis=0, keepdims=True))
+    for k, (o, do) in enumerate(zip((o0, o1, o2, o3), (do0, do1, do2, do3))):
+        at = pl.ds(pl.multiple_of((hset ^ k) * 192, 64), 192)
+        do[...] = nt(gml, so_ref[at, :]).astype(BF16)
+        so_acc[at, :] += tn(o[...], gml)
+
+    @pl.when(step == last)
+    def _():
+        dk = (dk_ref[...] * LN2).astype(BF16)
+        dv = dv_ref[...].astype(BF16)
+        count(10, jnp.sum(dv.astype(F32), axis=0, keepdims=True))
+        fr = fr_ref[...]
+        sog_ref[...] = so_acc[...].astype(BF16)
+        cog_ref[...] = co_acc[...].astype(BF16)
+        cig_ref[0] = cq_acc[...].astype(BF16)
+        cig_ref[1] = tn(fr, dk).astype(BF16)
+        cig_ref[2] = tn(fr, dv).astype(BF16)
+        eg_ref[...] = (nt(dk, ci_ref[1]) + nt(dv, ci_ref[2])).astype(BF16)
+
+
+def mid_back_call(meta, gt, og, ac, mid, n2, cq, ca, lse, kc, vc, frames, so, ci, co, vecs, pieces):
+    rows, width = gt.shape
+    tile = 256
+    nf = frames.shape[0]
+    row = pl.BlockSpec((tile, width), lambda i, m: (i, 0))
+    row4 = pl.BlockSpec((tile, 192), lambda i, m: (i, 0))
+    sds = jax.ShapeDtypeStruct
+    acc = pltpu.VMEM((width, width), F32)
+    return pl.pallas_call(
+        mid_back_kernel,
+        grid_spec=pltpu.PrefetchScalarGridSpec(
+            num_scalar_prefetch=1,
+            grid=(rows // tile,),
+            in_specs=[row] * 7
+            + [pl.BlockSpec((16, tile), lambda i, m: (0, i))]
+            + [whole(v.shape) for v in (kc, vc, frames, so, ci, co, vecs)]
+            + [row4] * 4,
+            out_specs=[row] + [row4] * 4
+            + [whole((width, width)), whole((3, width, width)), whole((width, width)), whole((nf, width)), whole((24, width))],
+            scratch_shapes=[
+                pltpu.VMEM((12, nf, 128), BF16), pltpu.VMEM((12, 128, nf), BF16), pltpu.VMEM((12, nf, 128), BF16),
+                pltpu.VMEM((nf, width), F32), pltpu.VMEM((nf, width), F32), acc, acc, acc,
+            ],
+        ),
+        out_shape=[sds((rows, width), F32)] + [sds((rows, 192), BF16)] * 4
+        + [sds((width, width), BF16), sds((3, width, width), BF16), sds((width, width), BF16), sds((nf, width), BF16), sds((24, width), F32)],
+        compiler_params=params(dimension_semantics=("arbitrary",)),
+        cost_estimate=cost(22e9, 35e6, 3e6),
+        name="middle_back",
+    )(meta, gt, og, ac, mid, n2, cq, ca, lse, kc, vc, frames, so, ci, co, vecs, *pieces)
+
+
+def first_back_kernel(a_ref, b_ref, gm_ref, tok_ref, vec_ref, out_ref, sums_ref):
+    @pl.when(pl.program_id(0) == 0)
+    def _():
+        sums_ref[...] = jnp.zeros_like(sums_ref)
+
+    e = a_ref[...].astype(F32) + b_ref[...].astype(F32)
+    back, gain, shift = norm_back(tok_ref[...].astype(F32), e, vec_ref[0:1, :])
+    sums_ref[0:1, :] += gain
+    sums_ref[1:2, :] += shift
+    out_ref[...] = (gm_ref[...] + back).astype(BF16)
+
+
+def first_back_call(a, b, gm, tok, vecs, part):
+    width = a.shape[1]
+    base = part * 2
+    row = pl.BlockSpec((256, width), lambda i: (i, 0))
+    off = pl.BlockSpec((256, width), lambda i: (i + base, 0))
+    return pl.pallas_call(
+        first_back_kernel,
+        grid=(2,),
+        in_specs=[row, row, off, off, whole(vecs.shape)],
+        out_specs=[row, whole((8, width))],
+        out_shape=[jax.ShapeDtypeStruct((512, width), BF16), jax.ShapeDtypeStruct((8, width), F32)],
+        compiler_params=params(dimension_semantics=("arbitrary",)),
+        cost_estimate=cost(1e7, 6e6),
+        name="first_back%d" % part,
+    )(a, b, gm, tok, vecs)
+
+
+def device_pairs(dp_count, move, back=False):
+    pairs = []
+    for dp in range(dp_count):
+        for seq in range(8):
+            y, c, z, x = move(dp // 2, dp % 2, seq // 2, seq % 2)
+            pair = (dp * 8 + seq, (y * 2 + c) * 8 + z * 2 + x)
+            pairs.append(pair[::-1] if back else pair)
+    return pairs
+
+
+def home_body(
+    tokens, encoder_states, out_grad, block_map, branch_fork, norm_gain, norm_bias, self_in,
+    self_out, self_bias, cross_in, cross_out, cross_bias, up_weight, up_bias, down_weight, down_bias,
+):
+    dp_count = lax.axis_size("dp")
+    dp, seq = lax.axis_index("dp"), lax.axis_index("seq")
+    c, z, x = dp & 1, seq >> 1, seq & 1
+    y = dp >> 1
+    flat = dp * 8 + seq
+    hset = 2 * c + x
+    parity = z & 1
+    rows, width = tokens.shape[1:]
+    frames = encoder_states.shape[1]
+
+    def send(v, move, back=False):
+        return lax.ppermute(v, AXES, device_pairs(dp_count, move, back))
+
+    def flip(k):
+        return lambda y, c, z, x: (y, c ^ (k >> 1), z, x ^ (k & 1))
+
+    def home(p):
+        return lambda y, c, z, x: (y, z >> 1, 2 * c + (p ^ (z & 1)), x)
+
+    def pick(v, p):
+        return jnp.where(parity == p, v[0], v[1])
+
+    def piece(v, parts):
+        return v.reshape(parts, -1).astype(BF16)
+
+    small = jnp.concatenate(
+        [v.reshape(-1) for v in (norm_gain, norm_bias, self_bias, cross_bias, down_bias, up_bias)]
+    )
+    small = jnp.pad(small, (0, 8 * 192 - small.shape[0])).reshape(8, 192)
+    shard = self_in.reshape(-1, width)
+    options = jnp.stack(
+        [jnp.concatenate([shard[:, 192 * j : 192 * j + 192], small]) for j in range(4)]
+    )
+
+    def merge(own, other, bit):
+        return jnp.stack([jnp.where(bit == 0, own, other), jnp.where(bit == 0, other, own)])
+
+    def option(k):
+        return lax.dynamic_index_in_dim(options, hset ^ k, 0, False)
+
+    got = [option(0)] + [send(option(k), flip(k)) for k in (1, 2, 3)]
+    tree = merge(merge(got[0], got[1], x), merge(got[2], got[3], x), c)
+    tree = merge(tree, send(tree, lambda y, c, z, x: (y, c, z ^ 2, x)), z >> 1)
+    tree = merge(tree, send(tree, lambda y, c, z, x: (y, c, z ^ 1, x)), z & 1)
+    for bit in range((dp_count // 2).bit_length() - 1):
+        tree = merge(
+            tree, send(tree, lambda y, c, z, x, bit=bit: (y ^ (1 << bit), c, z, x)), (y >> bit) & 1
+        )
+    y_count = dp_count // 2
+    nw = shard.shape[0] // 3
+    tree = tree.reshape(y_count, 2, 2, 2, 2, 3 * nw + 8, 192).transpose(0, 3, 2, 1, 4, 5, 6)
+    tree = tree.reshape(dp_count * 8, 3 * nw + 8, 192)
+    w2 = jnp.concatenate(
+        [tree[:, t * nw : (t + 1) * nw].reshape(width, 192) for t in range(3)], axis=1
+    )
+    flats = tree[:, 3 * nw :].reshape(dp_count * 8, -1)
+    lists = [
+        flats[:, i * nw : (i + 1) * nw].reshape(1, width) for i in range(13)
+    ]
+    tiles = up_weight.shape[1] // width
+    ub4 = flats[:, 13 * nw : (13 + tiles) * nw].reshape(tiles, width).astype(F32)
+    vecs = jnp.concatenate(lists + [jnp.zeros((3, width), BF16)]).astype(F32)
+    own_cols = lambda v: lax.dynamic_slice_in_dim(v, hset * 192, 192, 1)
+    zero_row = jnp.zeros((1, 192), F32)
+    qkv_bias = jnp.concatenate([own_cols(vecs[6:7]), zero_row, own_cols(vecs[7:8])], axis=1)
+
+    both = jnp.concatenate([tokens, encoder_states], axis=1)
+    mine = [send(pick(both, p), home(p)) for p in range(2)]
+    across = [send(v, flip(1)) for v in mine]
+    near = [send(v, flip(2)) for v in mine]
+    far = [send(v, flip(2)) for v in across]
+    pieces = mine + across + near + far
+
+    info = jnp.concatenate([block_map, branch_fork], axis=1)
+    info = jnp.where((z >> 1) == c, info, send(info, flip(2)))
+    info = jnp.where(parity == 0, info[0], info[1])
+    place = jnp.arange(32, dtype=jnp.int32)
+    k_of, p_of = place >> 3, (place >> 2) & 1
+    stored = (2 * (2 * (c ^ (k_of >> 1)) + (p_of ^ parity)) + (x ^ (k_of & 1))) * 4 + (place & 3)
+    logical = jnp.sum(jnp.where(stored[:, None] == place[None, :], info[None, :32], 0), axis=1)
+    spot = jnp.sum(jnp.where(logical[None, :] == place[:, None], place[None, :], 0), axis=1)
+    meta = jnp.concatenate(
+        [logical, spot, info[32:40], jnp.full((56,), hset, jnp.int32)]
+    ).astype(jnp.int32)
+
+    dense = jnp.concatenate(
+        [down_weight]
+        + [up_weight[:, j * width : (j + 1) * width] for j in range(tiles)]
+        + [self_out, cross_in[0], cross_in[1], cross_in[2], cross_out]
+    )
+    dense = lax.all_gather(dense, AXES, axis=0)
+    nd = down_weight.shape[0]
+
+    def gathered(i):
+        at = nd + i * nw
+        return dense[:, at : at + nw].reshape(width, width)
+
+    dn4 = dense[:, :nd].reshape(tiles, width, width)
+    up4 = jnp.stack([gathered(j) for j in range(tiles)])
+    so = gathered(tiles)
+    ci = jnp.stack([gathered(tiles + 1 + t) for t in range(3)])
+    co = gathered(tiles + 4)
+
+    q, kv, tr, n1 = qkv_call(meta, pieces, w2, vecs, qkv_bias)
+    og_pair, _ = lax.optimization_barrier((out_grad, far[1]))
+    og = jnp.concatenate([send(pick(og_pair, p), home(p)) for p in range(2)])
+    tok = jnp.concatenate([v[:rows] for v in mine])
+    all_frames = jnp.concatenate([v[rows:] for v in pieces])
+
+    o, lse = attend_call(meta, q, kv, tr)
+    o4 = o.reshape(4, 1024, 192)
+    o_home = [o4[0]] + [send(o4[k], flip(k)) for k in (1, 2, 3)]
+    mid, ac, n2, n3, cq, ca, lse_c, kc, vc = mid_call(
+        meta, tok, o_home, so, ci, co, all_frames, vecs
+    )
+    res, gt, ug, dg, ubg, dbg = feed_call(n3, og, ac, up4, dn4, ub4, vecs)
+    gm, d0, d1, d2, d3, sog, cig, cog, eg, sums = mid_back_call(
+        meta, gt, og, ac, mid, n2, cq, ca, lse_c, kc, vc, all_frames, so, ci, co, vecs, o_home
+    )
+    d_home = [d0] + [send(d, flip(k)) for k, d in ((1, d1), (2, d2), (3, d3))]
+
+    def rows_of(grad):
+        return grad.reshape(dp_count * 8, -1, width)
+
+    packed = jnp.concatenate(
+        [rows_of(dg)] + [rows_of(ug[j]) for j in range(tiles)]
+        + [rows_of(sog), rows_of(cig[0]), rows_of(cig[1]), rows_of(cig[2]), rows_of(cog)],
+        axis=1,
+    )
+    dense_grad = lax.psum_scatter(packed, AXES, scatter_dimension=0, tiled=True)[0].astype(F32)
+
+    dqkv = attend_back_call(meta, q, kv, tr, o, lse, d_home)
+    dx3 = dx_call(meta, dqkv, w2, 3)
+    near3 = send(dx3, flip(2))
+    dx1 = dx_call(meta, dqkv, w2, 1)
+    side = (dx1.astype(F32) + near3.astype(F32)).astype(BF16)
+    side = [send(side[p * rows : (p + 1) * rows], flip(1)) for p in range(2)]
+    dx2 = dx_call(meta, dqkv, w2, 2)
+    near2 = send(dx2, flip(2))
+    dx0 = dx_call(meta, dqkv, w2, 0)
+    own = (dx0.astype(F32) + near2.astype(F32)).astype(BF16)
+
+    wg, colsum = win_call(n1, dqkv)
+    wg = wg.reshape(y_count, 2, 4, 2, nw, 576)
+
+    def halve(v, move, bit, axis):
+        keep = lax.dynamic_index_in_dim(v, bit, axis, False)
+        give = lax.dynamic_index_in_dim(v, 1 - bit, axis, False)
+        return (keep.astype(F32) + send(give, move).astype(F32)).astype(BF16)
+
+    for bit in reversed(range((dp_count // 2).bit_length() - 1)):
+        half = wg.shape[0] // 2
+        wg = halve(
+            wg.reshape((2, half) + wg.shape[1:]),
+            lambda y, c, z, x, bit=bit: (y ^ (1 << bit), c, z, x), (y >> bit) & 1, 0,
+        )
+    wg = wg.reshape(2, 2, 2, 2, nw, 576)
+    wg = halve(wg, lambda y, c, z, x: (y, c, z ^ 1, x), z & 1, 2)
+    wg = halve(wg, lambda y, c, z, x: (y, c, z ^ 2, x), z >> 1, 1)
+    wg = wg.reshape(4, nw, 576)
+
+    def shard_for(k):
+        return lax.dynamic_index_in_dim(wg, hset ^ k, 0, False)
+
+    parts = jnp.stack([shard_for(0)] + [send(shard_for(k), flip(k)) for k in (1, 2, 3)])
+    cols = [lax.dynamic_index_in_dim(parts, hset ^ j, 0, False) for j in range(4)]
+    self_in_grad = jnp.stack(
+        [jnp.concatenate([v[:, 192 * t : 192 * t + 192] for v in cols], axis=1) for t in range(3)]
+    ).astype(F32)
+
+    grads, first_sums = [], None
+    for p in range(2):
+        tg, s = first_back_call(own[p * rows : (p + 1) * rows], side[p], gm, tok, vecs, p)
+        grads.append(send(tg, home(p), True))
+        first_sums = s if first_sums is None else first_sums + s
+    results = [send(res[p * rows : (p + 1) * rows], home(p), True) for p in range(2)]
+    eg4 = eg.reshape(4, 2 * frames, width)
+    eg_near = send(eg4[2:4], flip(2)).astype(F32)
+    eg_side = (eg4[1].astype(F32) + eg_near[1]).astype(BF16)
+    eg_sum = eg4[0].astype(F32) + eg_near[0] + send(eg_side, flip(1)).astype(F32)
+    eg_sum = eg_sum.astype(BF16)
+    eg_back = [send(eg_sum[p * frames : (p + 1) * frames], home(p), True) for p in range(2)]
+
+    def returned(pair, dtype):
+        pair = [v.astype(dtype) for v in pair]
+        return jnp.stack([jnp.where(parity == 0, pair[0], pair[1]), jnp.where(parity == 0, pair[1], pair[0])])
+
+    own_bias = lambda v: lax.dynamic_update_slice(
+        jnp.zeros((1, width), F32), v, (0, hset * 192)
+    )
+    ubg = ubg.reshape(tiles, 8, width)[:, 0]
+    table = jnp.concatenate(
+        [
+            first_sums[0:1], sums[1:3], first_sums[1:2], sums[4:6],
+            own_bias(colsum[0:1, 0:192]), own_bias(colsum[0:1, 384:576]), sums[8:12],
+            dbg[0:1], ubg, jnp.zeros((24 - 13 - tiles, width), F32),
+        ]
+    )
+    for k in (1, 2):
+        table = table + send(table, flip(k))
+    table = table + send(table, lambda y, c, z, x: (y, c, z ^ 1, x))
+    table = table + send(table, lambda y, c, z, x: (y, c, z ^ 2, x))
+    for bit in range((dp_count // 2).bit_length() - 1):
+        table = table + send(table, lambda y, c, z, x, bit=bit: (y ^ (1 << bit), c, z, x))
+    mine_of = lambda v: lax.dynamic_slice_in_dim(v, flat * nw, nw, 1)
+    vec_grad = mine_of(table[:13])
+    up_bias_grad = lax.dynamic_slice_in_dim(
+        table[13 : 13 + tiles].reshape(-1), flat * tiles * nw, tiles * nw, 0
+    )
+
+    def shard_grad(i):
+        at = nd + i * nw
+        return dense_grad[at : at + nw]
+
+    return (
+        returned(results, BF16),
+        returned(grads, F32),
+        returned(eg_back, F32),
+        vec_grad[0:3],
+        vec_grad[3:6],
+        self_in_grad,
+        shard_grad(tiles),
+        vec_grad[6:9],
+        jnp.stack([shard_grad(tiles + 1 + t) for t in range(3)]),
+        shard_grad(tiles + 4),
+        vec_grad[9:12],
+        jnp.concatenate([shard_grad(j) for j in range(tiles)], axis=1),
+        up_bias_grad,
+        dense_grad[:nd],
+        vec_grad[12],
+    )
+
+
 def solution(mesh):
     in_specs = (
         P("dp", "seq", None),
@@ -448,4 +1371,6 @@
         P(("dp", "seq"), None),
         P(("dp", "seq")),
     )
-    return jax.shard_map(body, mesh=mesh, in_specs=in_specs, out_specs=out_specs, check_vma=False)
+    sizes = dict(mesh.shape)
+    chosen = home_body if sizes["dp"] == 4 and sizes["seq"] == 8 else body
+    return jax.shard_map(chosen, mesh=mesh, in_specs=in_specs, out_specs=out_specs, check_vma=False)

time: 2790 us -> 752 us (0.27)
  waiting for transfers between devices: 1210 us -> 189 us
  matrix products: 701 us -> 0 us
  blocking collectives: 516 us -> 0 us
  Pallas kernels: 0 us -> 351 us
  other arithmetic: 224 us -> 23.9 us
  starting transfers between devices: 1.25 us -> 80.5 us
  local copies, waits for them, and re-layouts: 106 us -> 77.8 us
    reduce_scatter x10 -> x1, waiting for transfers between devices: 880 us -> 0.01 us  [home_body(): lax.psum_scatter(packed, AXES, scatter_dimension=0, tiled=True)[0]]
    dot_general x80 -> x0, matrix products: 602 us -> none  [the longest x4 142 us: attend_backward(): jnp.einsum('rhd,khd->hrk', grad_heads, head_split(value_rows), preferred_...]
    all_gather x8 -> x0, blocking collectives: 393 us -> none  [the longest x2 133 us: fetch_cross(): lax.all_gather(shards[7], ('dp', 'seq'), axis=1, tiled=True)]
    pallas_call x0 -> x13, Pallas kernels: none -> 351 us  [the longest x1 87.7 us: attend_back_call(): pl.pallas_call(attend_back_kernel, grid_spec=pltpu.PrefetchScalarGridSpec...]
    all_gather x16 -> x1, waiting for transfers between devices: 322 us -> 0.01 us  [home_body(): dense = lax.all_gather(dense, AXES, axis=0)]
    ppermute x0 -> x46, waiting for transfers between devices: none -> 189 us  [send(): return lax.ppermute(v, AXES, device_pairs(dp_count, move, back))]
    convert_element_type x20 -> x12, other arithmetic: 179 us -> 5.16 us  [the longest x1 1.87 us: home_body(): side = (dx1.astype(F32) + near3.astype(F32)).astype(BF16)]
    sub x4 -> x0, matrix products: 98.9 us -> none  [the longest x2 89.1 us: attend_backward(): shares_full = jnp.exp(scores - row_max) / row_total]
  transfers between devices with their start and end apart: 30 -> 48, of which waited for: 18 -> 17; matrix products, arithmetic and copies ran while one was open for 33% -> 9% of each run, Pallas kernels for 0% -> 32%
where the time goes in v1:
time: 752 us; the launch traced here: 737 us
  Pallas kernels  351 us (47%)
  waiting for transfers between devices  189 us (25%)
  starting transfers between devices  80.5 us (11%)
  local copies, waits for them, and re-layouts  77.8 us (10%)
  other arithmetic  23.9 us (3%)
  between operations  15.1 us (2%)
    ppermute x46, waiting for transfers between devices, send(): return lax.ppermute(v, AXES, device_pairs(dp_count, move, back))  189 us
    pallas_call x1, Pallas kernels, attend_back_call(): pl.pallas_call(attend_back_kernel, grid_spec=pltpu.PrefetchScalarGridSpec...  87.7 us
    pallas_call x1, Pallas kernels, attend_call(): pl.pallas_call(attend_kernel, grid_spec=pltpu.PrefetchScalarGridSpec(num_...  83.2 us
    ppermute x46, starting transfers between devices, send(): return lax.ppermute(v, AXES, device_pairs(dp_count, move, back))  80.4 us
    pallas_call x1, Pallas kernels, feed_call(): pl.pallas_call(feed_kernel, grid=(tiles,), in_specs=[whole(n3.shape), who...  43.1 us
    pallas_call x1, Pallas kernels, mid_back_call(): pl.pallas_call(mid_back_kernel, grid_spec=pltpu.PrefetchScalarGridSpec(nu...  41.2 us
    unnamed x82, local copies, waits for them, and re-layouts  34.6 us
    pallas_call x4, Pallas kernels, dx_call(): pl.pallas_call(functools.partial(dx_kernel, piece=piece), grid_spec=pltpu...  33.5 us
  transfers between devices with their start and end apart: 48, of which 17 were waited for; matrix products, arithmetic and copies ran while one was open for 9% of the time, Pallas kernels for 32%

profile of v1, /device:TPU:20, one launch (start us, length us, event | category | flops | bytes accessed | tf_op | source)
XLA Modules:
  0.0 736.9 jit_solution(15134891683241332550)
XLA Ops:
  30.1 70.5 %collective-permute-done.12 = bf16[2,2,80,192]{3,2,1,0:T(8,128)(2,1)S(1)} collective-permute-done((bf16[2,2,80,192]{3,2,1,0:T(8,128)(2,1)S(1)}, bf16[2,2,80,192]{3,2,1,0:T(8,128)(2,1)S(1)}, u32[]{:S(2)}, u32[]{:S(2)}) %collective-permute-start.12) | collective-permute-done | bytes 122912 | tf_op jit(solution)/shard_map/ppermute | solution.py:1115
  101.7 27.3 %collective-permute-done.13 = bf16[2,2,2,80,192]{4,3,2,0,1:T(8,128)(2,1)S(1)} collective-permute-done((bf16[2,2,2,80,192]{4,3,2,0,1:T(8,128)(2,1)S(1)}, bf16[2,2,2,80,192]{4,3,2,0,1:T(8,128)(2,1)S(1)}, u32[]{:S(2)}, u32[]{:S(2)}) %collective-permute-start.13) | collective-permute-done | bytes 245792 | tf_op jit(solution)/shard_map/ppermute | solution.py:1115
  138.1 8.8 %collective-permute-done.14 = bf16[2,2,2,2,80,192]{5,4,3,0,1,2:T(8,128)(2,1)S(1)} collective-permute-done((bf16[2,2,2,2,80,192]{5,4,3,0,1,2:T(8,128)(2,1)S(1)}, bf16[2,2,2,2,80,192]{5,4,3,0,1,2:T(8,128)(2,1)S(1)}, u32[]{:S(2)}, u32[]{:S(2)}) %collective-permute-start.14) | collective-permute-done | bytes 491552 | tf_op jit(solution)/shard_map/ppermute | solution.py:1115
  156.2 16.9 %collective-permute-done.4.refs_3_ = bf16[544,768]{1,0:T(8,128)(2,1)} collective-permute-done((bf16[544,768]{1,0:T(8,128)(2,1)}, bf16[544,768]{1,0:T(8,128)(2,1)}, u32[]{:S(2)}, u32[]{:S(2)}) %collective-permute-start.4) | collective-permute-done | bytes 835616 | tf_op jit(solution)/shard_map/ppermute | solution.py:1115
  183.2 17.5 %qkv.1 = (bf16[3,4096,128]{2,1,0:T(8,128)(2,1)}, bf16[3,4096,128]{2,1,0:T(8,128)(2,1)}, bf16[6,64,4096]{2,1,0:T(8,128)(2,1)}, bf16[4096,768]{1,0:T(8,128)(2,1)}) custom-call(s32[128]{0:T(128)} %pad_add_fusion.1.meta, bf16[544,768]{1,0:T(8,128)(2,1)} %collective-permute-done.1.refs_0_, bf16[544,768]{1,0:T(8,128)(2,1)} %collective-permute-done.2.refs_1_, ...), custom_call_target="tpu_custom_call" | custom-call | flops 3623878656 | bytes 20000000 | tf_op jit(solution)/shard_map/qkv/pallas_call | solution.py:517
  200.8 83.2 %attend.1 = (bf16[32,128,192]{2,1,0:T(8,128)(2,1)}, f32[8,4096]{1,0:T(8,128)}) custom-call(s32[128]{0:T(128)} %pad_add_fusion.1.meta, bf16[3,4096,128]{2,1,0:T(8,128)(2,1)} %get-tuple-element.53.q_ref, bf16[3,4096,128]{2,1,0:T(8,128)(2,1)} %get-tuple-element.54.kv_ref, bf16[6,64,4096]{2,1,0:T(8,128)(2,1)} %get-tuple-element.55.tr_ref), custom_call_target="tpu_custom_call" | custom-call | flops 20000000000 | bytes 10000000 | tf_op jit(solution)/shard_map/attend/pallas_call | solution.py:600
  297.2 5.9 fusion.19
  312.4 27.8 %middle.1 = (f32[1024,768]{1,0:T(8,128)}, f32[1024,768]{1,0:T(8,128)}, bf16[1024,768]{1,0:T(8,128)(2,1)}, bf16[1024,768]{1,0:T(8,128)(2,1)}, bf16[1024,768]{1,0:...) custom-call(s32[128]{0:T(128)} %pad_add_fusion.1.meta, ...), custom_call_target="tpu_custom_call" | custom-call | flops 8000000000 | bytes 25000000 | tf_op jit(solution)/shard_map/middle/pallas_call | solution.py:837
  340.2 43.1 %feed.1 = (bf16[1024,768]{1,0:T(8,128)(2,1)}, f32[1024,768]{1,0:T(8,128)}, bf16[4,768,768]{2,1,0:T(8,128)(2,1)}, bf16[4,768,768]{2,1,0:T(8,128)(2,1)}, f32[32,768]{1,0:T(8,128)}, /*index=5*/f32[8,768]{1,0:T(8,128)}) custom-call(bf16[1024,768]{1,0:T(8,128)(2,1)} %get-tuple-element.57.n3_ref, bf16[1024,768]{1,0:T(8,128)(2,1)} %constant_dynamic-update-slice_fusion.20.og_ref, ...), custom_call_target="tpu_custom_call" | custom-call | flops 28991029248 | bytes 35000000 | tf_op jit(solution)/shard_map/feed/pallas_call | solution.py:917
  383.3 41.2 %middle_back.1 = (f32[1024,768]{1,0:T(8,128)}, bf16[1024,192]{1,0:T(8,128)(2,1)}, bf16[1024,192]{1,0:T(8,128)(2,1)}, bf16[1024,192]{1,0:T(8,128)(2,1)}, bf16[102...) custom-call(s32[128]{0:T(128)} %pad_add_fusion.1.meta, ...), custom_call_target="tpu_custom_call" | custom-call | flops 22000001024 | bytes 35000000 | tf_op jit(solution)/shard_map/middle_back/pallas_call | solution.py:1037
  453.2 9.4 %collective-permute-start.20 = (bf16[512,768]{1,0:T(8,128)(2,1)}, bf16[512,768]{1,0:T(8,128)(2,1)}, u32[]{:S(2)}, u32[]{:S(2)}) collective-permute-start(bf16[512,768]{1,0:T(8,128)(2,1)} %get-tuple-element.121), channel_id=1, source_target_pairs={{0,0},{1,1},{2,2},{3,3},{8,4},{9,5},{10,6},{11,7},{4,8},{5,9},{6,1... | collective-permute-start | bytes 2359304 | tf_op jit(solution)/shard_map/ppermute | solution.py:1115
  468.2 7.1 collective-permute-start.33
  476.1 87.7 %attend_back.1.d_ref = bf16[4096,576]{1,0:T(8,128)(2,1)} custom-call(s32[128]{0:T(128)} %pad_add_fusion.1.meta, bf16[3,4096,128]{2,1,0:T(8,128)(2,1)} %get-tuple-element.53.q_ref, bf16[3,4096,128]{2,1,0:T(8,128)(2,1)} %get-tuple-element.54.kv_ref, bf16[6,64,4096]{2,1,0:T(8,128)(2,1)} %get-tuple-element.55.tr_ref, ...), custom_call_target="tpu_custom_call" | custom-call | flops 49999998976 | bytes 15000000 | tf_op jit(solution)/shard_map/attend_back/pallas_call | solution.py:688
  563.8 9.3 %win.1 = (bf16[768,576]{1,0:T(8,128)(2,1)}, f32[8,576]{1,0:T(8,128)}) custom-call(bf16[4096,768]{1,0:T(8,128)(2,1)} %get-tuple-element.81.n_ref, bf16[4096,576]{1,0:T(8,128)(2,1)} %attend_back.1.d_ref), custom_call_target="tpu_custom_call" | custom-call | flops 3623878656 | bytes 12000000 | tf_op jit(solution)/shard_map/win/pallas_call | solution.py:749
  574.2 15.1 %collective-permute-start.40 = (bf16[1,2,4,2,24,576]{5,4,3,2,1,0:T(8,128)(2,1)S(1)}, bf16[1,2,4,2,24,576]{5,4,3,2,1,0:T(8,128)(2,1)S(1)}, u32[]{:S(2)}, u32[]{:S(2)}) collective-permute-start(bf16[1,2,4,2,24,576]{5,4,3,2,1,0:T(8,128)(2,1)S(1)} %dynamic-slice_bitcast_fusion), channel_id=1, source_target_pairs={{0,16},{1,17},{2,18},{3,19},{4,20},{5,21},{6,22},{7,23},{8,24},{9,... | collective-permute-start | bytes 1327112 | tf_op jit(solution)/shard_map/ppermute | solution.py:1115
  590.0 8.6 %dx2.1 = bf16[1024,768]{1,0:T(8,128)(2,1)} custom-call(s32[128]{0:T(128)} %pad_add_fusion.1.meta, bf16[4096,576]{1,0:T(8,128)(2,1)} %attend_back.1.d_ref, bf16[768,576]{1,0:T(8,128)(2,1)} %pad_maximum_fusion.6.refs_8_.w_ref), custom_call_target="tpu_custom_call" | custom-call | flops 905969664 | bytes 6000000 | tf_op jit(solution)/shard_map/dx2/pallas_call | solution.py:716
  602.2 8.3 %dx3.1 = bf16[1024,768]{1,0:T(8,128)(2,1)} custom-call(s32[128]{0:T(128)} %pad_add_fusion.1.meta, bf16[4096,576]{1,0:T(8,128)(2,1)} %attend_back.1.d_ref, bf16[768,576]{1,0:T(8,128)(2,1)} %pad_maximum_fusion.6.refs_8_.w_ref), custom_call_target="tpu_custom_call" | custom-call | flops 905969664 | bytes 6000000 | tf_op jit(solution)/shard_map/dx3/pallas_call | solution.py:716
  610.9 8.3 %dx1.1 = bf16[1024,768]{1,0:T(8,128)(2,1)} custom-call(s32[128]{0:T(128)} %pad_add_fusion.1.meta, bf16[4096,576]{1,0:T(8,128)(2,1)} %attend_back.1.d_ref, bf16[768,576]{1,0:T(8,128)(2,1)} %pad_maximum_fusion.6.refs_8_.w_ref), custom_call_target="tpu_custom_call" | custom-call | flops 905969664 | bytes 6000000 | tf_op jit(solution)/shard_map/dx1/pallas_call | solution.py:716
  619.1 8.3 %dx0.1 = bf16[1024,768]{1,0:T(8,128)(2,1)} custom-call(s32[128]{0:T(128)} %pad_add_fusion.1.meta, bf16[4096,576]{1,0:T(8,128)(2,1)} %attend_back.1.d_ref, bf16[768,576]{1,0:T(8,128)(2,1)} %pad_maximum_fusion.6.refs_8_.w_ref), custom_call_target="tpu_custom_call" | custom-call | flops 905969664 | bytes 6000000 | tf_op jit(solution)/shard_map/dx0/pallas_call | solution.py:716
  627.6 9.8 %collective-permute-start.42 = (bf16[2,2,24,576]{3,2,1,0:T(8,128)(2,1)S(1)}, bf16[2,2,24,576]{3,2,1,0:T(8,128)(2,1)S(1)}, u32[]{:S(2)}, u32[]{:S(2)}) collective-permute-start(bf16[2,2,24,576]{3,2,1,0:T(8,128)(2,1)S(1)} %dynamic-slice_bitcast_fusion.2), channel_id=1, source_target_pairs={{0,4},{1,5},{2,6},{3,7},{4,0},{5,1},{6,2},{7,3},{8,12},{9,13},{10,... | collective-permute-start | bytes 331784 | tf_op jit(solution)/shard_map/ppermute | solution.py:1115
  654.7 16.5 %collective-permute-done.29.b_ref = bf16[512,768]{1,0:T(8,128)(2,1)S(1)} collective-permute-done((bf16[512,768]{1,0:T(8,128)(2,1)S(1)}, bf16[512,768]{1,0:T(8,128)(2,1)S(1)}, u32[]{:S(2)}, u32[]{:S(2)}) %collective-permute-start.29) | collective-permute-done | bytes 786464 | tf_op jit(solution)/shard_map/ppermute | solution.py:1115
  675.9 10.1 %collective-permute-done.27.b_ref = bf16[512,768]{1,0:T(8,128)(2,1)S(1)} collective-permute-done((bf16[512,768]{1,0:T(8,128)(2,1)}, bf16[512,768]{1,0:T(8,128)(2,1)S(1)}, u32[]{:S(2)}, u32[]{:S(2)}) %collective-permute-start.27) | collective-permute-done | bytes 786464 | tf_op jit(solution)/shard_map/ppermute | solution.py:1115
  698.8 8.8 %collective-permute-done.37 = f32[24,768]{1,0:T(8,128)S(1)} collective-permute-done((f32[24,768]{1,0:T(8,128)S(1)}, f32[24,768]{1,0:T(8,128)S(1)}, u32[]{:S(2)}, u32[]{:S(2)}) %collective-permute-start.37) | collective-permute-done | bytes 73760 | tf_op jit(solution)/shard_map/ppermute | solution.py:1115
  707.8 8.8 %collective-permute-done.38 = f32[24,768]{1,0:T(8,128)S(1)} collective-permute-done((f32[24,768]{1,0:T(8,128)S(1)}, f32[24,768]{1,0:T(8,128)S(1)}, u32[]{:S(2)}, u32[]{:S(2)}) %collective-permute-start.38) | collective-permute-done | bytes 73760 | tf_op jit(solution)/shard_map/ppermute | solution.py:1115
  (309 shorter events, 163.5 us)
Async XLA Ops:
  7.2 285.1 %all-gather.3.cloned.1.call-start = ((), (), s32[]{:S(2)}) async-start(), calls=%async_computation.2 | async-start | bytes 15814656 | tf_op jit(solution)/shard_map/all_gather | solution.py:1194
  16.0 709.1 %reduce-scatter.2.cloned.1.call-start = ((), (), s32[]{:S(2)}) async-start(), calls=%async_computation.1 | async-start | bytes 15814656 | tf_op jit(solution)/shard_map/reduce_scatter | solution.py:1233
  24.9 105.0 %collective-permute-start.1 = (bf16[544,768]{1,0:T(8,128)(2,1)S(1)}, bf16[544,768]{1,0:T(8,128)(2,1)}, u32[]{:S(2)}, u32[]{:S(2)}) collective-permute-start(bf16[544,768]{1,0:T(8,128)(2,1)S(1)} %get-tuple-element.111), channel_id=1, source_target_pairs={{0,0},{1,1},{2,2},{3,3},{4,8},{5,9},{6,10},{7,11},{8,4},{9,5},{10,... | collective-permute-start | bytes 2506760 | tf_op jit(solution)/shard_map/ppermute | solution.py:1115
  27.1 104.0 %collective-permute-start.2 = (bf16[544,768]{1,0:T(8,128)(2,1)S(1)}, bf16[544,768]{1,0:T(8,128)(2,1)}, u32[]{:S(2)}, u32[]{:S(2)}) collective-permute-start(bf16[544,768]{1,0:T(8,128)(2,1)S(1)} %get-tuple-element.112), channel_id=1, source_target_pairs={{0,2},{1,3},{2,0},{3,1},{4,10},{5,11},{6,8},{7,9},{8,6},{9,7},{10,... | collective-permute-start | bytes 2506760 | tf_op jit(solution)/shard_map/ppermute | solution.py:1115
  30.0 70.6 %collective-permute-start.12 = (bf16[2,2,80,192]{3,2,1,0:T(8,128)(2,1)S(1)}, bf16[2,2,80,192]{3,2,1,0:T(8,128)(2,1)S(1)}, u32[]{:S(2)}, u32[]{:S(2)}) collective-permute-start(bf16[2,2,80,192]{3,2,1,0:T(8,128)(2,1)S(1)} %pad_maximum_fusion.13), channel_id=1, source_target_pairs={{0,4},{1,5},{2,6},{3,7},{4,0},{5,1},{6,2},{7,3},{8,12},{9,13},{10,... | collective-permute-start | bytes 368648 | tf_op jit(solution)/shard_map/ppermute | solution.py:1115
  100.7 28.3 %collective-permute-start.13 = (bf16[2,2,2,80,192]{4,3,2,0,1:T(8,128)(2,1)S(1)}, bf16[2,2,2,80,192]{4,3,2,0,1:T(8,128)(2,1)S(1)}, u32[]{:S(2)}, u32[]{:S(2)}) collective-permute-start(bf16[2,2,2,80,192]{4,3,2,0,1:T(8,128)(2,1)S(1)} %pad_maximum_fusion.8), channel_id=1, source_target_pairs={{0,2},{1,3},{2,0},{3,1},{4,6},{5,7},{6,4},{7,5},{8,10},{9,11},{10,... | collective-permute-start | bytes 737288 | tf_op jit(solution)/shard_map/ppermute | solution.py:1115
  133.6 41.1 %collective-permute-start.5 = (bf16[544,768]{1,0:T(8,128)(2,1)}, bf16[544,768]{1,0:T(8,128)(2,1)}, u32[]{:S(2)}, u32[]{:S(2)}) collective-permute-start(bf16[544,768]{1,0:T(8,128)(2,1)} %collective-permute-done.1.refs_0_), channel_id=1, source_target_pairs={{0,8},{1,9},{2,10},{3,11},{4,12},{5,13},{6,14},{7,15},{8,0},{9,1},... | collective-permute-start | bytes 2506760 | tf_op jit(solution)/shard_map/ppermute | solution.py:1115
  135.9 39.7 %collective-permute-start.6 = (bf16[544,768]{1,0:T(8,128)(2,1)}, bf16[544,768]{1,0:T(8,128)(2,1)}, u32[]{:S(2)}, u32[]{:S(2)}) collective-permute-start(bf16[544,768]{1,0:T(8,128)(2,1)} %collective-permute-done.2.refs_1_), channel_id=1, source_target_pairs={{0,8},{1,9},{2,10},{3,11},{4,12},{5,13},{6,14},{7,15},{8,0},{9,1},... | collective-permute-start | bytes 2506760 | tf_op jit(solution)/shard_map/ppermute | solution.py:1115
  135.9 37.3 %collective-permute-start.4 = (bf16[544,768]{1,0:T(8,128)(2,1)}, bf16[544,768]{1,0:T(8,128)(2,1)}, u32[]{:S(2)}, u32[]{:S(2)}) collective-permute-start(bf16[544,768]{1,0:T(8,128)(2,1)} %collective-permute-done.2.refs_1_), channel_id=1, source_target_pairs={{0,1},{1,0},{2,3},{3,2},{4,5},{5,4},{6,7},{7,6},{8,9},{9,8},{10,11... | collective-permute-start | bytes 2506760 | tf_op jit(solution)/shard_map/ppermute | solution.py:1115
  156.2 27.0 %collective-permute-start.7 = (bf16[544,768]{1,0:T(8,128)(2,1)}, bf16[544,768]{1,0:T(8,128)(2,1)}, u32[]{:S(2)}, u32[]{:S(2)}) collective-permute-start(bf16[544,768]{1,0:T(8,128)(2,1)} %collective-permute-done.3.refs_2_), channel_id=1, source_target_pairs={{0,8},{1,9},{2,10},{3,11},{4,12},{5,13},{6,14},{7,15},{8,0},{9,1},... | collective-permute-start | bytes 2506760 | tf_op jit(solution)/shard_map/ppermute | solution.py:1115
  176.5 114.9 %collective-permute-start.19 = (bf16[512,768]{1,0:T(8,128)(2,1)S(1)}, bf16[512,768]{1,0:T(8,128)(2,1)S(1)}, u32[]{:S(2)}, u32[]{:S(2)}) collective-permute-start(bf16[512,768]{1,0:T(8,128)(2,1)S(1)} %get-tuple-element.123), channel_id=1, source_target_pairs={{0,2},{1,3},{2,0},{3,1},{4,10},{5,11},{6,8},{7,9},{8,6},{9,7},{10,... | collective-permute-start | bytes 2359304 | tf_op jit(solution)/shard_map/ppermute | solution.py:1115
  178.4 112.0 %collective-permute-start.18 = (bf16[512,768]{1,0:T(8,128)(2,1)S(1)}, bf16[512,768]{1,0:T(8,128)(2,1)S(1)}, u32[]{:S(2)}, u32[]{:S(2)}) collective-permute-start(bf16[512,768]{1,0:T(8,128)(2,1)S(1)} %get-tuple-element.124), channel_id=1, source_target_pairs={{0,0},{1,1},{2,2},{3,3},{4,8},{5,9},{6,10},{7,11},{8,4},{9,5},{10,... | collective-permute-start | bytes 2359304 | tf_op jit(solution)/shard_map/ppermute | solution.py:1115
  288.3 24.1 %collective-permute-start.15 = (bf16[1024,192]{1,0:T(8,128)(2,1)S(1)}, bf16[1024,192]{1,0:T(8,128)(2,1)}, u32[]{:S(2)}, u32[]{:S(2)}) collective-permute-start(bf16[1024,192]{1,0:T(8,128)(2,1)S(1)} %bitcast.220), channel_id=1, source_target_pairs={{0,1},{1,0},{2,3},{3,2},{4,5},{5,4},{6,7},{7,6},{8,9},{9,8},{10,11... | collective-permute-start | bytes 1179656 | tf_op jit(solution)/shard_map/ppermute | solution.py:1115
  453.2 184.2 %collective-permute-start.20 = (bf16[512,768]{1,0:T(8,128)(2,1)}, bf16[512,768]{1,0:T(8,128)(2,1)}, u32[]{:S(2)}, u32[]{:S(2)}) collective-permute-start(bf16[512,768]{1,0:T(8,128)(2,1)} %get-tuple-element.121), channel_id=1, source_target_pairs={{0,0},{1,1},{2,2},{3,3},{8,4},{9,5},{10,6},{11,7},{4,8},{5,9},{6,1... | collective-permute-start | bytes 2359304 | tf_op jit(solution)/shard_map/ppermute | solution.py:1115
  462.6 174.8 %collective-permute-start.21 = (bf16[512,768]{1,0:T(8,128)(2,1)}, bf16[512,768]{1,0:T(8,128)(2,1)}, u32[]{:S(2)}, u32[]{:S(2)}) collective-permute-start(bf16[512,768]{1,0:T(8,128)(2,1)} %get-tuple-element.122), channel_id=1, source_target_pairs={{2,0},{3,1},{0,2},{1,3},{10,4},{11,5},{8,6},{9,7},{6,8},{7,9},{4,1... | collective-permute-start | bytes 2359304 | tf_op jit(solution)/shard_map/ppermute | solution.py:1115
  465.9 123.4 %collective-permute-start.34 = (bf16[32,768]{1,0:T(8,128)(2,1)S(1)}, bf16[32,768]{1,0:T(8,128)(2,1)S(1)}, u32[]{:S(2)}, u32[]{:S(2)}) collective-permute-start(bf16[32,768]{1,0:T(8,128)(2,1)S(1)} %get-tuple-element.164), channel_id=1, source_target_pairs={{2,0},{3,1},{0,2},{1,3},{10,4},{11,5},{8,6},{9,7},{6,8},{7,9},{4,1... | collective-permute-start | bytes 147464 | tf_op jit(solution)/shard_map/ppermute | solution.py:1115
  468.2 121.1 %collective-permute-start.33 = (bf16[32,768]{1,0:T(8,128)(2,1)S(1)}, bf16[32,768]{1,0:T(8,128)(2,1)S(1)}, u32[]{:S(2)}, u32[]{:S(2)}) collective-permute-start(bf16[32,768]{1,0:T(8,128)(2,1)S(1)} %get-tuple-element.165), channel_id=1, source_target_pairs={{0,0},{1,1},{2,2},{3,3},{8,4},{9,5},{10,6},{11,7},{4,8},{5,9},{6,1... | collective-permute-start | bytes 147464 | tf_op jit(solution)/shard_map/ppermute | solution.py:1115
  574.2 26.8 %collective-permute-start.40 = (bf16[1,2,4,2,24,576]{5,4,3,2,1,0:T(8,128)(2,1)S(1)}, bf16[1,2,4,2,24,576]{5,4,3,2,1,0:T(8,128)(2,1)S(1)}, u32[]{:S(2)}, u32[]{:S(2)}) collective-permute-start(bf16[1,2,4,2,24,576]{5,4,3,2,1,0:T(8,128)(2,1)S(1)} %dynamic-slice_bitcast_fusion), channel_id=1, source_target_pairs={{0,16},{1,17},{2,18},{3,19},{4,20},{5,21},{6,22},{7,23},{8,24},{9,... | collective-permute-start | bytes 1327112 | tf_op jit(solution)/shard_map/ppermute | solution.py:1115
  598.6 54.4 %collective-permute-start.25 = (bf16[1024,768]{1,0:T(8,128)(2,1)}, bf16[1024,768]{1,0:T(8,128)(2,1)S(1)}, u32[]{:S(2)}, u32[]{:S(2)}) collective-permute-start(bf16[1024,768]{1,0:T(8,128)(2,1)} %dx2.1), channel_id=1, source_target_pairs={{0,8},{1,9},{2,10},{3,11},{4,12},{5,13},{6,14},{7,15},{8,0},{9,1},... | collective-permute-start | bytes 4718600 | tf_op jit(solution)/shard_map/ppermute | solution.py:1115
  601.1 26.3 %collective-permute-start.41 = (bf16[2,2,2,24,576]{4,3,2,1,0:T(8,128)(2,1)S(1)}, bf16[2,2,2,24,576]{4,3,2,1,0:T(8,128)(2,1)S(1)}, u32[]{:S(2)}, u32[]{:S(2)}) collective-permute-start(bf16[2,2,2,24,576]{4,3,2,1,0:T(8,128)(2,1)S(1)} %dynamic-slice_bitcast_fusion.1), channel_id=1, source_target_pairs={{0,2},{1,3},{2,0},{3,1},{4,6},{5,7},{6,4},{7,5},{8,10},{9,11},{10,... | collective-permute-start | bytes 663560 | tf_op jit(solution)/shard_map/ppermute | solution.py:1115
  610.5 37.5 %collective-permute-start.26 = (bf16[1024,768]{1,0:T(8,128)(2,1)}, bf16[1024,768]{1,0:T(8,128)(2,1)}, u32[]{:S(2)}, u32[]{:S(2)}) collective-permute-start(bf16[1024,768]{1,0:T(8,128)(2,1)} %dx3.1), channel_id=1, source_target_pairs={{0,8},{1,9},{2,10},{3,11},{4,12},{5,13},{6,14},{7,15},{8,0},{9,1},... | collective-permute-start | bytes 4718600 | tf_op jit(solution)/shard_map/ppermute | solution.py:1115
  651.9 34.2 %collective-permute-start.27 = (bf16[512,768]{1,0:T(8,128)(2,1)}, bf16[512,768]{1,0:T(8,128)(2,1)S(1)}, u32[]{:S(2)}, u32[]{:S(2)}) collective-permute-start(bf16[512,768]{1,0:T(8,128)(2,1)} %get-tuple-element.116), channel_id=1, source_target_pairs={{0,1},{1,0},{2,3},{3,2},{4,5},{5,4},{6,7},{7,6},{8,9},{9,8},{10,11... | collective-permute-start | bytes 2359304 | tf_op jit(solution)/shard_map/ppermute | solution.py:1115
  675.9 47.1 %collective-permute-start.30 = (bf16[512,768]{1,0:T(8,128)(2,1)}, bf16[512,768]{1,0:T(8,128)(2,1)S(1)}, u32[]{:S(2)}, u32[]{:S(2)}) collective-permute-start(bf16[512,768]{1,0:T(8,128)(2,1)} %get-tuple-element.76), channel_id=1, source_target_pairs={{2,0},{3,1},{0,2},{1,3},{10,4},{11,5},{8,6},{9,7},{6,8},{7,9},{4,1... | collective-permute-start | bytes 2359304 | tf_op jit(solution)/shard_map/ppermute | solution.py:1115
  692.7 30.3 %collective-permute-start.28 = (bf16[512,768]{1,0:T(8,128)(2,1)}, bf16[512,768]{1,0:T(8,128)(2,1)S(1)}, u32[]{:S(2)}, u32[]{:S(2)}) collective-permute-start(bf16[512,768]{1,0:T(8,128)(2,1)} %get-tuple-element.75), channel_id=1, source_target_pairs={{0,0},{1,1},{2,2},{3,3},{8,4},{9,5},{10,6},{11,7},{4,8},{5,9},{6,1... | collective-permute-start | bytes 2359304 | tf_op jit(solution)/shard_map/ppermute | solution.py:1115
  (51 other events, 411.7 us)
Sparse Core Ops, SparseCore 0:
  16.2 137.6 all-gather.2
  443.4 187.9 reduce-scatter.1

commit v2 on v1

--- a/solution.py
+++ b/solution.py
@@ -621,7 +621,8 @@
 
 
 def attend_back_kernel(
-    meta, q_ref, kv_ref, tr_ref, o_ref, lse_ref, d0, d1, d2, d3, out_ref, do_ref, di_ref, dq_ref, acc_ref
+    meta, q_ref, kv_ref, tr_ref, o_ref, lse_ref, d0, d1, d2, d3, w_ref,
+    out_ref, x0, x1, x2, x3, do_ref, di_ref, dq_ref, acc_ref,
 ):
     pieces = (d0, d1, d2, d3)
     zero = jnp.zeros((128, 64), BF16)
@@ -681,17 +682,21 @@
         return carry
 
     lax.fori_loop(0, 16, finish, 0)
-
-
-def attend_back_call(meta, q, kv, tr, o, lse, pieces):
-    ins = [q, kv, tr, o, lse, *pieces]
+    for k, x_ref in enumerate((x0, x1, x2, x3)):
+        for kk in range(8):
+            at = pl.ds(pl.multiple_of(meta[k * 8 + kk] * 128, 128), 128)
+            x_ref[kk * 128 : (kk + 1) * 128, :] = nt(out_ref[at, :], w_ref[...]).astype(BF16)
+
+
+def attend_back_call(meta, q, kv, tr, o, lse, pieces, w2):
+    ins = [q, kv, tr, o, lse, *pieces, w2]
     return pl.pallas_call(
         attend_back_kernel,
         grid_spec=pltpu.PrefetchScalarGridSpec(
             num_scalar_prefetch=1,
             grid=(1,),
             in_specs=[whole(v.shape) for v in ins],
-            out_specs=whole((4096, 576)),
+            out_specs=[whole((4096, 576))] + [whole((1024, 768))] * 4,
             scratch_shapes=[
                 pltpu.VMEM((3, 4096, 128), BF16),
                 pltpu.VMEM((8, 4096), F32),
@@ -699,33 +704,12 @@
                 pltpu.VMEM((3, 4096, 128), F32),
             ],
         ),
-        out_shape=jax.ShapeDtypeStruct((4096, 576), BF16),
+        out_shape=[jax.ShapeDtypeStruct((4096, 576), BF16)]
+        + [jax.ShapeDtypeStruct((1024, 768), BF16)] * 4,
         compiler_params=params(dimension_semantics=("arbitrary",)),
         cost_estimate=cost(50e9, 15e6, 20e6),
         name="attend_back",
     )(meta, *ins)
-
-
-def dx_kernel(meta, d_ref, w_ref, out_ref, *, piece):
-    kk = pl.program_id(0)
-    at = pl.ds(pl.multiple_of(meta[piece * 8 + kk] * 128, 128), 128)
-    out_ref[...] = nt(d_ref[at, :], w_ref[...]).astype(BF16)
-
-
-def dx_call(meta, dqkv, w2, piece):
-    return pl.pallas_call(
-        functools.partial(dx_kernel, piece=piece),
-        grid_spec=pltpu.PrefetchScalarGridSpec(
-            num_scalar_prefetch=1,
-            grid=(8,),
-            in_specs=[whole(dqkv.shape), whole(w2.shape)],
-            out_specs=pl.BlockSpec((128, 768), lambda i, m: (i, 0)),
-        ),
-        out_shape=jax.ShapeDtypeStruct((1024, 768), BF16),
-        compiler_params=params(dimension_semantics=("arbitrary",)),
-        cost_estimate=cost(2 * 1024 * 768 * 576, 6e6),
-        name="dx%d" % piece,
-    )(meta, dqkv, w2)
 
 
 def win_kernel(n_ref, d_ref, g_ref, s_ref, acc_ref):
@@ -1058,19 +1042,19 @@
     )(meta, gt, og, ac, mid, n2, cq, ca, lse, kc, vc, frames, so, ci, co, vecs, *pieces)
 
 
-def first_back_kernel(a_ref, b_ref, gm_ref, tok_ref, vec_ref, out_ref, sums_ref):
+def first_back_kernel(a_ref, b_ref, c_ref, gm_ref, tok_ref, vec_ref, out_ref, sums_ref):
     @pl.when(pl.program_id(0) == 0)
     def _():
         sums_ref[...] = jnp.zeros_like(sums_ref)
 
-    e = a_ref[...].astype(F32) + b_ref[...].astype(F32)
+    e = a_ref[...].astype(F32) + b_ref[...].astype(F32) + c_ref[...].astype(F32)
     back, gain, shift = norm_back(tok_ref[...].astype(F32), e, vec_ref[0:1, :])
     sums_ref[0:1, :] += gain
     sums_ref[1:2, :] += shift
     out_ref[...] = (gm_ref[...] + back).astype(BF16)
 
 
-def first_back_call(a, b, gm, tok, vecs, part):
+def first_back_call(a, b, c, gm, tok, vecs, part):
     width = a.shape[1]
     base = part * 2
     row = pl.BlockSpec((256, width), lambda i: (i, 0))
@@ -1078,13 +1062,13 @@
     return pl.pallas_call(
         first_back_kernel,
         grid=(2,),
-        in_specs=[row, row, off, off, whole(vecs.shape)],
+        in_specs=[off, off, row, off, off, whole(vecs.shape)],
         out_specs=[row, whole((8, width))],
         out_shape=[jax.ShapeDtypeStruct((512, width), BF16), jax.ShapeDtypeStruct((8, width), F32)],
         compiler_params=params(dimension_semantics=("arbitrary",)),
         cost_estimate=cost(1e7, 6e6),
         name="first_back%d" % part,
-    )(a, b, gm, tok, vecs)
+    )(a, b, c, gm, tok, vecs)
 
 
 def device_pairs(dp_count, move, back=False):
@@ -1143,15 +1127,20 @@
 
     got = [option(0)] + [send(option(k), flip(k)) for k in (1, 2, 3)]
     tree = merge(merge(got[0], got[1], x), merge(got[2], got[3], x), c)
-    tree = merge(tree, send(tree, lambda y, c, z, x: (y, c, z ^ 2, x)), z >> 1)
-    tree = merge(tree, send(tree, lambda y, c, z, x: (y, c, z ^ 1, x)), z & 1)
     for bit in range((dp_count // 2).bit_length() - 1):
         tree = merge(
             tree, send(tree, lambda y, c, z, x, bit=bit: (y ^ (1 << bit), c, z, x)), (y >> bit) & 1
         )
+    both = jnp.concatenate([tokens, encoder_states], axis=1)
+    mine = [send(pick(both, p), home(p)) for p in range(2)]
+    tree, mine[0] = lax.optimization_barrier((tree, mine[0]))
+    across = [send(v, flip(1)) for v in mine]
+    near = [send(v, flip(2)) for v in mine]
+    tree = merge(tree, send(tree, lambda y, c, z, x: (y, c, z ^ 2, x)), z >> 1)
+    tree = merge(tree, send(tree, lambda y, c, z, x: (y, c, z ^ 1, x)), z & 1)
     y_count = dp_count // 2
     nw = shard.shape[0] // 3
-    tree = tree.reshape(y_count, 2, 2, 2, 2, 3 * nw + 8, 192).transpose(0, 3, 2, 1, 4, 5, 6)
+    tree = tree.reshape(2, 2, y_count, 2, 2, 3 * nw + 8, 192).transpose(2, 3, 1, 0, 4, 5, 6)
     tree = tree.reshape(dp_count * 8, 3 * nw + 8, 192)
     w2 = jnp.concatenate(
         [tree[:, t * nw : (t + 1) * nw].reshape(width, 192) for t in range(3)], axis=1
@@ -1166,13 +1155,6 @@
     own_cols = lambda v: lax.dynamic_slice_in_dim(v, hset * 192, 192, 1)
     zero_row = jnp.zeros((1, 192), F32)
     qkv_bias = jnp.concatenate([own_cols(vecs[6:7]), zero_row, own_cols(vecs[7:8])], axis=1)
-
-    both = jnp.concatenate([tokens, encoder_states], axis=1)
-    mine = [send(pick(both, p), home(p)) for p in range(2)]
-    across = [send(v, flip(1)) for v in mine]
-    near = [send(v, flip(2)) for v in mine]
-    far = [send(v, flip(2)) for v in across]
-    pieces = mine + across + near + far
 
     info = jnp.concatenate([block_map, branch_fork], axis=1)
     info = jnp.where((z >> 1) == c, info, send(info, flip(2)))
@@ -1191,7 +1173,11 @@
         + [up_weight[:, j * width : (j + 1) * width] for j in range(tiles)]
         + [self_out, cross_in[0], cross_in[1], cross_in[2], cross_out]
     )
+    dense, w2, *across = lax.optimization_barrier((dense, w2, *across))
     dense = lax.all_gather(dense, AXES, axis=0)
+    far = [send(v, flip(2)) for v in across]
+    out_grad, far[1] = lax.optimization_barrier((out_grad, far[1]))
+    pieces = mine + across + near + far
     nd = down_weight.shape[0]
 
     def gathered(i):
@@ -1205,8 +1191,7 @@
     co = gathered(tiles + 4)
 
     q, kv, tr, n1 = qkv_call(meta, pieces, w2, vecs, qkv_bias)
-    og_pair, _ = lax.optimization_barrier((out_grad, far[1]))
-    og = jnp.concatenate([send(pick(og_pair, p), home(p)) for p in range(2)])
+    og = jnp.concatenate([send(pick(out_grad, p), home(p)) for p in range(2)])
     tok = jnp.concatenate([v[:rows] for v in mine])
     all_frames = jnp.concatenate([v[rows:] for v in pieces])
 
@@ -1230,52 +1215,9 @@
         + [rows_of(sog), rows_of(cig[0]), rows_of(cig[1]), rows_of(cig[2]), rows_of(cog)],
         axis=1,
     )
+    packed, *d_home = lax.optimization_barrier((packed, *d_home))
     dense_grad = lax.psum_scatter(packed, AXES, scatter_dimension=0, tiled=True)[0].astype(F32)
 
-    dqkv = attend_back_call(meta, q, kv, tr, o, lse, d_home)
-    dx3 = dx_call(meta, dqkv, w2, 3)
-    near3 = send(dx3, flip(2))
-    dx1 = dx_call(meta, dqkv, w2, 1)
-    side = (dx1.astype(F32) + near3.astype(F32)).astype(BF16)
-    side = [send(side[p * rows : (p + 1) * rows], flip(1)) for p in range(2)]
-    dx2 = dx_call(meta, dqkv, w2, 2)
-    near2 = send(dx2, flip(2))
-    dx0 = dx_call(meta, dqkv, w2, 0)
-    own = (dx0.astype(F32) + near2.astype(F32)).astype(BF16)
-
-    wg, colsum = win_call(n1, dqkv)
-    wg = wg.reshape(y_count, 2, 4, 2, nw, 576)
-
-    def halve(v, move, bit, axis):
-        keep = lax.dynamic_index_in_dim(v, bit, axis, False)
-        give = lax.dynamic_index_in_dim(v, 1 - bit, axis, False)
-        return (keep.astype(F32) + send(give, move).astype(F32)).astype(BF16)
-
-    for bit in reversed(range((dp_count // 2).bit_length() - 1)):
-        half = wg.shape[0] // 2
-        wg = halve(
-            wg.reshape((2, half) + wg.shape[1:]),
-            lambda y, c, z, x, bit=bit: (y ^ (1 << bit), c, z, x), (y >> bit) & 1, 0,
-        )
-    wg = wg.reshape(2, 2, 2, 2, nw, 576)
-    wg = halve(wg, lambda y, c, z, x: (y, c, z ^ 1, x), z & 1, 2)
-    wg = halve(wg, lambda y, c, z, x: (y, c, z ^ 2, x), z >> 1, 1)
-    wg = wg.reshape(4, nw, 576)
-
-    def shard_for(k):
-        return lax.dynamic_index_in_dim(wg, hset ^ k, 0, False)
-
-    parts = jnp.stack([shard_for(0)] + [send(shard_for(k), flip(k)) for k in (1, 2, 3)])
-    cols = [lax.dynamic_index_in_dim(parts, hset ^ j, 0, False) for j in range(4)]
-    self_in_grad = jnp.stack(
-        [jnp.concatenate([v[:, 192 * t : 192 * t + 192] for v in cols], axis=1) for t in range(3)]
-    ).astype(F32)
-
-    grads, first_sums = [], None
-    for p in range(2):
-        tg, s = first_back_call(own[p * rows : (p + 1) * rows], side[p], gm, tok, vecs, p)
-        grads.append(send(tg, home(p), True))
-        first_sums = s if first_sums is None else first_sums + s
     results = [send(res[p * rows : (p + 1) * rows], home(p), True) for p in range(2)]
     eg4 = eg.reshape(4, 2 * frames, width)
     eg_near = send(eg4[2:4], flip(2)).astype(F32)
@@ -1284,6 +1226,51 @@
     eg_sum = eg_sum.astype(BF16)
     eg_back = [send(eg_sum[p * frames : (p + 1) * frames], home(p), True) for p in range(2)]
 
+    dqkv, dx0, dx1, dx2, dx3 = attend_back_call(meta, q, kv, tr, o, lse, d_home, w2)
+    dx3, results[0], results[1], eg_back[0], eg_back[1] = lax.optimization_barrier(
+        (dx3, *results, *eg_back)
+    )
+    near3 = send(dx3, flip(2))
+    side = (dx1.astype(F32) + near3.astype(F32)).astype(BF16)
+    side_parts = [side[p * rows : (p + 1) * rows] for p in range(2)]
+    side = [send(v, flip(1)) for v in side_parts]
+    near2 = send(dx2, flip(2))
+    n1, near3 = lax.optimization_barrier((n1, near3))
+
+    wg, colsum = win_call(n1, dqkv)
+    wg = wg.reshape(y_count, 2, 4, 2, nw, 576)
+
+    def halve(v, move, bit, axis):
+        keep = lax.dynamic_index_in_dim(v, bit, axis, False)
+        give = lax.dynamic_index_in_dim(v, 1 - bit, axis, False)
+        return (keep.astype(F32) + send(give, move).astype(F32)).astype(BF16)
+
+    for bit in reversed(range((dp_count // 2).bit_length() - 1)):
+        half = wg.shape[0] // 2
+        wg = halve(
+            wg.reshape((2, half) + wg.shape[1:]),
+            lambda y, c, z, x, bit=bit: (y ^ (1 << bit), c, z, x), (y >> bit) & 1, 0,
+        )
+    wg = wg.reshape(2, 2, 2, 2, nw, 576)
+    wg = halve(wg, lambda y, c, z, x: (y, c, z ^ 1, x), z & 1, 2)
+
+    first = [first_back_call(dx0, near2, side[p], gm, tok, vecs, p) for p in range(2)]
+    grads = [v[0] for v in first]
+    first_sums = first[0][1] + first[1][1]
+    wg, grads[0] = lax.optimization_barrier((wg, grads[0]))
+    grads = [send(v, home(p), True) for p, v in enumerate(grads)]
+    wg = halve(wg, lambda y, c, z, x: (y, c, z ^ 2, x), z >> 1, 1)
+    wg = wg.reshape(4, nw, 576)
+
+    def shard_for(k):
+        return lax.dynamic_index_in_dim(wg, hset ^ k, 0, False)
+
+    parts = jnp.stack([shard_for(0)] + [send(shard_for(k), flip(k)) for k in (1, 2, 3)])
+    cols = [lax.dynamic_index_in_dim(parts, hset ^ j, 0, False) for j in range(4)]
+    self_in_grad = jnp.stack(
+        [jnp.concatenate([v[:, 192 * t : 192 * t + 192] for v in cols], axis=1) for t in range(3)]
+    ).astype(F32)
+
     def returned(pair, dtype):
         pair = [v.astype(dtype) for v in pair]
         return jnp.stack([jnp.where(parity == 0, pair[0], pair[1]), jnp.where(parity == 0, pair[1], pair[0])])
@@ -1292,19 +1279,30 @@
         jnp.zeros((1, width), F32), v, (0, hset * 192)
     )
     ubg = ubg.reshape(tiles, 8, width)[:, 0]
+    def over_all(table):
+        for k in (1, 2):
+            table = table + send(table, flip(k))
+        table = table + send(table, lambda y, c, z, x: (y, c, z ^ 1, x))
+        table = table + send(table, lambda y, c, z, x: (y, c, z ^ 2, x))
+        for bit in range((dp_count // 2).bit_length() - 1):
+            table = table + send(table, lambda y, c, z, x, bit=bit: (y ^ (1 << bit), c, z, x))
+        return table
+
     table = jnp.concatenate(
         [
-            first_sums[0:1], sums[1:3], first_sums[1:2], sums[4:6],
-            own_bias(colsum[0:1, 0:192]), own_bias(colsum[0:1, 384:576]), sums[8:12],
-            dbg[0:1], ubg, jnp.zeros((24 - 13 - tiles, width), F32),
+            sums[1:3], sums[4:6], sums[8:12],
+            own_bias(colsum[0:1, 0:192]), own_bias(colsum[0:1, 384:576]),
+            dbg[0:1], ubg, jnp.zeros((16 - 11 - tiles, width), F32),
         ]
     )
-    for k in (1, 2):
-        table = table + send(table, flip(k))
-    table = table + send(table, lambda y, c, z, x: (y, c, z ^ 1, x))
-    table = table + send(table, lambda y, c, z, x: (y, c, z ^ 2, x))
-    for bit in range((dp_count // 2).bit_length() - 1):
-        table = table + send(table, lambda y, c, z, x, bit=bit: (y ^ (1 << bit), c, z, x))
+    table = over_all(table)
+    first_table = over_all(first_sums)
+    table = jnp.concatenate(
+        [
+            first_table[0:1], table[0:2], first_table[1:2], table[2:4],
+            table[8:10], table[4:8], table[10 : 11 + tiles],
+        ]
+    )
     mine_of = lambda v: lax.dynamic_slice_in_dim(v, flat * nw, nw, 1)
     vec_grad = mine_of(table[:13])
     up_bias_grad = lax.dynamic_slice_in_dim(

time: 752 us -> 667 us (0.89)
  waiting for transfers between devices: 189 us -> 142 us
  Pallas kernels: 351 us -> 334 us
  local copies, waits for them, and re-layouts: 77.8 us -> 66.8 us
    ppermute x46 -> x51, waiting for transfers between devices: 189 us -> 142 us  [send(): return lax.ppermute(v, AXES, device_pairs(dp_count, move, back))]
    pallas_call x6 -> x2, Pallas kernels: 41 us -> 8.33 us  [first_back_call(): pl.pallas_call(first_back_kernel, grid=(2,), in_specs=[off, off, row, off...]
    pallas_call x1, Pallas kernels: 87.7 us -> 101 us  [attend_back_call(): pl.pallas_call(attend_back_kernel, grid_spec=pltpu.PrefetchScalarGridSpec...]
    unnamed x82 -> x80, local copies, waits for them, and re-layouts: 34.6 us -> 26.9 us
    ppermute x46 -> x51, starting transfers between devices: 80.4 us -> 76.3 us  [send(): return lax.ppermute(v, AXES, device_pairs(dp_count, move, back))]
  transfers between devices with their start and end apart: 48 -> 53, of which waited for: 17 -> 20; matrix products, arithmetic and copies ran while one was open for 9% -> 11% of each run, Pallas kernels for 32% -> 34%
where the time goes in v2:
time: 667 us; the launch traced here: 657 us
  Pallas kernels  334 us (50%)
  waiting for transfers between devices  142 us (21%)
  starting transfers between devices  76.4 us (11%)
  local copies, waits for them, and re-layouts  66.8 us (10%)
  other arithmetic  22.9 us (3%)
  between operations  15.3 us (2%)
    ppermute x51, waiting for transfers between devices, send(): return lax.ppermute(v, AXES, device_pairs(dp_count, move, back))  142 us
    pallas_call x1, Pallas kernels, attend_back_call(): pl.pallas_call(attend_back_kernel, grid_spec=pltpu.PrefetchScalarGridSpec...  101 us
    pallas_call x1, Pallas kernels, attend_call(): pl.pallas_call(attend_kernel, grid_spec=pltpu.PrefetchScalarGridSpec(num_...  86 us
    ppermute x51, starting transfers between devices, send(): return lax.ppermute(v, AXES, device_pairs(dp_count, move, back))  76.3 us
    pallas_call x1, Pallas kernels, feed_call(): pl.pallas_call(feed_kernel, grid=(tiles,), in_specs=[whole(n3.shape), who...  43.4 us
    pallas_call x1, Pallas kernels, mid_back_call(): pl.pallas_call(mid_back_kernel, grid_spec=pltpu.PrefetchScalarGridSpec(nu...  40.8 us
    pallas_call x1, Pallas kernels, mid_call(): pl.pallas_call(mid_kernel, grid_spec=pltpu.PrefetchScalarGridSpec(num_sca...  27.8 us
    unnamed x80, local copies, waits for them, and re-layouts  26.9 us
  transfers between devices with their start and end apart: 53, of which 20 were waited for; matrix products, arithmetic and copies ran while one was open for 11% of the time, Pallas kernels for 34%

profile of v2, /device:TPU:20, one launch (start us, length us, event | category | flops | bytes accessed | tf_op | source)
XLA Modules:
  0.0 656.8 jit_solution(5285738725646500752)
XLA Ops:
  17.0 5.5 collective-permute-start.5
  23.4 4.8 collective-permute-done.4
  28.3 25.6 %collective-permute-done.5.refs_0_ = bf16[544,768]{1,0:T(8,128)(2,1)} collective-permute-done((bf16[544,768]{1,0:T(8,128)(2,1)S(1)}, bf16[544,768]{1,0:T(8,128)(2,1)}, u32[]{:S(2)}, u32[]{:S(2)}) %collective-permute-start.5) | collective-permute-done | bytes 835616 | tf_op jit(solution)/shard_map/ppermute | solution.py:1099
  54.0 13.6 %collective-permute-done.7 = bf16[2,2,2,80,192]{4,3,2,1,0:T(8,128)(2,1)S(1)} collective-permute-done((bf16[2,2,2,80,192]{4,3,2,1,0:T(8,128)(2,1)S(1)}, bf16[2,2,2,80,192]{4,3,2,1,0:T(8,128)(2,1)S(1)}, u32[]{:S(2)}, u32[]{:S(2)}) %collective-permute-start.7) | collective-permute-done | bytes 245792 | tf_op jit(solution)/shard_map/ppermute | solution.py:1099
  67.7 4.3 collective-permute-start.8
  74.1 11.9 %collective-permute-done.8 = bf16[2,2,2,2,80,192]{5,4,3,0,2,1:T(8,128)(2,1)S(1)} collective-permute-done((bf16[2,2,2,2,80,192]{5,4,3,0,2,1:T(8,128)(2,1)S(1)}, bf16[2,2,2,2,80,192]{5,4,3,0,2,1:T(8,128)(2,1)S(1)}, u32[]{:S(2)}, u32[]{:S(2)}) %collective-permute-start.8) | collective-permute-done | bytes 491552 | tf_op jit(solution)/shard_map/ppermute | solution.py:1099
  87.9 20.9 %collective-permute-done.10.refs_3_ = bf16[544,768]{1,0:T(8,128)(2,1)} collective-permute-done((bf16[544,768]{1,0:T(8,128)(2,1)}, bf16[544,768]{1,0:T(8,128)(2,1)}, u32[]{:S(2)}, u32[]{:S(2)}) %collective-permute-start.10) | collective-permute-done | bytes 835616 | tf_op jit(solution)/shard_map/ppermute | solution.py:1099
  130.4 17.5 %qkv.1 = (bf16[3,4096,128]{2,1,0:T(8,128)(2,1)}, bf16[3,4096,128]{2,1,0:T(8,128)(2,1)}, bf16[6,64,4096]{2,1,0:T(8,128)(2,1)}, bf16[4096,768]{1,0:T(8,128)(2,1)}) custom-call(s32[128]{0:T(128)} %pad_add_fusion.1.meta, bf16[544,768]{1,0:T(8,128)(2,1)} %collective-permute-done.5.refs_0_, bf16[544,768]{1,0:T(8,128)(2,1)} %collective-permute-done.6.refs_1_, ...), custom_call_target="tpu_custom_call" | custom-call | flops 3623878656 | bytes 20000000 | tf_op jit(solution)/shard_map/qkv/pallas_call | solution.py:517
  147.9 86.0 %attend.1 = (bf16[32,128,192]{2,1,0:T(8,128)(2,1)}, f32[8,4096]{1,0:T(8,128)}) custom-call(s32[128]{0:T(128)} %pad_add_fusion.1.meta, bf16[3,4096,128]{2,1,0:T(8,128)(2,1)} %get-tuple-element.84.q_ref, bf16[3,4096,128]{2,1,0:T(8,128)(2,1)} %get-tuple-element.85.kv_ref, bf16[6,64,4096]{2,1,0:T(8,128)(2,1)} %get-tuple-element.86.tr_ref), custom_call_target="tpu_custom_call" | custom-call | flops 20000000000 | bytes 10000000 | tf_op jit(solution)/shard_map/attend/pallas_call | solution.py:600
  242.4 4.8 slice.589
  247.2 5.9 fusion.19
  257.5 4.9 collective-permute-done.15.o1
  262.4 27.8 %middle.1 = (f32[1024,768]{1,0:T(8,128)}, f32[1024,768]{1,0:T(8,128)}, bf16[1024,768]{1,0:T(8,128)(2,1)}, bf16[1024,768]{1,0:T(8,128)(2,1)}, bf16[1024,768]{1,0:...) custom-call(s32[128]{0:T(128)} %pad_add_fusion.1.meta, ...), custom_call_target="tpu_custom_call" | custom-call | flops 8000000000 | bytes 25000000 | tf_op jit(solution)/shard_map/middle/pallas_call | solution.py:821
  290.2 43.4 %feed.1 = (bf16[1024,768]{1,0:T(8,128)(2,1)}, f32[1024,768]{1,0:T(8,128)}, bf16[4,768,768]{2,1,0:T(8,128)(2,1)}, bf16[4,768,768]{2,1,0:T(8,128)(2,1)}, f32[32,768]{1,0:T(8,128)}, /*index=5*/f32[8,768]{1,0:T(8,128)}) custom-call(bf16[1024,768]{1,0:T(8,128)(2,1)} %get-tuple-element.90.n3_ref, bf16[1024,768]{1,0:T(8,128)(2,1)} %constant_dynamic-update-slice_fusion.20.og_ref, ...), custom_call_target="tpu_custom_call" | custom-call | flops 28991029248 | bytes 35000000 | tf_op jit(solution)/shard_map/feed/pallas_call | solution.py:901
  333.6 40.8 %middle_back.1 = (f32[1024,768]{1,0:T(8,128)}, bf16[1024,192]{1,0:T(8,128)(2,1)}, bf16[1024,192]{1,0:T(8,128)(2,1)}, bf16[1024,192]{1,0:T(8,128)(2,1)}, bf16[102...) custom-call(s32[128]{0:T(128)} %pad_add_fusion.1.meta, ...), custom_call_target="tpu_custom_call" | custom-call | flops 22000001024 | bytes 35000000 | tf_op jit(solution)/shard_map/middle_back/pallas_call | solution.py:1021
  403.6 6.0 collective-permute-start.24
  417.4 100.9 %attend_back.1 = (bf16[4096,576]{1,0:T(8,128)(2,1)}, bf16[1024,768]{1,0:T(8,128)(2,1)}, bf16[1024,768]{1,0:T(8,128)(2,1)}, bf16[1024,768]{1,0:T(8,128)(2,1)}, bf16[1024,768]{1,0:T(8,128)(2,1)}) custom-call(s32[128]{0:T(128)} %pad_add_fusion.1.meta, bf16[3,4096,128]{2,1,0:T(8,128)(2,1)} %get-tuple-element.84.q_ref, ...), custom_call_target="tpu_custom_call" | custom-call | flops 49999998976 | bytes 15000000 | tf_op jit(solution)/shard_map/attend_back/pallas_call | solution.py:693
  523.6 9.1 %win.1 = (bf16[768,576]{1,0:T(8,128)(2,1)}, f32[8,576]{1,0:T(8,128)}) custom-call(bf16[4096,768]{1,0:T(8,128)(2,1)} %get-tuple-element.121.n_ref, bf16[4096,576]{1,0:T(8,128)(2,1)} %get-tuple-element.122.d_ref), custom_call_target="tpu_custom_call" | custom-call | flops 3623878656 | bytes 12000000 | tf_op jit(solution)/shard_map/win/pallas_call | solution.py:733
  543.0 5.2 collective-permute-done.44
  548.2 8.1 %collective-permute-start.45 = (f32[16,768]{1,0:T(8,128)S(1)}, f32[16,768]{1,0:T(8,128)S(1)}, u32[]{:S(2)}, u32[]{:S(2)}) collective-permute-start(f32[16,768]{1,0:T(8,128)S(1)} %add.170), channel_id=1, source_target_pairs={{0,4},{1,5},{2,6},{3,7},{4,0},{5,1},{6,2},{7,3},{8,12},{9,13},{10,... | collective-permute-start | bytes 147464 | tf_op jit(solution)/shard_map/ppermute | solution.py:1099
  569.0 11.9 %collective-permute-done.33.c_ref = bf16[512,768]{1,0:T(8,128)(2,1)} collective-permute-done((bf16[512,768]{1,0:T(8,128)(2,1)}, bf16[512,768]{1,0:T(8,128)(2,1)}, u32[]{:S(2)}, u32[]{:S(2)}) %collective-permute-start.33) | collective-permute-done | bytes 786464 | tf_op jit(solution)/shard_map/ppermute | solution.py:1099
  591.0 9.0 %collective-permute-start.47 = (bf16[2,2,24,576]{3,2,1,0:T(8,128)(2,1)S(1)}, bf16[2,2,24,576]{3,2,1,0:T(8,128)(2,1)S(1)}, u32[]{:S(2)}, u32[]{:S(2)}) collective-permute-start(bf16[2,2,24,576]{3,2,1,0:T(8,128)(2,1)S(1)} %dynamic-slice_bitcast_fusion.2), channel_id=1, source_target_pairs={{0,4},{1,5},{2,6},{3,7},{4,0},{5,1},{6,2},{7,3},{8,12},{9,13},{10,... | collective-permute-start | bytes 331784 | tf_op jit(solution)/shard_map/ppermute | solution.py:1099
  616.8 15.9 %collective-permute-done.34 = bf16[512,768]{1,0:T(8,128)(2,1)S(1)} collective-permute-done((bf16[512,768]{1,0:T(8,128)(2,1)}, bf16[512,768]{1,0:T(8,128)(2,1)S(1)}, u32[]{:S(2)}, u32[]{:S(2)}) %collective-permute-start.34) | collective-permute-done | bytes 786464 | tf_op jit(solution)/shard_map/ppermute | solution.py:1099
  632.7 10.1 %collective-permute-done.36 = bf16[512,768]{1,0:T(8,128)(2,1)S(1)} collective-permute-done((bf16[512,768]{1,0:T(8,128)(2,1)S(1)}, bf16[512,768]{1,0:T(8,128)(2,1)S(1)}, u32[]{:S(2)}, u32[]{:S(2)}) %collective-permute-start.36) | collective-permute-done | bytes 786464 | tf_op jit(solution)/shard_map/ppermute | solution.py:1099
  (319 shorter events, 147.8 us)
Async XLA Ops:
  7.2 235.3 %all-gather.3.cloned.1.call-start = ((), (), s32[]{:S(2)}) async-start(), calls=%async_computation.2 | async-start | bytes 15814656 | tf_op jit(solution)/shard_map/all_gather | solution.py:1177
  16.9 56.7 %collective-permute-start.6 = (bf16[544,768]{1,0:T(8,128)(2,1)S(1)}, bf16[544,768]{1,0:T(8,128)(2,1)}, u32[]{:S(2)}, u32[]{:S(2)}) collective-permute-start(bf16[544,768]{1,0:T(8,128)(2,1)S(1)} %get-tuple-element.161), channel_id=1, source_target_pairs={{0,2},{1,3},{2,0},{3,1},{4,10},{5,11},{6,8},{7,9},{8,6},{9,7},{10,... | collective-permute-start | bytes 2506760 | tf_op jit(solution)/shard_map/ppermute | solution.py:1099
  17.0 36.9 %collective-permute-start.5 = (bf16[544,768]{1,0:T(8,128)(2,1)S(1)}, bf16[544,768]{1,0:T(8,128)(2,1)}, u32[]{:S(2)}, u32[]{:S(2)}) collective-permute-start(bf16[544,768]{1,0:T(8,128)(2,1)S(1)} %get-tuple-element.162), channel_id=1, source_target_pairs={{0,0},{1,1},{2,2},{3,3},{4,8},{5,9},{6,10},{7,11},{8,4},{9,5},{10,... | collective-permute-start | bytes 2506760 | tf_op jit(solution)/shard_map/ppermute | solution.py:1099
  72.0 36.7 %collective-permute-start.9 = (bf16[544,768]{1,0:T(8,128)(2,1)}, bf16[544,768]{1,0:T(8,128)(2,1)}, u32[]{:S(2)}, u32[]{:S(2)}) collective-permute-start(bf16[544,768]{1,0:T(8,128)(2,1)} %collective-permute-done.5.refs_0_), channel_id=1, source_target_pairs={{0,1},{1,0},{2,3},{3,2},{4,5},{5,4},{6,7},{7,6},{8,9},{9,8},{10,11... | collective-permute-start | bytes 2506760 | tf_op jit(solution)/shard_map/ppermute | solution.py:1099
  73.6 35.2 %collective-permute-start.10 = (bf16[544,768]{1,0:T(8,128)(2,1)}, bf16[544,768]{1,0:T(8,128)(2,1)}, u32[]{:S(2)}, u32[]{:S(2)}) collective-permute-start(bf16[544,768]{1,0:T(8,128)(2,1)} %collective-permute-done.6.refs_1_), channel_id=1, source_target_pairs={{0,1},{1,0},{2,3},{3,2},{4,5},{5,4},{6,7},{7,6},{8,9},{9,8},{10,11... | collective-permute-start | bytes 2506760 | tf_op jit(solution)/shard_map/ppermute | solution.py:1099
  108.8 536.1 %reduce-scatter.2.cloned.1.call-start = ((), (), s32[]{:S(2)}) async-start(), calls=%async_computation.1 | async-start | bytes 15814656 | tf_op jit(solution)/shard_map/reduce_scatter | solution.py:1219
  124.9 116.5 %collective-permute-start.19 = (bf16[512,768]{1,0:T(8,128)(2,1)S(1)}, bf16[512,768]{1,0:T(8,128)(2,1)S(1)}, u32[]{:S(2)}, u32[]{:S(2)}) collective-permute-start(bf16[512,768]{1,0:T(8,128)(2,1)S(1)} %get-tuple-element.171), channel_id=1, source_target_pairs={{0,2},{1,3},{2,0},{3,1},{4,10},{5,11},{6,8},{7,9},{8,6},{9,7},{10,... | collective-permute-start | bytes 2359304 | tf_op jit(solution)/shard_map/ppermute | solution.py:1099
  127.3 113.1 %collective-permute-start.18 = (bf16[512,768]{1,0:T(8,128)(2,1)S(1)}, bf16[512,768]{1,0:T(8,128)(2,1)S(1)}, u32[]{:S(2)}, u32[]{:S(2)}) collective-permute-start(bf16[512,768]{1,0:T(8,128)(2,1)S(1)} %get-tuple-element.172), channel_id=1, source_target_pairs={{0,0},{1,1},{2,2},{3,3},{4,8},{5,9},{6,10},{7,11},{8,4},{9,5},{10,... | collective-permute-start | bytes 2359304 | tf_op jit(solution)/shard_map/ppermute | solution.py:1099
  236.6 20.9 %collective-permute-start.16 = (bf16[1024,192]{1,0:T(8,128)(2,1)}, bf16[1024,192]{1,0:T(8,128)(2,1)}, u32[]{:S(2)}, u32[]{:S(2)}) collective-permute-start(bf16[1024,192]{1,0:T(8,128)(2,1)} %bitcast.36), channel_id=1, source_target_pairs={{0,8},{1,9},{2,10},{3,11},{4,12},{5,13},{6,14},{7,15},{8,0},{9,1},... | collective-permute-start | bytes 1179656 | tf_op jit(solution)/shard_map/ppermute | solution.py:1099
  236.6 20.9 %collective-permute-start.17 = (bf16[1024,192]{1,0:T(8,128)(2,1)}, bf16[1024,192]{1,0:T(8,128)(2,1)}, u32[]{:S(2)}, u32[]{:S(2)}) collective-permute-start(bf16[1024,192]{1,0:T(8,128)(2,1)} %bitcast.37), channel_id=1, source_target_pairs={{0,9},{1,8},{2,11},{3,10},{4,13},{5,12},{6,15},{7,14},{8,1},{9,0},... | collective-permute-start | bytes 1179656 | tf_op jit(solution)/shard_map/ppermute | solution.py:1099
  238.2 24.2 %collective-permute-start.15 = (bf16[1024,192]{1,0:T(8,128)(2,1)S(1)}, bf16[1024,192]{1,0:T(8,128)(2,1)}, u32[]{:S(2)}, u32[]{:S(2)}) collective-permute-start(bf16[1024,192]{1,0:T(8,128)(2,1)S(1)} %bitcast.220), channel_id=1, source_target_pairs={{0,1},{1,0},{2,3},{3,2},{4,5},{5,4},{6,7},{7,6},{8,9},{9,8},{10,11... | collective-permute-start | bytes 1179656 | tf_op jit(solution)/shard_map/ppermute | solution.py:1099
  374.3 21.2 %collective-permute-start.20 = (bf16[1024,192]{1,0:T(8,128)(2,1)}, bf16[1024,192]{1,0:T(8,128)(2,1)S(1)}, u32[]{:S(2)}, u32[]{:S(2)}) collective-permute-start(bf16[1024,192]{1,0:T(8,128)(2,1)} %get-tuple-element.107), channel_id=1, source_target_pairs={{0,1},{1,0},{2,3},{3,2},{4,5},{5,4},{6,7},{7,6},{8,9},{9,8},{10,11... | collective-permute-start | bytes 1179656 | tf_op jit(solution)/shard_map/ppermute | solution.py:1099
  375.9 22.3 %collective-permute-start.22 = (bf16[1024,192]{1,0:T(8,128)(2,1)}, bf16[1024,192]{1,0:T(8,128)(2,1)S(1)}, u32[]{:S(2)}, u32[]{:S(2)}) collective-permute-start(bf16[1024,192]{1,0:T(8,128)(2,1)} %get-tuple-element.109), channel_id=1, source_target_pairs={{0,9},{1,8},{2,11},{3,10},{4,13},{5,12},{6,15},{7,14},{8,1},{9,0},... | collective-permute-start | bytes 1179656 | tf_op jit(solution)/shard_map/ppermute | solution.py:1099
  403.6 114.6 %collective-permute-start.24 = (bf16[512,768]{1,0:T(8,128)(2,1)S(1)}, bf16[512,768]{1,0:T(8,128)(2,1)S(1)}, u32[]{:S(2)}, u32[]{:S(2)}) collective-permute-start(bf16[512,768]{1,0:T(8,128)(2,1)S(1)} %get-tuple-element.169), channel_id=1, source_target_pairs={{2,0},{3,1},{0,2},{1,3},{10,4},{11,5},{8,6},{9,7},{6,8},{7,9},{4,1... | collective-permute-start | bytes 2359304 | tf_op jit(solution)/shard_map/ppermute | solution.py:1099
  409.6 108.6 %collective-permute-start.23 = (bf16[512,768]{1,0:T(8,128)(2,1)S(1)}, bf16[512,768]{1,0:T(8,128)(2,1)}, u32[]{:S(2)}, u32[]{:S(2)}) collective-permute-start(bf16[512,768]{1,0:T(8,128)(2,1)S(1)} %get-tuple-element.170), channel_id=1, source_target_pairs={{0,0},{1,1},{2,2},{3,3},{8,4},{9,5},{10,6},{11,7},{4,8},{5,9},{6,1... | collective-permute-start | bytes 2359304 | tf_op jit(solution)/shard_map/ppermute | solution.py:1099
  411.6 106.6 %collective-permute-start.28 = (bf16[32,768]{1,0:T(8,128)(2,1)S(1)}, bf16[32,768]{1,0:T(8,128)(2,1)S(1)}, u32[]{:S(2)}, u32[]{:S(2)}) collective-permute-start(bf16[32,768]{1,0:T(8,128)(2,1)S(1)} %get-tuple-element.212), channel_id=1, source_target_pairs={{2,0},{3,1},{0,2},{1,3},{10,4},{11,5},{8,6},{9,7},{6,8},{7,9},{4,1... | collective-permute-start | bytes 147464 | tf_op jit(solution)/shard_map/ppermute | solution.py:1099
  413.4 104.8 %collective-permute-start.27 = (bf16[32,768]{1,0:T(8,128)(2,1)S(1)}, bf16[32,768]{1,0:T(8,128)(2,1)S(1)}, u32[]{:S(2)}, u32[]{:S(2)}) collective-permute-start(bf16[32,768]{1,0:T(8,128)(2,1)S(1)} %get-tuple-element.213), channel_id=1, source_target_pairs={{0,0},{1,1},{2,2},{3,3},{8,4},{9,5},{10,6},{11,7},{4,8},{5,9},{6,1... | collective-permute-start | bytes 147464 | tf_op jit(solution)/shard_map/ppermute | solution.py:1099
  521.6 42.1 %collective-permute-start.32 = (bf16[1024,768]{1,0:T(8,128)(2,1)}, bf16[1024,768]{1,0:T(8,128)(2,1)S(1)}, u32[]{:S(2)}, u32[]{:S(2)}) collective-permute-start(bf16[1024,768]{1,0:T(8,128)(2,1)} %get-tuple-element.125), channel_id=1, source_target_pairs={{0,8},{1,9},{2,10},{3,11},{4,12},{5,13},{6,14},{7,15},{8,0},{9,1},... | collective-permute-start | bytes 4718600 | tf_op jit(solution)/shard_map/ppermute | solution.py:1099
  538.7 24.7 %collective-permute-start.30 = (bf16[1,2,4,2,24,576]{5,4,3,2,1,0:T(8,128)(2,1)S(1)}, bf16[1,2,4,2,24,576]{5,4,3,2,1,0:T(8,128)(2,1)S(1)}, u32[]{:S(2)}, u32[]{:S(2)}) collective-permute-start(bf16[1,2,4,2,24,576]{5,4,3,2,1,0:T(8,128)(2,1)S(1)} %dynamic-slice_bitcast_fusion), channel_id=1, source_target_pairs={{0,16},{1,17},{2,18},{3,19},{4,20},{5,21},{6,22},{7,23},{8,24},{9,... | collective-permute-start | bytes 1327112 | tf_op jit(solution)/shard_map/ppermute | solution.py:1099
  540.9 22.9 %collective-permute-start.35 = (bf16[512,768]{1,0:T(8,128)(2,1)S(1)}, bf16[512,768]{1,0:T(8,128)(2,1)}, u32[]{:S(2)}, u32[]{:S(2)}) collective-permute-start(bf16[512,768]{1,0:T(8,128)(2,1)S(1)} %get-tuple-element.165), channel_id=1, source_target_pairs={{0,1},{1,0},{2,3},{3,2},{4,5},{5,4},{6,7},{7,6},{8,9},{9,8},{10,11... | collective-permute-start | bytes 2359304 | tf_op jit(solution)/shard_map/ppermute | solution.py:1099
  542.5 38.4 %collective-permute-start.33 = (bf16[512,768]{1,0:T(8,128)(2,1)}, bf16[512,768]{1,0:T(8,128)(2,1)}, u32[]{:S(2)}, u32[]{:S(2)}) collective-permute-start(bf16[512,768]{1,0:T(8,128)(2,1)} %get-tuple-element.166), channel_id=1, source_target_pairs={{0,1},{1,0},{2,3},{3,2},{4,5},{5,4},{6,7},{7,6},{8,9},{9,8},{10,11... | collective-permute-start | bytes 2359304 | tf_op jit(solution)/shard_map/ppermute | solution.py:1099
  563.7 26.1 %collective-permute-start.31 = (bf16[2,2,2,24,576]{4,3,2,1,0:T(8,128)(2,1)S(1)}, bf16[2,2,2,24,576]{4,3,2,1,0:T(8,128)(2,1)S(1)}, u32[]{:S(2)}, u32[]{:S(2)}) collective-permute-start(bf16[2,2,2,24,576]{4,3,2,1,0:T(8,128)(2,1)S(1)} %dynamic-slice_bitcast_fusion.1), channel_id=1, source_target_pairs={{0,2},{1,3},{2,0},{3,1},{4,6},{5,7},{6,4},{7,5},{8,10},{9,11},{10,... | collective-permute-start | bytes 663560 | tf_op jit(solution)/shard_map/ppermute | solution.py:1099
  604.3 28.4 %collective-permute-start.34 = (bf16[512,768]{1,0:T(8,128)(2,1)}, bf16[512,768]{1,0:T(8,128)(2,1)S(1)}, u32[]{:S(2)}, u32[]{:S(2)}) collective-permute-start(bf16[512,768]{1,0:T(8,128)(2,1)} %get-tuple-element.129), channel_id=1, source_target_pairs={{0,0},{1,1},{2,2},{3,3},{8,4},{9,5},{10,6},{11,7},{4,8},{5,9},{6,1... | collective-permute-start | bytes 2359304 | tf_op jit(solution)/shard_map/ppermute | solution.py:1099
  606.2 36.6 %collective-permute-start.36 = (bf16[512,768]{1,0:T(8,128)(2,1)S(1)}, bf16[512,768]{1,0:T(8,128)(2,1)S(1)}, u32[]{:S(2)}, u32[]{:S(2)}) collective-permute-start(bf16[512,768]{1,0:T(8,128)(2,1)S(1)} %copy-done.20), channel_id=1, source_target_pairs={{2,0},{3,1},{0,2},{1,3},{10,4},{11,5},{8,6},{9,7},{6,8},{7,9},{4,1... | collective-permute-start | bytes 2359304 | tf_op jit(solution)/shard_map/ppermute | solution.py:1099
  (55 other events, 506.8 us)
Sparse Core Ops, SparseCore 0:
  108.9 125.6 all-gather.2
  399.2 179.5 reduce-scatter.1

commit v3 on v2

--- a/solution.py
+++ b/solution.py
@@ -540,49 +540,67 @@
     )(meta, *pieces, w2, vecs, bias)
 
 
-def tile_mask(diag, kt, limit):
-    key = lax.broadcasted_iota(jnp.int32, (256, 256), 0)
-    if diag:
-        return key <= lax.broadcasted_iota(jnp.int32, (256, 256), 1)
-    return key + kt * 256 < limit
+def tile_plan(meta, qi):
+    branch = qi >= 8
+    fork = meta[64 + jnp.maximum(qi - 8, 0)]
+    count = jnp.where(branch, (fork + 255) // 256, qi) + 1
+    reach = jnp.where(branch, fork, 4096)
+
+    def tile(t, own):
+        if own:
+            kt = qi
+        else:
+            kt = jnp.where(t == count - 1, qi, t)
+        key = lax.broadcasted_iota(jnp.int32, (256, 256), 0)
+        query = lax.broadcasted_iota(jnp.int32, (256, 256), 1)
+        if own:
+            mask = key <= query
+        else:
+            limit = jnp.where(t == count - 1, 0, jnp.minimum(reach - t * 256, 256) - 1)
+            slope = jnp.where(t == count - 1, 1, 0)
+            mask = key <= query[0:1, :] * slope + limit
+        return pl.ds(pl.multiple_of(kt * 256, 256), 256), mask
+
+    return count, tile
+
+
+def tile_pairs(count, step):
+    def pair(i, carry):
+        step(i * 2, False)
+        step(i * 2 + 1, False)
+        return carry
+
+    lax.fori_loop(0, count // 2, pair, 0)
+
+    @pl.when(count % 2 == 1)
+    def _():
+        step(count - 1, True)
 
 
 def attend_kernel(meta, q_ref, kv_ref, tr_ref, o_ref, lse_ref, m_ref, l_ref, acc_ref):
     def q_tile(qi, carry):
-        branch = qi >= 8
-        fork = meta[64 + jnp.maximum(qi - 8, 0)]
-        full = jnp.where(branch, fork // 256, qi)
+        count, tile = tile_plan(meta, qi)
         qs = pl.ds(pl.multiple_of(qi * 256, 256), 256)
         m_ref[...] = jnp.full_like(m_ref, -1e30)
         l_ref[...] = jnp.zeros_like(l_ref)
         acc_ref[...] = jnp.zeros_like(acc_ref)
 
-        def k_tile(kt, mask):
-            ks = pl.ds(pl.multiple_of(kt * 256, 256), 256)
+        def k_tile(t, own):
+            ks, mask = tile(t, own)
+            s = [nt(kv_ref[h, ks, :], q_ref[h, qs, :]) for h in range(3)]
+            s = [jnp.where(mask, v, -1e30) for v in s]
+            old = [m_ref[h : h + 1, :] for h in range(3)]
+            new = [jnp.maximum(old[h], jnp.max(s[h], axis=0, keepdims=True)) for h in range(3)]
+            p = [jnp.exp2(s[h] - new[h]) for h in range(3)]
+            out = [nn(tr_ref[3 + h, :, ks], p[h].astype(BF16)) for h in range(3)]
             for h in range(3):
-                s = nt(kv_ref[h, ks, :], q_ref[h, qs, :])
-                if mask is not None:
-                    s = jnp.where(mask, s, -1e30)
-                old = m_ref[h : h + 1, :]
-                new = jnp.maximum(old, jnp.max(s, axis=0, keepdims=True))
-                p = jnp.exp2(s - new)
-                alpha = jnp.exp2(old - new)
-                m_ref[h : h + 1, :] = new
-                l_ref[h : h + 1, :] = l_ref[h : h + 1, :] * alpha + jnp.sum(p, axis=0, keepdims=True)
+                alpha = jnp.exp2(old[h] - new[h])
+                m_ref[h : h + 1, :] = new[h]
+                l_ref[h : h + 1, :] = l_ref[h : h + 1, :] * alpha + jnp.sum(p[h], axis=0, keepdims=True)
                 hs = slice(h * 64, h * 64 + 64)
-                acc_ref[hs, :] = acc_ref[hs, :] * alpha + nn(tr_ref[3 + h, :, ks], p.astype(BF16))
-
-        def full_tile(kt, c):
-            k_tile(kt, None)
-            return c
-
-        lax.fori_loop(0, full, full_tile, 0)
-
-        @pl.when(branch & (fork % 256 != 0))
-        def _():
-            k_tile(full, tile_mask(False, full, fork))
-
-        k_tile(qi, tile_mask(True, 0, 0))
+                acc_ref[hs, :] = acc_ref[hs, :] * alpha + out[h]
+
+        tile_pairs(count, k_tile)
         for h in range(3):
             hs = slice(h * 64, h * 64 + 64)
             l = l_ref[h : h + 1, :]
@@ -622,52 +640,54 @@
 
 def attend_back_kernel(
     meta, q_ref, kv_ref, tr_ref, o_ref, lse_ref, d0, d1, d2, d3, w_ref,
-    out_ref, x0, x1, x2, x3, do_ref, di_ref, dq_ref, acc_ref,
+    out_ref, x0, x1, x2, x3, do_ref, di_ref, dq_ref, acc_ref, wt_ref,
 ):
     pieces = (d0, d1, d2, d3)
     zero = jnp.zeros((128, 64), BF16)
-    for k in range(4):
-        for kk in range(8):
+    head = lax.broadcasted_iota(jnp.int32, (8, 192), 0) * 64
+    lane = lax.broadcasted_iota(jnp.int32, (8, 192), 1)
+    pick = jnp.where((lane >= head) & (lane < head + 64), 1.0, 0.0).astype(BF16)
+
+    def arrange(kk, carry):
+        rs = pl.ds(pl.multiple_of(kk * 128, 128), 128)
+        for k in range(4):
             b = k * 8 + kk
             at = pl.ds(pl.multiple_of(meta[b] * 128, 128), 128)
-            do = pieces[k][kk * 128 : (kk + 1) * 128, :]
-            prod = jnp.transpose(do.astype(F32) * o_ref[b].astype(F32))
+            do = pieces[k][rs, :]
+            prod = do.astype(F32) * o_ref[b].astype(F32)
+            high = prod.astype(BF16)
+            low = (prod - high.astype(F32)).astype(BF16)
+            di_ref[:, at] = nt(pick, high) + nt(pick, low)
             for h in range(3):
-                di_ref[h : h + 1, at] = jnp.sum(prod[h * 64 : h * 64 + 64, :], axis=0, keepdims=True)
                 do_ref[h, at, :] = jnp.concatenate([zero, do[:, h * 64 : h * 64 + 64]], axis=1)
+        return carry
+
+    lax.fori_loop(0, 8, arrange, 0)
     acc_ref[...] = jnp.zeros_like(acc_ref)
 
     def q_tile(qi, carry):
-        branch = qi >= 8
-        fork = meta[64 + jnp.maximum(qi - 8, 0)]
-        full = jnp.where(branch, fork // 256, qi)
+        count, tile = tile_plan(meta, qi)
         qs = pl.ds(pl.multiple_of(qi * 256, 256), 256)
         dq_ref[...] = jnp.zeros_like(dq_ref)
 
-        def k_tile(kt, mask):
-            ks = pl.ds(pl.multiple_of(kt * 256, 256), 256)
+        def k_tile(t, own):
+            ks, mask = tile(t, own)
+            q = [q_ref[h, qs, :] for h in range(3)]
+            do = [do_ref[h, qs, :] for h in range(3)]
+            kv = [kv_ref[h, ks, :] for h in range(3)]
+            s = [nt(kv[h], q[h]) for h in range(3)]
+            dp = [nt(kv[h], do[h]) for h in range(3)]
+            p, ds = [], []
             for h in range(3):
-                kv = kv_ref[h, ks, :]
-                q, do = q_ref[h, qs, :], do_ref[h, qs, :]
-                p = jnp.exp2(nt(kv, q) - lse_ref[h : h + 1, qs])
-                if mask is not None:
-                    p = jnp.where(mask, p, 0.0)
-                ds = (p * (nt(kv, do) - di_ref[h : h + 1, qs])).astype(BF16)
-                acc_ref[h, ks, :] += nn(ds, q) + nn(p.astype(BF16), do)
+                e = jnp.where(mask, jnp.exp2(s[h] - lse_ref[h : h + 1, qs]), 0.0)
+                p.append(e.astype(BF16))
+                ds.append((e * (dp[h] - di_ref[h : h + 1, qs])).astype(BF16))
+            for h in range(3):
+                acc_ref[h, ks, :] += nn(ds[h], q[h]) + nn(p[h], do[h])
                 hs = slice(h * 64, h * 64 + 64)
-                dq_ref[hs, :] += nn(tr_ref[h, :, ks], ds)
-
-        def full_tile(kt, c):
-            k_tile(kt, None)
-            return c
-
-        lax.fori_loop(0, full, full_tile, 0)
-
-        @pl.when(branch & (fork % 256 != 0))
-        def _():
-            k_tile(full, tile_mask(False, full, fork))
-
-        k_tile(qi, tile_mask(True, 0, 0))
+                dq_ref[hs, :] += nn(tr_ref[h, :, ks], ds[h])
+
+        tile_pairs(count, k_tile)
         out_ref[qs, 0:192] = (jnp.transpose(dq_ref[...]) * HEAD ** (-0.5)).astype(BF16)
         return carry
 
@@ -682,10 +702,20 @@
         return carry
 
     lax.fori_loop(0, 16, finish, 0)
-    for k, x_ref in enumerate((x0, x1, x2, x3)):
-        for kk in range(8):
-            at = pl.ds(pl.multiple_of(meta[k * 8 + kk] * 128, 128), 128)
-            x_ref[kk * 128 : (kk + 1) * 128, :] = nt(out_ref[at, :], w_ref[...]).astype(BF16)
+    wt = jnp.transpose(w_ref[...])
+    wt_ref[...] = wt
+
+    def spread(i, carry):
+        rs = pl.ds(pl.multiple_of(i * 512, 512), 512)
+        for k, x_ref in enumerate((x0, x1, x2, x3)):
+            rows = [
+                out_ref[pl.ds(pl.multiple_of(meta[k * 8 + i * 4 + u] * 128, 128), 128), :]
+                for u in range(4)
+            ]
+            x_ref[rs, :] = nn(jnp.concatenate(rows, axis=0), wt_ref[...]).astype(BF16)
+        return carry
+
+    lax.fori_loop(0, 2, spread, 0)
 
 
 def attend_back_call(meta, q, kv, tr, o, lse, pieces, w2):
@@ -702,6 +732,7 @@
                 pltpu.VMEM((8, 4096), F32),
                 pltpu.VMEM((192, 256), F32),
                 pltpu.VMEM((3, 4096, 128), F32),
+                pltpu.VMEM((576, 768), BF16),
             ],
         ),
         out_shape=[jax.ShapeDtypeStruct((4096, 576), BF16)]

time: 667 us -> 635 us (0.952)
  Pallas kernels: 334 us -> 268 us
  waiting for transfers between devices: 142 us -> 188 us
  starting transfers between devices: 76.4 us -> 66.5 us
    all_gather x1, waiting for transfers between devices: 0.01 us -> 46 us  [home_body(): dense = lax.all_gather(dense, AXES, axis=0)]
    pallas_call x1, Pallas kernels: 86 us -> 47.1 us  [attend_call(): pl.pallas_call(attend_kernel, grid_spec=pltpu.PrefetchScalarGridSpec(num_...]
    pallas_call x1, Pallas kernels: 101 us -> 73.9 us  [attend_back_call(): pl.pallas_call(attend_back_kernel, grid_spec=pltpu.PrefetchScalarGridSpec...]
    ppermute x51, starting transfers between devices: 76.3 us -> 66.4 us  [send(): return lax.ppermute(v, AXES, device_pairs(dp_count, move, back))]
  transfers between devices with their start and end apart: 53 -> 53, of which waited for: 20 -> 23; matrix products, arithmetic and copies ran while one was open for 11% -> 12% of each run, Pallas kernels for 34% -> 25%
where the time goes in v3:
time: 635 us; the launch traced here: 626 us
  Pallas kernels  268 us (42%)
  waiting for transfers between devices  188 us (30%)
  starting transfers between devices  66.5 us (10%)
  local copies, waits for them, and re-layouts  65.4 us (10%)
  other arithmetic  23.1 us (4%)
  between operations  15.2 us (2%)
    ppermute x51, waiting for transfers between devices, send(): return lax.ppermute(v, AXES, device_pairs(dp_count, move, back))  142 us
    pallas_call x1, Pallas kernels, attend_back_call(): pl.pallas_call(attend_back_kernel, grid_spec=pltpu.PrefetchScalarGridSpec...  73.9 us
    ppermute x51, starting transfers between devices, send(): return lax.ppermute(v, AXES, device_pairs(dp_count, move, back))  66.4 us
    pallas_call x1, Pallas kernels, attend_call(): pl.pallas_call(attend_kernel, grid_spec=pltpu.PrefetchScalarGridSpec(num_...  47.1 us
    all_gather x1, waiting for transfers between devices, home_body(): dense = lax.all_gather(dense, AXES, axis=0)  46 us
    pallas_call x1, Pallas kernels, feed_call(): pl.pallas_call(feed_kernel, grid=(tiles,), in_specs=[whole(n3.shape), who...  43.1 us
    pallas_call x1, Pallas kernels, mid_back_call(): pl.pallas_call(mid_back_kernel, grid_spec=pltpu.PrefetchScalarGridSpec(nu...  41.1 us
    pallas_call x1, Pallas kernels, mid_call(): pl.pallas_call(mid_kernel, grid_spec=pltpu.PrefetchScalarGridSpec(num_sca...  27.8 us
  transfers between devices with their start and end apart: 53, of which 23 were waited for; matrix products, arithmetic and copies ran while one was open for 12% of the time, Pallas kernels for 25%

profile of v3, /device:TPU:20, one launch (start us, length us, event | category | flops | bytes accessed | tf_op | source)
XLA Modules:
  0.0 626.1 jit_solution(16627632701847959828)
XLA Ops:
  17.0 5.5 collective-permute-start.5
  23.4 4.8 collective-permute-done.4
  28.3 25.6 %collective-permute-done.5.refs_0_ = bf16[544,768]{1,0:T(8,128)(2,1)} collective-permute-done((bf16[544,768]{1,0:T(8,128)(2,1)S(1)}, bf16[544,768]{1,0:T(8,128)(2,1)}, u32[]{:S(2)}, u32[]{:S(2)}) %collective-permute-start.5) | collective-permute-done | bytes 835616 | tf_op jit(solution)/shard_map/ppermute | solution.py:1130
  54.0 13.6 %collective-permute-done.7 = bf16[2,2,2,80,192]{4,3,2,1,0:T(8,128)(2,1)S(1)} collective-permute-done((bf16[2,2,2,80,192]{4,3,2,1,0:T(8,128)(2,1)S(1)}, bf16[2,2,2,80,192]{4,3,2,1,0:T(8,128)(2,1)S(1)}, u32[]{:S(2)}, u32[]{:S(2)}) %collective-permute-start.7) | collective-permute-done | bytes 245792 | tf_op jit(solution)/shard_map/ppermute | solution.py:1130
  67.7 4.3 collective-permute-start.8
  74.1 11.9 %collective-permute-done.8 = bf16[2,2,2,2,80,192]{5,4,3,0,2,1:T(8,128)(2,1)S(1)} collective-permute-done((bf16[2,2,2,2,80,192]{5,4,3,0,2,1:T(8,128)(2,1)S(1)}, bf16[2,2,2,2,80,192]{5,4,3,0,2,1:T(8,128)(2,1)S(1)}, u32[]{:S(2)}, u32[]{:S(2)}) %collective-permute-start.8) | collective-permute-done | bytes 491552 | tf_op jit(solution)/shard_map/ppermute | solution.py:1130
  87.9 20.9 %collective-permute-done.10.refs_3_ = bf16[544,768]{1,0:T(8,128)(2,1)} collective-permute-done((bf16[544,768]{1,0:T(8,128)(2,1)}, bf16[544,768]{1,0:T(8,128)(2,1)}, u32[]{:S(2)}, u32[]{:S(2)}) %collective-permute-start.10) | collective-permute-done | bytes 835616 | tf_op jit(solution)/shard_map/ppermute | solution.py:1130
  130.3 17.5 %qkv.1 = (bf16[3,4096,128]{2,1,0:T(8,128)(2,1)}, bf16[3,4096,128]{2,1,0:T(8,128)(2,1)}, bf16[6,64,4096]{2,1,0:T(8,128)(2,1)}, bf16[4096,768]{1,0:T(8,128)(2,1)}) custom-call(s32[128]{0:T(128)} %pad_add_fusion.1.meta, bf16[544,768]{1,0:T(8,128)(2,1)} %collective-permute-done.5.refs_0_, bf16[544,768]{1,0:T(8,128)(2,1)} %collective-permute-done.6.refs_1_, ...), custom_call_target="tpu_custom_call" | custom-call | flops 3623878656 | bytes 20000000 | tf_op jit(solution)/shard_map/qkv/pallas_call | solution.py:517
  147.9 47.1 %attend.1 = (bf16[32,128,192]{2,1,0:T(8,128)(2,1)}, f32[8,4096]{1,0:T(8,128)}) custom-call(s32[128]{0:T(128)} %pad_add_fusion.1.meta, bf16[3,4096,128]{2,1,0:T(8,128)(2,1)} %get-tuple-element.84.q_ref, bf16[3,4096,128]{2,1,0:T(8,128)(2,1)} %get-tuple-element.85.kv_ref, bf16[6,64,4096]{2,1,0:T(8,128)(2,1)} %get-tuple-element.86.tr_ref), custom_call_target="tpu_custom_call" | custom-call | flops 20000000000 | bytes 10000000 | tf_op jit(solution)/shard_map/attend/pallas_call | solution.py:618
  203.5 46.0 %all-gather.3.cloned.1.call-done = bf16[9984,768]{1,0:T(8,128)(2,1)} async-done(((bf16[312,768]{1,0:T(8,128)(2,1)}), bf16[9984,768]{1,0:T(8,128)(2,1)}) %all-gather.3.cloned.1.call-update) | async-done | bytes 15335440 | tf_op jit(solution)/shard_map/all_gather | solution.py:1208
  249.4 4.8 slice.589
  254.2 5.9 fusion.19
  264.5 27.8 %middle.1 = (f32[1024,768]{1,0:T(8,128)}, f32[1024,768]{1,0:T(8,128)}, bf16[1024,768]{1,0:T(8,128)(2,1)}, bf16[1024,768]{1,0:T(8,128)(2,1)}, bf16[1024,768]{1,0:...) custom-call(s32[128]{0:T(128)} %pad_add_fusion.1.meta, ...), custom_call_target="tpu_custom_call" | custom-call | flops 8000000000 | bytes 25000000 | tf_op jit(solution)/shard_map/middle/pallas_call | solution.py:852
  292.3 43.1 %feed.1 = (bf16[1024,768]{1,0:T(8,128)(2,1)}, f32[1024,768]{1,0:T(8,128)}, bf16[4,768,768]{2,1,0:T(8,128)(2,1)}, bf16[4,768,768]{2,1,0:T(8,128)(2,1)}, f32[32,768]{1,0:T(8,128)}, /*index=5*/f32[8,768]{1,0:T(8,128)}) custom-call(bf16[1024,768]{1,0:T(8,128)(2,1)} %get-tuple-element.90.n3_ref, bf16[1024,768]{1,0:T(8,128)(2,1)} %constant_dynamic-update-slice_fusion.20.og_ref, ...), custom_call_target="tpu_custom_call" | custom-call | flops 28991029248 | bytes 35000000 | tf_op jit(solution)/shard_map/feed/pallas_call | solution.py:932
  335.4 41.1 %middle_back.1 = (f32[1024,768]{1,0:T(8,128)}, bf16[1024,192]{1,0:T(8,128)(2,1)}, bf16[1024,192]{1,0:T(8,128)(2,1)}, bf16[1024,192]{1,0:T(8,128)(2,1)}, bf16[102...) custom-call(s32[128]{0:T(128)} %pad_add_fusion.1.meta, ...), custom_call_target="tpu_custom_call" | custom-call | flops 22000001024 | bytes 35000000 | tf_op jit(solution)/shard_map/middle_back/pallas_call | solution.py:1052
  410.2 4.8 collective-permute-start.27
  415.0 73.9 %attend_back.1 = (bf16[4096,576]{1,0:T(8,128)(2,1)}, bf16[1024,768]{1,0:T(8,128)(2,1)}, bf16[1024,768]{1,0:T(8,128)(2,1)}, bf16[1024,768]{1,0:T(8,128)(2,1)}, bf16[1024,768]{1,0:T(8,128)(2,1)}) custom-call(s32[128]{0:T(128)} %pad_add_fusion.1.meta, bf16[3,4096,128]{2,1,0:T(8,128)(2,1)} %get-tuple-element.84.q_ref, ...), custom_call_target="tpu_custom_call" | custom-call | flops 49999998976 | bytes 15000000 | tf_op jit(solution)/shard_map/attend_back/pallas_call | solution.py:723
  494.5 9.3 %win.1 = (bf16[768,576]{1,0:T(8,128)(2,1)}, f32[8,576]{1,0:T(8,128)}) custom-call(bf16[4096,768]{1,0:T(8,128)(2,1)} %get-tuple-element.121.n_ref, bf16[4096,576]{1,0:T(8,128)(2,1)} %get-tuple-element.122.d_ref), custom_call_target="tpu_custom_call" | custom-call | flops 3623878656 | bytes 12000000 | tf_op jit(solution)/shard_map/win/pallas_call | solution.py:764
  532.7 5.4 collective-permute-done.35.c_ref
  538.1 4.1 first_back1.1
  542.2 11.9 %collective-permute-done.33.c_ref = bf16[512,768]{1,0:T(8,128)(2,1)} collective-permute-done((bf16[512,768]{1,0:T(8,128)(2,1)}, bf16[512,768]{1,0:T(8,128)(2,1)}, u32[]{:S(2)}, u32[]{:S(2)}) %collective-permute-start.33) | collective-permute-done | bytes 786464 | tf_op jit(solution)/shard_map/ppermute | solution.py:1130
  554.2 4.3 first_back0.1
  586.9 15.8 %collective-permute-done.34 = bf16[512,768]{1,0:T(8,128)(2,1)S(1)} collective-permute-done((bf16[512,768]{1,0:T(8,128)(2,1)}, bf16[512,768]{1,0:T(8,128)(2,1)S(1)}, u32[]{:S(2)}, u32[]{:S(2)}) %collective-permute-start.34) | collective-permute-done | bytes 786464 | tf_op jit(solution)/shard_map/ppermute | solution.py:1130
  602.6 9.5 %collective-permute-done.36 = bf16[512,768]{1,0:T(8,128)(2,1)S(1)} collective-permute-done((bf16[512,768]{1,0:T(8,128)(2,1)S(1)}, bf16[512,768]{1,0:T(8,128)(2,1)S(1)}, u32[]{:S(2)}, u32[]{:S(2)}) %collective-permute-start.36) | collective-permute-done | bytes 786464 | tf_op jit(solution)/shard_map/ppermute | solution.py:1130
  (319 shorter events, 152.0 us)
Async XLA Ops:
  7.2 242.2 %all-gather.3.cloned.1.call-start = ((), (), s32[]{:S(2)}) async-start(), calls=%async_computation.2 | async-start | bytes 15814656 | tf_op jit(solution)/shard_map/all_gather | solution.py:1208
  16.9 56.7 %collective-permute-start.6 = (bf16[544,768]{1,0:T(8,128)(2,1)S(1)}, bf16[544,768]{1,0:T(8,128)(2,1)}, u32[]{:S(2)}, u32[]{:S(2)}) collective-permute-start(bf16[544,768]{1,0:T(8,128)(2,1)S(1)} %get-tuple-element.161), channel_id=1, source_target_pairs={{0,2},{1,3},{2,0},{3,1},{4,10},{5,11},{6,8},{7,9},{8,6},{9,7},{10,... | collective-permute-start | bytes 2506760 | tf_op jit(solution)/shard_map/ppermute | solution.py:1130
  17.0 36.9 %collective-permute-start.5 = (bf16[544,768]{1,0:T(8,128)(2,1)S(1)}, bf16[544,768]{1,0:T(8,128)(2,1)}, u32[]{:S(2)}, u32[]{:S(2)}) collective-permute-start(bf16[544,768]{1,0:T(8,128)(2,1)S(1)} %get-tuple-element.162), channel_id=1, source_target_pairs={{0,0},{1,1},{2,2},{3,3},{4,8},{5,9},{6,10},{7,11},{8,4},{9,5},{10,... | collective-permute-start | bytes 2506760 | tf_op jit(solution)/shard_map/ppermute | solution.py:1130
  72.0 36.7 %collective-permute-start.9 = (bf16[544,768]{1,0:T(8,128)(2,1)}, bf16[544,768]{1,0:T(8,128)(2,1)}, u32[]{:S(2)}, u32[]{:S(2)}) collective-permute-start(bf16[544,768]{1,0:T(8,128)(2,1)} %collective-permute-done.5.refs_0_), channel_id=1, source_target_pairs={{0,1},{1,0},{2,3},{3,2},{4,5},{5,4},{6,7},{7,6},{8,9},{9,8},{10,11... | collective-permute-start | bytes 2506760 | tf_op jit(solution)/shard_map/ppermute | solution.py:1130
  73.6 35.2 %collective-permute-start.10 = (bf16[544,768]{1,0:T(8,128)(2,1)}, bf16[544,768]{1,0:T(8,128)(2,1)}, u32[]{:S(2)}, u32[]{:S(2)}) collective-permute-start(bf16[544,768]{1,0:T(8,128)(2,1)} %collective-permute-done.6.refs_1_), channel_id=1, source_target_pairs={{0,1},{1,0},{2,3},{3,2},{4,5},{5,4},{6,7},{7,6},{8,9},{9,8},{10,11... | collective-permute-start | bytes 2506760 | tf_op jit(solution)/shard_map/ppermute | solution.py:1130
  108.8 505.5 %reduce-scatter.2.cloned.1.call-start = ((), (), s32[]{:S(2)}) async-start(), calls=%async_computation.1 | async-start | bytes 15814656 | tf_op jit(solution)/shard_map/reduce_scatter | solution.py:1250
  124.9 77.6 %collective-permute-start.19 = (bf16[512,768]{1,0:T(8,128)(2,1)S(1)}, bf16[512,768]{1,0:T(8,128)(2,1)S(1)}, u32[]{:S(2)}, u32[]{:S(2)}) collective-permute-start(bf16[512,768]{1,0:T(8,128)(2,1)S(1)} %get-tuple-element.171), channel_id=1, source_target_pairs={{0,2},{1,3},{2,0},{3,1},{4,10},{5,11},{6,8},{7,9},{8,6},{9,7},{10,... | collective-permute-start | bytes 2359304 | tf_op jit(solution)/shard_map/ppermute | solution.py:1130
  127.3 74.1 %collective-permute-start.18 = (bf16[512,768]{1,0:T(8,128)(2,1)S(1)}, bf16[512,768]{1,0:T(8,128)(2,1)S(1)}, u32[]{:S(2)}, u32[]{:S(2)}) collective-permute-start(bf16[512,768]{1,0:T(8,128)(2,1)S(1)} %get-tuple-element.172), channel_id=1, source_target_pairs={{0,0},{1,1},{2,2},{3,3},{4,8},{5,9},{6,10},{7,11},{8,4},{9,5},{10,... | collective-permute-start | bytes 2359304 | tf_op jit(solution)/shard_map/ppermute | solution.py:1130
  197.7 66.9 %collective-permute-start.16 = (bf16[1024,192]{1,0:T(8,128)(2,1)}, bf16[1024,192]{1,0:T(8,128)(2,1)}, u32[]{:S(2)}, u32[]{:S(2)}) collective-permute-start(bf16[1024,192]{1,0:T(8,128)(2,1)} %bitcast.36), channel_id=1, source_target_pairs={{0,8},{1,9},{2,10},{3,11},{4,12},{5,13},{6,14},{7,15},{8,0},{9,1},... | collective-permute-start | bytes 1179656 | tf_op jit(solution)/shard_map/ppermute | solution.py:1130
  197.7 66.9 %collective-permute-start.17 = (bf16[1024,192]{1,0:T(8,128)(2,1)}, bf16[1024,192]{1,0:T(8,128)(2,1)}, u32[]{:S(2)}, u32[]{:S(2)}) collective-permute-start(bf16[1024,192]{1,0:T(8,128)(2,1)} %bitcast.37), channel_id=1, source_target_pairs={{0,9},{1,8},{2,11},{3,10},{4,13},{5,12},{6,15},{7,14},{8,1},{9,0},... | collective-permute-start | bytes 1179656 | tf_op jit(solution)/shard_map/ppermute | solution.py:1130
  199.3 65.2 %collective-permute-start.15 = (bf16[1024,192]{1,0:T(8,128)(2,1)S(1)}, bf16[1024,192]{1,0:T(8,128)(2,1)}, u32[]{:S(2)}, u32[]{:S(2)}) collective-permute-start(bf16[1024,192]{1,0:T(8,128)(2,1)S(1)} %bitcast.220), channel_id=1, source_target_pairs={{0,1},{1,0},{2,3},{3,2},{4,5},{5,4},{6,7},{7,6},{8,9},{9,8},{10,11... | collective-permute-start | bytes 1179656 | tf_op jit(solution)/shard_map/ppermute | solution.py:1130
  376.5 21.2 %collective-permute-start.20 = (bf16[1024,192]{1,0:T(8,128)(2,1)}, bf16[1024,192]{1,0:T(8,128)(2,1)S(1)}, u32[]{:S(2)}, u32[]{:S(2)}) collective-permute-start(bf16[1024,192]{1,0:T(8,128)(2,1)} %get-tuple-element.107), channel_id=1, source_target_pairs={{0,1},{1,0},{2,3},{3,2},{4,5},{5,4},{6,7},{7,6},{8,9},{9,8},{10,11... | collective-permute-start | bytes 1179656 | tf_op jit(solution)/shard_map/ppermute | solution.py:1130
  376.6 21.1 %collective-permute-start.21 = (bf16[1024,192]{1,0:T(8,128)(2,1)}, bf16[1024,192]{1,0:T(8,128)(2,1)S(1)}, u32[]{:S(2)}, u32[]{:S(2)}) collective-permute-start(bf16[1024,192]{1,0:T(8,128)(2,1)} %get-tuple-element.108), channel_id=1, source_target_pairs={{0,8},{1,9},{2,10},{3,11},{4,12},{5,13},{6,14},{7,15},{8,0},{9,1},... | collective-permute-start | bytes 1179656 | tf_op jit(solution)/shard_map/ppermute | solution.py:1130
  376.9 24.5 %collective-permute-start.22 = (bf16[1024,192]{1,0:T(8,128)(2,1)}, bf16[1024,192]{1,0:T(8,128)(2,1)S(1)}, u32[]{:S(2)}, u32[]{:S(2)}) collective-permute-start(bf16[1024,192]{1,0:T(8,128)(2,1)} %get-tuple-element.109), channel_id=1, source_target_pairs={{0,9},{1,8},{2,11},{3,10},{4,13},{5,12},{6,15},{7,14},{8,1},{9,0},... | collective-permute-start | bytes 1179656 | tf_op jit(solution)/shard_map/ppermute | solution.py:1130
  405.5 83.4 %collective-permute-start.24 = (bf16[512,768]{1,0:T(8,128)(2,1)S(1)}, bf16[512,768]{1,0:T(8,128)(2,1)S(1)}, u32[]{:S(2)}, u32[]{:S(2)}) collective-permute-start(bf16[512,768]{1,0:T(8,128)(2,1)S(1)} %get-tuple-element.169), channel_id=1, source_target_pairs={{2,0},{3,1},{0,2},{1,3},{10,4},{11,5},{8,6},{9,7},{6,8},{7,9},{4,1... | collective-permute-start | bytes 2359304 | tf_op jit(solution)/shard_map/ppermute | solution.py:1130
  405.9 83.0 %collective-permute-start.23 = (bf16[512,768]{1,0:T(8,128)(2,1)S(1)}, bf16[512,768]{1,0:T(8,128)(2,1)}, u32[]{:S(2)}, u32[]{:S(2)}) collective-permute-start(bf16[512,768]{1,0:T(8,128)(2,1)S(1)} %get-tuple-element.170), channel_id=1, source_target_pairs={{0,0},{1,1},{2,2},{3,3},{8,4},{9,5},{10,6},{11,7},{4,8},{5,9},{6,1... | collective-permute-start | bytes 2359304 | tf_op jit(solution)/shard_map/ppermute | solution.py:1130
  410.1 78.8 %collective-permute-start.28 = (bf16[32,768]{1,0:T(8,128)(2,1)S(1)}, bf16[32,768]{1,0:T(8,128)(2,1)S(1)}, u32[]{:S(2)}, u32[]{:S(2)}) collective-permute-start(bf16[32,768]{1,0:T(8,128)(2,1)S(1)} %get-tuple-element.212), channel_id=1, source_target_pairs={{2,0},{3,1},{0,2},{1,3},{10,4},{11,5},{8,6},{9,7},{6,8},{7,9},{4,1... | collective-permute-start | bytes 147464 | tf_op jit(solution)/shard_map/ppermute | solution.py:1130
  410.2 78.7 %collective-permute-start.27 = (bf16[32,768]{1,0:T(8,128)(2,1)S(1)}, bf16[32,768]{1,0:T(8,128)(2,1)S(1)}, u32[]{:S(2)}, u32[]{:S(2)}) collective-permute-start(bf16[32,768]{1,0:T(8,128)(2,1)S(1)} %get-tuple-element.213), channel_id=1, source_target_pairs={{0,0},{1,1},{2,2},{3,3},{8,4},{9,5},{10,6},{11,7},{4,8},{5,9},{6,1... | collective-permute-start | bytes 147464 | tf_op jit(solution)/shard_map/ppermute | solution.py:1130
  492.3 40.4 %collective-permute-start.32 = (bf16[1024,768]{1,0:T(8,128)(2,1)}, bf16[1024,768]{1,0:T(8,128)(2,1)S(1)}, u32[]{:S(2)}, u32[]{:S(2)}) collective-permute-start(bf16[1024,768]{1,0:T(8,128)(2,1)} %get-tuple-element.125), channel_id=1, source_target_pairs={{0,8},{1,9},{2,10},{3,11},{4,12},{5,13},{6,14},{7,15},{8,0},{9,1},... | collective-permute-start | bytes 4718600 | tf_op jit(solution)/shard_map/ppermute | solution.py:1130
  510.7 27.4 %collective-permute-start.35 = (bf16[512,768]{1,0:T(8,128)(2,1)S(1)}, bf16[512,768]{1,0:T(8,128)(2,1)}, u32[]{:S(2)}, u32[]{:S(2)}) collective-permute-start(bf16[512,768]{1,0:T(8,128)(2,1)S(1)} %get-tuple-element.165), channel_id=1, source_target_pairs={{0,1},{1,0},{2,3},{3,2},{4,5},{5,4},{6,7},{7,6},{8,9},{9,8},{10,11... | collective-permute-start | bytes 2359304 | tf_op jit(solution)/shard_map/ppermute | solution.py:1130
  511.2 42.9 %collective-permute-start.33 = (bf16[512,768]{1,0:T(8,128)(2,1)}, bf16[512,768]{1,0:T(8,128)(2,1)}, u32[]{:S(2)}, u32[]{:S(2)}) collective-permute-start(bf16[512,768]{1,0:T(8,128)(2,1)} %get-tuple-element.166), channel_id=1, source_target_pairs={{0,1},{1,0},{2,3},{3,2},{4,5},{5,4},{6,7},{7,6},{8,9},{9,8},{10,11... | collective-permute-start | bytes 2359304 | tf_op jit(solution)/shard_map/ppermute | solution.py:1130
  529.3 34.3 %collective-permute-start.31 = (bf16[2,2,2,24,576]{4,3,2,1,0:T(8,128)(2,1)S(1)}, bf16[2,2,2,24,576]{4,3,2,1,0:T(8,128)(2,1)S(1)}, u32[]{:S(2)}, u32[]{:S(2)}) collective-permute-start(bf16[2,2,2,24,576]{4,3,2,1,0:T(8,128)(2,1)S(1)} %dynamic-slice_bitcast_fusion.1), channel_id=1, source_target_pairs={{0,2},{1,3},{2,0},{3,1},{4,6},{5,7},{6,4},{7,5},{8,10},{9,11},{10,... | collective-permute-start | bytes 663560 | tf_op jit(solution)/shard_map/ppermute | solution.py:1130
  573.1 29.5 %collective-permute-start.34 = (bf16[512,768]{1,0:T(8,128)(2,1)}, bf16[512,768]{1,0:T(8,128)(2,1)S(1)}, u32[]{:S(2)}, u32[]{:S(2)}) collective-permute-start(bf16[512,768]{1,0:T(8,128)(2,1)} %get-tuple-element.129), channel_id=1, source_target_pairs={{0,0},{1,1},{2,2},{3,3},{8,4},{9,5},{10,6},{11,7},{4,8},{5,9},{6,1... | collective-permute-start | bytes 2359304 | tf_op jit(solution)/shard_map/ppermute | solution.py:1130
  575.1 37.1 %collective-permute-start.36 = (bf16[512,768]{1,0:T(8,128)(2,1)S(1)}, bf16[512,768]{1,0:T(8,128)(2,1)S(1)}, u32[]{:S(2)}, u32[]{:S(2)}) collective-permute-start(bf16[512,768]{1,0:T(8,128)(2,1)S(1)} %copy-done.20), channel_id=1, source_target_pairs={{2,0},{3,1},{0,2},{1,3},{10,4},{11,5},{8,6},{9,7},{6,8},{7,9},{4,1... | collective-permute-start | bytes 2359304 | tf_op jit(solution)/shard_map/ppermute | solution.py:1130
  (55 other events, 487.1 us)
Sparse Core Ops, SparseCore 0:
  108.9 140.4 all-gather.2
  402.3 174.2 reduce-scatter.1

commit v4 on v3

--- a/solution.py
+++ b/solution.py
@@ -821,19 +821,18 @@
     cq = ((nn(n2, ci_ref[0]) + vec_ref[9:10, :]) * QSCALE).astype(BF16)
     cq_ref[...] = cq
     ca = []
-    for hp in range(6):
-        qp = cq[:, hp * 128 : hp * 128 + 128]
-        out = None
-        for e in range(2):
-            h = hp * 2 + e
-            s = nt(km_ref[h], qp)
-            m = jnp.max(s, axis=0, keepdims=True)
-            p = jnp.exp2(s - m)
-            l = jnp.sum(p, axis=0, keepdims=True)
-            lse_ref[h : h + 1, :] = m + jnp.log2(l)
-            part = nn(vmt_ref[h], p.astype(BF16)) * (1.0 / l)
-            out = part if out is None else out + part
-        ca.append(jnp.transpose(out).astype(BF16))
+    for first in range(0, 12, 4):
+        heads = range(first, first + 4)
+        s = [nt(km_ref[h], cq[:, (h // 2) * 128 : (h // 2) * 128 + 128]) for h in heads]
+        m = [jnp.max(v, axis=0, keepdims=True) for v in s]
+        p = [jnp.exp2(v - w) for v, w in zip(s, m)]
+        part = [nn(vmt_ref[h], v.astype(BF16)) for h, v in zip(heads, p)]
+        for i, h in enumerate(heads):
+            l = jnp.sum(p[i], axis=0, keepdims=True)
+            lse_ref[h : h + 1, :] = m[i] + jnp.log2(l)
+            part[i] = part[i] * (1.0 / l)
+        for i in (0, 2):
+            ca.append(jnp.transpose(part[i] + part[i + 1]).astype(BF16))
     ca = jnp.concatenate(ca, axis=1)
     ca_ref[...] = ca
     ac = acc + nn(ca, co_ref[...]) + vec_ref[11:12, :]
@@ -994,23 +993,23 @@
     dca = nt(gal, co_ref[...]).astype(BF16)
     cq = cq_ref[...]
     dq = []
-    for hp in range(6):
-        ls = slice(hp * 128, hp * 128 + 128)
-        qp, dp_ = cq[:, ls], dca[:, ls]
-        dqt = None
-        parts = []
-        for e in range(2):
-            h = hp * 2 + e
-            p = jnp.exp2(nt(km_ref[h], qp) - lse_ref[h : h + 1, :])
-            dp = nt(vm_ref[h], dp_)
-            inner = jnp.sum(dp * p, axis=0, keepdims=True)
-            ds = (p * (dp - inner)).astype(BF16)
-            part = nn(kmt_ref[h], ds)
-            dqt = part if dqt is None else dqt + part
-            parts.append((nn(ds, qp), nn(p.astype(BF16), dp_)))
-        dq.append(jnp.transpose(dqt))
-        dk_ref[:, ls] += jnp.where(masks[0], parts[0][0], parts[1][0])
-        dv_ref[:, ls] += jnp.where(masks[0], parts[0][1], parts[1][1])
+    for first in range(0, 12, 4):
+        heads = range(first, first + 4)
+        slices = [slice((h // 2) * 128, (h // 2) * 128 + 128) for h in heads]
+        s = [nt(km_ref[h], cq[:, ls]) for h, ls in zip(heads, slices)]
+        dp = [nt(vm_ref[h], dca[:, ls]) for h, ls in zip(heads, slices)]
+        p = [jnp.exp2(v - lse_ref[h : h + 1, :]) for h, v in zip(heads, s)]
+        ds = []
+        for i in range(4):
+            inner = jnp.sum(dp[i] * p[i], axis=0, keepdims=True)
+            ds.append((p[i] * (dp[i] - inner)).astype(BF16))
+        dqt = [nn(kmt_ref[h], v) for h, v in zip(heads, ds)]
+        dk = [nn(v, cq[:, ls]) for v, ls in zip(ds, slices)]
+        dv = [nn(v.astype(BF16), dca[:, ls]) for v, ls in zip(p, slices)]
+        for i in (0, 2):
+            dq.append(jnp.transpose(dqt[i] + dqt[i + 1]))
+            dk_ref[:, slices[i]] += jnp.where(masks[0], dk[i], dk[i + 1])
+            dv_ref[:, slices[i]] += jnp.where(masks[0], dv[i], dv[i + 1])
     dcq = (jnp.concatenate(dq, axis=1) * HEAD ** (-0.5)).astype(BF16)
     count(9, jnp.sum(dcq.astype(F32), axis=0, keepdims=True))
     cq_acc[...] += tn(n2_ref[...], dcq)
@@ -1164,7 +1163,7 @@
         )
     both = jnp.concatenate([tokens, encoder_states], axis=1)
     mine = [send(pick(both, p), home(p)) for p in range(2)]
-    tree, mine[0] = lax.optimization_barrier((tree, mine[0]))
+    tree, *mine = lax.optimization_barrier((tree, *mine))
     across = [send(v, flip(1)) for v in mine]
     near = [send(v, flip(2)) for v in mine]
     tree = merge(tree, send(tree, lambda y, c, z, x: (y, c, z ^ 2, x)), z >> 1)

time: 635 us -> 624 us (0.983)
  Pallas kernels: 268 us -> 253 us
  waiting for transfers between devices: 188 us -> 199 us
    ppermute x51, waiting for transfers between devices: 142 us -> 154 us  [send(): return lax.ppermute(v, AXES, device_pairs(dp_count, move, back))]
    pallas_call x1, Pallas kernels: 27.8 us -> 20 us  [mid_call(): pl.pallas_call(mid_kernel, grid_spec=pltpu.PrefetchScalarGridSpec(num_sca...]
    pallas_call x1, Pallas kernels: 41.1 us -> 34.7 us  [mid_back_call(): pl.pallas_call(mid_back_kernel, grid_spec=pltpu.PrefetchScalarGridSpec(nu...]
  transfers between devices with their start and end apart: 53 -> 53, of which waited for: 23 -> 26; matrix products, arithmetic and copies ran while one was open for 12% -> 12% of each run, Pallas kernels for 25% -> 25%
where the time goes in v4:
time: 624 us; the launch traced here: 618 us
  Pallas kernels  253 us (41%)
  waiting for transfers between devices  199 us (32%)
  local copies, waits for them, and re-layouts  65.4 us (10%)
  starting transfers between devices  61.6 us (10%)
  other arithmetic  23.2 us (4%)
  between operations  15.3 us (2%)
    ppermute x51, waiting for transfers between devices, send(): return lax.ppermute(v, AXES, device_pairs(dp_count, move, back))  154 us
    pallas_call x1, Pallas kernels, attend_back_call(): pl.pallas_call(attend_back_kernel, grid_spec=pltpu.PrefetchScalarGridSpec...  73.5 us
    ppermute x51, starting transfers between devices, send(): return lax.ppermute(v, AXES, device_pairs(dp_count, move, back))  61.5 us
    pallas_call x1, Pallas kernels, attend_call(): pl.pallas_call(attend_kernel, grid_spec=pltpu.PrefetchScalarGridSpec(num_...  46.6 us
    all_gather x1, waiting for transfers between devices, home_body(): dense = lax.all_gather(dense, AXES, axis=0)  44.7 us
    pallas_call x1, Pallas kernels, feed_call(): pl.pallas_call(feed_kernel, grid=(tiles,), in_specs=[whole(n3.shape), who...  43 us
    pallas_call x1, Pallas kernels, mid_back_call(): pl.pallas_call(mid_back_kernel, grid_spec=pltpu.PrefetchScalarGridSpec(nu...  34.7 us
    unnamed x80, local copies, waits for them, and re-layouts  25.8 us
  transfers between devices with their start and end apart: 53, of which 26 were waited for; matrix products, arithmetic and copies ran while one was open for 12% of the time, Pallas kernels for 25%

profile of v4, /device:TPU:20, one launch (start us, length us, event | category | flops | bytes accessed | tf_op | source)
XLA Modules:
  0.0 617.6 jit_solution(17997785526671117377)
XLA Ops:
  17.0 5.5 collective-permute-start.5
  23.4 4.8 collective-permute-done.4
  28.3 7.7 %collective-permute-done.6.refs_1_ = bf16[544,768]{1,0:T(8,128)(2,1)} collective-permute-done((bf16[544,768]{1,0:T(8,128)(2,1)S(1)}, bf16[544,768]{1,0:T(8,128)(2,1)}, u32[]{:S(2)}, u32[]{:S(2)}) %collective-permute-start.6) | collective-permute-done | bytes 835616 | tf_op jit(solution)/shard_map/ppermute | solution.py:1129
  36.1 17.9 %collective-permute-done.5.refs_0_ = bf16[544,768]{1,0:T(8,128)(2,1)} collective-permute-done((bf16[544,768]{1,0:T(8,128)(2,1)S(1)}, bf16[544,768]{1,0:T(8,128)(2,1)}, u32[]{:S(2)}, u32[]{:S(2)}) %collective-permute-start.5) | collective-permute-done | bytes 835616 | tf_op jit(solution)/shard_map/ppermute | solution.py:1129
  54.0 13.6 %collective-permute-done.7 = bf16[2,2,2,80,192]{4,3,2,1,0:T(8,128)(2,1)S(1)} collective-permute-done((bf16[2,2,2,80,192]{4,3,2,1,0:T(8,128)(2,1)S(1)}, bf16[2,2,2,80,192]{4,3,2,1,0:T(8,128)(2,1)S(1)}, u32[]{:S(2)}, u32[]{:S(2)}) %collective-permute-start.7) | collective-permute-done | bytes 245792 | tf_op jit(solution)/shard_map/ppermute | solution.py:1129
  74.1 11.9 %collective-permute-done.8 = bf16[2,2,2,2,80,192]{5,4,3,0,2,1:T(8,128)(2,1)S(1)} collective-permute-done((bf16[2,2,2,2,80,192]{5,4,3,0,2,1:T(8,128)(2,1)S(1)}, bf16[2,2,2,2,80,192]{5,4,3,0,2,1:T(8,128)(2,1)S(1)}, u32[]{:S(2)}, u32[]{:S(2)}) %collective-permute-start.8) | collective-permute-done | bytes 491552 | tf_op jit(solution)/shard_map/ppermute | solution.py:1129
  87.9 6.0 collective-permute-done.9.refs_2_
  93.9 14.9 %collective-permute-done.10.refs_3_ = bf16[544,768]{1,0:T(8,128)(2,1)} collective-permute-done((bf16[544,768]{1,0:T(8,128)(2,1)}, bf16[544,768]{1,0:T(8,128)(2,1)}, u32[]{:S(2)}, u32[]{:S(2)}) %collective-permute-start.10) | collective-permute-done | bytes 835616 | tf_op jit(solution)/shard_map/ppermute | solution.py:1129
  130.2 17.5 %qkv.1 = (bf16[3,4096,128]{2,1,0:T(8,128)(2,1)}, bf16[3,4096,128]{2,1,0:T(8,128)(2,1)}, bf16[6,64,4096]{2,1,0:T(8,128)(2,1)}, bf16[4096,768]{1,0:T(8,128)(2,1)}) custom-call(s32[128]{0:T(128)} %pad_add_fusion.1.meta, bf16[544,768]{1,0:T(8,128)(2,1)} %collective-permute-done.5.refs_0_, bf16[544,768]{1,0:T(8,128)(2,1)} %collective-permute-done.6.refs_1_, ...), custom_call_target="tpu_custom_call" | custom-call | flops 3623878656 | bytes 20000000 | tf_op jit(solution)/shard_map/qkv/pallas_call | solution.py:517
  147.8 46.6 %attend.1 = (bf16[32,128,192]{2,1,0:T(8,128)(2,1)}, f32[8,4096]{1,0:T(8,128)}) custom-call(s32[128]{0:T(128)} %pad_add_fusion.1.meta, bf16[3,4096,128]{2,1,0:T(8,128)(2,1)} %get-tuple-element.86.q_ref, bf16[3,4096,128]{2,1,0:T(8,128)(2,1)} %get-tuple-element.87.kv_ref, bf16[6,64,4096]{2,1,0:T(8,128)(2,1)} %get-tuple-element.88.tr_ref), custom_call_target="tpu_custom_call" | custom-call | flops 20000000000 | bytes 10000000 | tf_op jit(solution)/shard_map/attend/pallas_call | solution.py:618
  202.8 44.7 %all-gather.3.cloned.1.call-done = bf16[9984,768]{1,0:T(8,128)(2,1)} async-done(((bf16[312,768]{1,0:T(8,128)(2,1)}), bf16[9984,768]{1,0:T(8,128)(2,1)}) %all-gather.3.cloned.1.call-update) | async-done | bytes 15335440 | tf_op jit(solution)/shard_map/all_gather | solution.py:1207
  252.3 5.9 fusion.19
  262.7 20.0 %middle.1 = (f32[1024,768]{1,0:T(8,128)}, f32[1024,768]{1,0:T(8,128)}, bf16[1024,768]{1,0:T(8,128)(2,1)}, bf16[1024,768]{1,0:T(8,128)(2,1)}, bf16[1024,768]{1,0:...) custom-call(s32[128]{0:T(128)} %pad_add_fusion.1.meta, ...), custom_call_target="tpu_custom_call" | custom-call | flops 8000000000 | bytes 25000000 | tf_op jit(solution)/shard_map/middle/pallas_call | solution.py:851
  282.7 43.0 %feed.1 = (bf16[1024,768]{1,0:T(8,128)(2,1)}, f32[1024,768]{1,0:T(8,128)}, bf16[4,768,768]{2,1,0:T(8,128)(2,1)}, bf16[4,768,768]{2,1,0:T(8,128)(2,1)}, f32[32,768]{1,0:T(8,128)}, /*index=5*/f32[8,768]{1,0:T(8,128)}) custom-call(bf16[1024,768]{1,0:T(8,128)(2,1)} %get-tuple-element.92.n3_ref, bf16[1024,768]{1,0:T(8,128)(2,1)} %constant_dynamic-update-slice_fusion.20.og_ref, ...), custom_call_target="tpu_custom_call" | custom-call | flops 28991029248 | bytes 35000000 | tf_op jit(solution)/shard_map/feed/pallas_call | solution.py:931
  325.7 34.7 %middle_back.1 = (f32[1024,768]{1,0:T(8,128)}, bf16[1024,192]{1,0:T(8,128)(2,1)}, bf16[1024,192]{1,0:T(8,128)(2,1)}, bf16[1024,192]{1,0:T(8,128)(2,1)}, bf16[102...) custom-call(s32[128]{0:T(128)} %pad_add_fusion.1.meta, ...), custom_call_target="tpu_custom_call" | custom-call | flops 22000001024 | bytes 35000000 | tf_op jit(solution)/shard_map/middle_back/pallas_call | solution.py:1051
  399.1 73.5 %attend_back.1 = (bf16[4096,576]{1,0:T(8,128)(2,1)}, bf16[1024,768]{1,0:T(8,128)(2,1)}, bf16[1024,768]{1,0:T(8,128)(2,1)}, bf16[1024,768]{1,0:T(8,128)(2,1)}, bf16[1024,768]{1,0:T(8,128)(2,1)}) custom-call(s32[128]{0:T(128)} %pad_add_fusion.1.meta, bf16[3,4096,128]{2,1,0:T(8,128)(2,1)} %get-tuple-element.86.q_ref, ...), custom_call_target="tpu_custom_call" | custom-call | flops 49999998976 | bytes 15000000 | tf_op jit(solution)/shard_map/attend_back/pallas_call | solution.py:723
  478.1 9.1 %win.1 = (bf16[768,576]{1,0:T(8,128)(2,1)}, f32[8,576]{1,0:T(8,128)}) custom-call(bf16[4096,768]{1,0:T(8,128)(2,1)} %get-tuple-element.123.n_ref, bf16[4096,576]{1,0:T(8,128)(2,1)} %get-tuple-element.124.d_ref), custom_call_target="tpu_custom_call" | custom-call | flops 3623878656 | bytes 12000000 | tf_op jit(solution)/shard_map/win/pallas_call | solution.py:764
  494.4 11.3 %collective-permute-start.30 = (bf16[1,2,4,2,24,576]{5,4,3,2,1,0:T(8,128)(2,1)S(1)}, bf16[1,2,4,2,24,576]{5,4,3,2,1,0:T(8,128)(2,1)S(1)}, u32[]{:S(2)}, u32[]{:S(2)}) collective-permute-start(bf16[1,2,4,2,24,576]{5,4,3,2,1,0:T(8,128)(2,1)S(1)} %dynamic-slice_bitcast_fusion), channel_id=1, source_target_pairs={{0,16},{1,17},{2,18},{3,19},{4,20},{5,21},{6,22},{7,23},{8,24},{9,... | collective-permute-start | bytes 1327112 | tf_op jit(solution)/shard_map/ppermute | solution.py:1129
  513.4 4.9 collective-permute-done.45
  519.1 6.9 %collective-permute-done.46 = f32[16,768]{1,0:T(8,128)S(1)} collective-permute-done((f32[16,768]{1,0:T(8,128)S(1)}, f32[16,768]{1,0:T(8,128)S(1)}, u32[]{:S(2)}, u32[]{:S(2)}) %collective-permute-start.46) | collective-permute-done | bytes 49184 | tf_op jit(solution)/shard_map/ppermute | solution.py:1129
  526.5 6.7 %collective-permute-done.35.c_ref = bf16[512,768]{1,0:T(8,128)(2,1)} collective-permute-done((bf16[512,768]{1,0:T(8,128)(2,1)S(1)}, bf16[512,768]{1,0:T(8,128)(2,1)}, u32[]{:S(2)}, u32[]{:S(2)}) %collective-permute-start.35) | collective-permute-done | bytes 786464 | tf_op jit(solution)/shard_map/ppermute | solution.py:1129
  537.3 11.5 %collective-permute-done.33.c_ref = bf16[512,768]{1,0:T(8,128)(2,1)} collective-permute-done((bf16[512,768]{1,0:T(8,128)(2,1)}, bf16[512,768]{1,0:T(8,128)(2,1)}, u32[]{:S(2)}, u32[]{:S(2)}) %collective-permute-start.33) | collective-permute-done | bytes 786464 | tf_op jit(solution)/shard_map/ppermute | solution.py:1129
  577.6 16.3 %collective-permute-done.34 = bf16[512,768]{1,0:T(8,128)(2,1)S(1)} collective-permute-done((bf16[512,768]{1,0:T(8,128)(2,1)}, bf16[512,768]{1,0:T(8,128)(2,1)S(1)}, u32[]{:S(2)}, u32[]{:S(2)}) %collective-permute-start.34) | collective-permute-done | bytes 786464 | tf_op jit(solution)/shard_map/ppermute | solution.py:1129
  593.9 9.7 %collective-permute-done.36 = bf16[512,768]{1,0:T(8,128)(2,1)S(1)} collective-permute-done((bf16[512,768]{1,0:T(8,128)(2,1)S(1)}, bf16[512,768]{1,0:T(8,128)(2,1)S(1)}, u32[]{:S(2)}, u32[]{:S(2)}) %collective-permute-start.36) | collective-permute-done | bytes 786464 | tf_op jit(solution)/shard_map/ppermute | solution.py:1129
  (319 shorter events, 157.7 us)
Async XLA Ops:
  7.2 240.4 %all-gather.3.cloned.1.call-start = ((), (), s32[]{:S(2)}) async-start(), calls=%async_computation.2 | async-start | bytes 15814656 | tf_op jit(solution)/shard_map/all_gather | solution.py:1207
  17.0 36.9 %collective-permute-start.5 = (bf16[544,768]{1,0:T(8,128)(2,1)S(1)}, bf16[544,768]{1,0:T(8,128)(2,1)}, u32[]{:S(2)}, u32[]{:S(2)}) collective-permute-start(bf16[544,768]{1,0:T(8,128)(2,1)S(1)} %get-tuple-element.164), channel_id=1, source_target_pairs={{0,0},{1,1},{2,2},{3,3},{4,8},{5,9},{6,10},{7,11},{8,4},{9,5},{10,... | collective-permute-start | bytes 2506760 | tf_op jit(solution)/shard_map/ppermute | solution.py:1129
  72.0 21.8 %collective-permute-start.9 = (bf16[544,768]{1,0:T(8,128)(2,1)}, bf16[544,768]{1,0:T(8,128)(2,1)}, u32[]{:S(2)}, u32[]{:S(2)}) collective-permute-start(bf16[544,768]{1,0:T(8,128)(2,1)} %collective-permute-done.5.refs_0_), channel_id=1, source_target_pairs={{0,1},{1,0},{2,3},{3,2},{4,5},{5,4},{6,7},{7,6},{8,9},{9,8},{10,11... | collective-permute-start | bytes 2506760 | tf_op jit(solution)/shard_map/ppermute | solution.py:1129
  73.6 35.2 %collective-permute-start.10 = (bf16[544,768]{1,0:T(8,128)(2,1)}, bf16[544,768]{1,0:T(8,128)(2,1)}, u32[]{:S(2)}, u32[]{:S(2)}) collective-permute-start(bf16[544,768]{1,0:T(8,128)(2,1)} %collective-permute-done.6.refs_1_), channel_id=1, source_target_pairs={{0,1},{1,0},{2,3},{3,2},{4,5},{5,4},{6,7},{7,6},{8,9},{9,8},{10,11... | collective-permute-start | bytes 2506760 | tf_op jit(solution)/shard_map/ppermute | solution.py:1129
  108.8 497.0 %reduce-scatter.2.cloned.1.call-start = ((), (), s32[]{:S(2)}) async-start(), calls=%async_computation.1 | async-start | bytes 15814656 | tf_op jit(solution)/shard_map/reduce_scatter | solution.py:1249
  124.8 77.0 %collective-permute-start.19 = (bf16[512,768]{1,0:T(8,128)(2,1)S(1)}, bf16[512,768]{1,0:T(8,128)(2,1)S(1)}, u32[]{:S(2)}, u32[]{:S(2)}) collective-permute-start(bf16[512,768]{1,0:T(8,128)(2,1)S(1)} %get-tuple-element.173), channel_id=1, source_target_pairs={{0,2},{1,3},{2,0},{3,1},{4,10},{5,11},{6,8},{7,9},{8,6},{9,7},{10,... | collective-permute-start | bytes 2359304 | tf_op jit(solution)/shard_map/ppermute | solution.py:1129
  127.2 73.5 %collective-permute-start.18 = (bf16[512,768]{1,0:T(8,128)(2,1)S(1)}, bf16[512,768]{1,0:T(8,128)(2,1)S(1)}, u32[]{:S(2)}, u32[]{:S(2)}) collective-permute-start(bf16[512,768]{1,0:T(8,128)(2,1)S(1)} %get-tuple-element.174), channel_id=1, source_target_pairs={{0,0},{1,1},{2,2},{3,3},{4,8},{5,9},{6,10},{7,11},{8,4},{9,5},{10,... | collective-permute-start | bytes 2359304 | tf_op jit(solution)/shard_map/ppermute | solution.py:1129
  197.0 65.6 %collective-permute-start.16 = (bf16[1024,192]{1,0:T(8,128)(2,1)}, bf16[1024,192]{1,0:T(8,128)(2,1)}, u32[]{:S(2)}, u32[]{:S(2)}) collective-permute-start(bf16[1024,192]{1,0:T(8,128)(2,1)} %bitcast.36), channel_id=1, source_target_pairs={{0,8},{1,9},{2,10},{3,11},{4,12},{5,13},{6,14},{7,15},{8,0},{9,1},... | collective-permute-start | bytes 1179656 | tf_op jit(solution)/shard_map/ppermute | solution.py:1129
  197.0 65.6 %collective-permute-start.17 = (bf16[1024,192]{1,0:T(8,128)(2,1)}, bf16[1024,192]{1,0:T(8,128)(2,1)}, u32[]{:S(2)}, u32[]{:S(2)}) collective-permute-start(bf16[1024,192]{1,0:T(8,128)(2,1)} %bitcast.37), channel_id=1, source_target_pairs={{0,9},{1,8},{2,11},{3,10},{4,13},{5,12},{6,15},{7,14},{8,1},{9,0},... | collective-permute-start | bytes 1179656 | tf_op jit(solution)/shard_map/ppermute | solution.py:1129
  198.6 64.0 %collective-permute-start.15 = (bf16[1024,192]{1,0:T(8,128)(2,1)S(1)}, bf16[1024,192]{1,0:T(8,128)(2,1)}, u32[]{:S(2)}, u32[]{:S(2)}) collective-permute-start(bf16[1024,192]{1,0:T(8,128)(2,1)S(1)} %bitcast.220), channel_id=1, source_target_pairs={{0,1},{1,0},{2,3},{3,2},{4,5},{5,4},{6,7},{7,6},{8,9},{9,8},{10,11... | collective-permute-start | bytes 1179656 | tf_op jit(solution)/shard_map/ppermute | solution.py:1129
  360.4 21.2 %collective-permute-start.20 = (bf16[1024,192]{1,0:T(8,128)(2,1)}, bf16[1024,192]{1,0:T(8,128)(2,1)S(1)}, u32[]{:S(2)}, u32[]{:S(2)}) collective-permute-start(bf16[1024,192]{1,0:T(8,128)(2,1)} %get-tuple-element.109), channel_id=1, source_target_pairs={{0,1},{1,0},{2,3},{3,2},{4,5},{5,4},{6,7},{7,6},{8,9},{9,8},{10,11... | collective-permute-start | bytes 1179656 | tf_op jit(solution)/shard_map/ppermute | solution.py:1129
  360.5 21.1 %collective-permute-start.21 = (bf16[1024,192]{1,0:T(8,128)(2,1)}, bf16[1024,192]{1,0:T(8,128)(2,1)S(1)}, u32[]{:S(2)}, u32[]{:S(2)}) collective-permute-start(bf16[1024,192]{1,0:T(8,128)(2,1)} %get-tuple-element.110), channel_id=1, source_target_pairs={{0,8},{1,9},{2,10},{3,11},{4,12},{5,13},{6,14},{7,15},{8,0},{9,1},... | collective-permute-start | bytes 1179656 | tf_op jit(solution)/shard_map/ppermute | solution.py:1129
  360.8 24.5 %collective-permute-start.22 = (bf16[1024,192]{1,0:T(8,128)(2,1)}, bf16[1024,192]{1,0:T(8,128)(2,1)S(1)}, u32[]{:S(2)}, u32[]{:S(2)}) collective-permute-start(bf16[1024,192]{1,0:T(8,128)(2,1)} %get-tuple-element.111), channel_id=1, source_target_pairs={{0,9},{1,8},{2,11},{3,10},{4,13},{5,12},{6,15},{7,14},{8,1},{9,0},... | collective-permute-start | bytes 1179656 | tf_op jit(solution)/shard_map/ppermute | solution.py:1129
  389.4 83.2 %collective-permute-start.24 = (bf16[512,768]{1,0:T(8,128)(2,1)S(1)}, bf16[512,768]{1,0:T(8,128)(2,1)S(1)}, u32[]{:S(2)}, u32[]{:S(2)}) collective-permute-start(bf16[512,768]{1,0:T(8,128)(2,1)S(1)} %get-tuple-element.171), channel_id=1, source_target_pairs={{2,0},{3,1},{0,2},{1,3},{10,4},{11,5},{8,6},{9,7},{6,8},{7,9},{4,1... | collective-permute-start | bytes 2359304 | tf_op jit(solution)/shard_map/ppermute | solution.py:1129
  389.9 82.7 %collective-permute-start.23 = (bf16[512,768]{1,0:T(8,128)(2,1)S(1)}, bf16[512,768]{1,0:T(8,128)(2,1)}, u32[]{:S(2)}, u32[]{:S(2)}) collective-permute-start(bf16[512,768]{1,0:T(8,128)(2,1)S(1)} %get-tuple-element.172), channel_id=1, source_target_pairs={{0,0},{1,1},{2,2},{3,3},{8,4},{9,5},{10,6},{11,7},{4,8},{5,9},{6,1... | collective-permute-start | bytes 2359304 | tf_op jit(solution)/shard_map/ppermute | solution.py:1129
  394.1 78.6 %collective-permute-start.28 = (bf16[32,768]{1,0:T(8,128)(2,1)S(1)}, bf16[32,768]{1,0:T(8,128)(2,1)S(1)}, u32[]{:S(2)}, u32[]{:S(2)}) collective-permute-start(bf16[32,768]{1,0:T(8,128)(2,1)S(1)} %get-tuple-element.214), channel_id=1, source_target_pairs={{2,0},{3,1},{0,2},{1,3},{10,4},{11,5},{8,6},{9,7},{6,8},{7,9},{4,1... | collective-permute-start | bytes 147464 | tf_op jit(solution)/shard_map/ppermute | solution.py:1129
  396.3 76.3 %collective-permute-start.27 = (bf16[32,768]{1,0:T(8,128)(2,1)S(1)}, bf16[32,768]{1,0:T(8,128)(2,1)S(1)}, u32[]{:S(2)}, u32[]{:S(2)}) collective-permute-start(bf16[32,768]{1,0:T(8,128)(2,1)S(1)} %get-tuple-element.215), channel_id=1, source_target_pairs={{0,0},{1,1},{2,2},{3,3},{8,4},{9,5},{10,6},{11,7},{4,8},{5,9},{6,1... | collective-permute-start | bytes 147464 | tf_op jit(solution)/shard_map/ppermute | solution.py:1129
  476.0 50.4 %collective-permute-start.32 = (bf16[1024,768]{1,0:T(8,128)(2,1)}, bf16[1024,768]{1,0:T(8,128)(2,1)S(1)}, u32[]{:S(2)}, u32[]{:S(2)}) collective-permute-start(bf16[1024,768]{1,0:T(8,128)(2,1)} %get-tuple-element.127), channel_id=1, source_target_pairs={{0,8},{1,9},{2,10},{3,11},{4,12},{5,13},{6,14},{7,15},{8,0},{9,1},... | collective-permute-start | bytes 4718600 | tf_op jit(solution)/shard_map/ppermute | solution.py:1129
  494.4 31.5 %collective-permute-start.30 = (bf16[1,2,4,2,24,576]{5,4,3,2,1,0:T(8,128)(2,1)S(1)}, bf16[1,2,4,2,24,576]{5,4,3,2,1,0:T(8,128)(2,1)S(1)}, u32[]{:S(2)}, u32[]{:S(2)}) collective-permute-start(bf16[1,2,4,2,24,576]{5,4,3,2,1,0:T(8,128)(2,1)S(1)} %dynamic-slice_bitcast_fusion), channel_id=1, source_target_pairs={{0,16},{1,17},{2,18},{3,19},{4,20},{5,21},{6,22},{7,23},{8,24},{9,... | collective-permute-start | bytes 1327112 | tf_op jit(solution)/shard_map/ppermute | solution.py:1129
  505.8 27.4 %collective-permute-start.35 = (bf16[512,768]{1,0:T(8,128)(2,1)S(1)}, bf16[512,768]{1,0:T(8,128)(2,1)}, u32[]{:S(2)}, u32[]{:S(2)}) collective-permute-start(bf16[512,768]{1,0:T(8,128)(2,1)S(1)} %get-tuple-element.167), channel_id=1, source_target_pairs={{0,1},{1,0},{2,3},{3,2},{4,5},{5,4},{6,7},{7,6},{8,9},{9,8},{10,11... | collective-permute-start | bytes 2359304 | tf_op jit(solution)/shard_map/ppermute | solution.py:1129
  506.2 42.6 %collective-permute-start.33 = (bf16[512,768]{1,0:T(8,128)(2,1)}, bf16[512,768]{1,0:T(8,128)(2,1)}, u32[]{:S(2)}, u32[]{:S(2)}) collective-permute-start(bf16[512,768]{1,0:T(8,128)(2,1)} %get-tuple-element.168), channel_id=1, source_target_pairs={{0,1},{1,0},{2,3},{3,2},{4,5},{5,4},{6,7},{7,6},{8,9},{9,8},{10,11... | collective-permute-start | bytes 2359304 | tf_op jit(solution)/shard_map/ppermute | solution.py:1129
  526.1 31.6 %collective-permute-start.31 = (bf16[2,2,2,24,576]{4,3,2,1,0:T(8,128)(2,1)S(1)}, bf16[2,2,2,24,576]{4,3,2,1,0:T(8,128)(2,1)S(1)}, u32[]{:S(2)}, u32[]{:S(2)}) collective-permute-start(bf16[2,2,2,24,576]{4,3,2,1,0:T(8,128)(2,1)S(1)} %dynamic-slice_bitcast_fusion.1), channel_id=1, source_target_pairs={{0,2},{1,3},{2,0},{3,1},{4,6},{5,7},{6,4},{7,5},{8,10},{9,11},{10,... | collective-permute-start | bytes 663560 | tf_op jit(solution)/shard_map/ppermute | solution.py:1129
  564.1 29.8 %collective-permute-start.34 = (bf16[512,768]{1,0:T(8,128)(2,1)}, bf16[512,768]{1,0:T(8,128)(2,1)S(1)}, u32[]{:S(2)}, u32[]{:S(2)}) collective-permute-start(bf16[512,768]{1,0:T(8,128)(2,1)} %get-tuple-element.131), channel_id=1, source_target_pairs={{0,0},{1,1},{2,2},{3,3},{8,4},{9,5},{10,6},{11,7},{4,8},{5,9},{6,1... | collective-permute-start | bytes 2359304 | tf_op jit(solution)/shard_map/ppermute | solution.py:1129
  567.2 36.4 %collective-permute-start.36 = (bf16[512,768]{1,0:T(8,128)(2,1)S(1)}, bf16[512,768]{1,0:T(8,128)(2,1)S(1)}, u32[]{:S(2)}, u32[]{:S(2)}) collective-permute-start(bf16[512,768]{1,0:T(8,128)(2,1)S(1)} %copy-done.20), channel_id=1, source_target_pairs={{2,0},{3,1},{0,2},{1,3},{10,4},{11,5},{8,6},{9,7},{6,8},{7,9},{4,1... | collective-permute-start | bytes 2359304 | tf_op jit(solution)/shard_map/ppermute | solution.py:1129
  (55 other events, 491.6 us)
Sparse Core Ops, SparseCore 0:
  108.9 138.6 all-gather.2
  386.3 181.7 reduce-scatter.1

commit v5 on v4

--- a/solution.py
+++ b/solution.py
@@ -1203,7 +1203,7 @@
         + [up_weight[:, j * width : (j + 1) * width] for j in range(tiles)]
         + [self_out, cross_in[0], cross_in[1], cross_in[2], cross_out]
     )
-    dense, w2, *across = lax.optimization_barrier((dense, w2, *across))
+    dense, w2, across[0] = lax.optimization_barrier((dense, w2, across[0]))
     dense = lax.all_gather(dense, AXES, axis=0)
     far = [send(v, flip(2)) for v in across]
     out_grad, far[1] = lax.optimization_barrier((out_grad, far[1]))

time: 624 us -> 596 us (0.955)
  waiting for transfers between devices: 199 us -> 169 us
  starting transfers between devices: 61.6 us -> 69.3 us
    all_gather x1, waiting for transfers between devices: 44.7 us -> 4.36 us  [home_body(): dense = lax.all_gather(dense, AXES, axis=0)]
    ppermute x51, waiting for transfers between devices: 154 us -> 165 us  [send(): return lax.ppermute(v, AXES, device_pairs(dp_count, move, back))]
    ppermute x51, starting transfers between devices: 61.5 us -> 69.2 us  [send(): return lax.ppermute(v, AXES, device_pairs(dp_count, move, back))]
where the time goes in v5:
time: 596 us; the launch traced here: 590 us
  Pallas kernels  248 us (42%)
  waiting for transfers between devices  169 us (28%)
  starting transfers between devices  69.3 us (12%)
  local copies, waits for them, and re-layouts  65 us (11%)
  other arithmetic  23 us (4%)
  between operations  15.3 us (3%)
    ppermute x51, waiting for transfers between devices, send(): return lax.ppermute(v, AXES, device_pairs(dp_count, move, back))  165 us
    pallas_call x1, Pallas kernels, attend_back_call(): pl.pallas_call(attend_back_kernel, grid_spec=pltpu.PrefetchScalarGridSpec...  70.7 us
    ppermute x51, starting transfers between devices, send(): return lax.ppermute(v, AXES, device_pairs(dp_count, move, back))  69.2 us
    pallas_call x1, Pallas kernels, attend_call(): pl.pallas_call(attend_kernel, grid_spec=pltpu.PrefetchScalarGridSpec(num_...  44.3 us
    pallas_call x1, Pallas kernels, feed_call(): pl.pallas_call(feed_kernel, grid=(tiles,), in_specs=[whole(n3.shape), who...  43 us
    pallas_call x1, Pallas kernels, mid_back_call(): pl.pallas_call(mid_back_kernel, grid_spec=pltpu.PrefetchScalarGridSpec(nu...  34.7 us
    unnamed x80, local copies, waits for them, and re-layouts  25.4 us
    pallas_call x1, Pallas kernels, mid_call(): pl.pallas_call(mid_kernel, grid_spec=pltpu.PrefetchScalarGridSpec(num_sca...  20 us
  transfers between devices with their start and end apart: 53, of which 26 were waited for; matrix products, arithmetic and copies ran while one was open for 12% of the time, Pallas kernels for 25%

profile of v5, /device:TPU:20, one launch (start us, length us, event | category | flops | bytes accessed | tf_op | source)
XLA Modules:
  0.0 589.6 jit_solution(1227605232504633835)
XLA Ops:
  17.0 5.5 collective-permute-start.5
  23.4 4.8 collective-permute-done.4
  28.3 7.7 %collective-permute-done.6.refs_1_ = bf16[544,768]{1,0:T(8,128)(2,1)} collective-permute-done((bf16[544,768]{1,0:T(8,128)(2,1)S(1)}, bf16[544,768]{1,0:T(8,128)(2,1)}, u32[]{:S(2)}, u32[]{:S(2)}) %collective-permute-start.6) | collective-permute-done | bytes 835616 | tf_op jit(solution)/shard_map/ppermute | solution.py:1129
  36.1 17.9 %collective-permute-done.5.refs_0_ = bf16[544,768]{1,0:T(8,128)(2,1)} collective-permute-done((bf16[544,768]{1,0:T(8,128)(2,1)S(1)}, bf16[544,768]{1,0:T(8,128)(2,1)}, u32[]{:S(2)}, u32[]{:S(2)}) %collective-permute-start.5) | collective-permute-done | bytes 835616 | tf_op jit(solution)/shard_map/ppermute | solution.py:1129
  54.0 13.6 %collective-permute-done.7 = bf16[2,2,2,80,192]{4,3,2,1,0:T(8,128)(2,1)S(1)} collective-permute-done((bf16[2,2,2,80,192]{4,3,2,1,0:T(8,128)(2,1)S(1)}, bf16[2,2,2,80,192]{4,3,2,1,0:T(8,128)(2,1)S(1)}, u32[]{:S(2)}, u32[]{:S(2)}) %collective-permute-start.7) | collective-permute-done | bytes 245792 | tf_op jit(solution)/shard_map/ppermute | solution.py:1129
  73.6 12.4 %collective-permute-done.8 = bf16[2,2,2,2,80,192]{5,4,3,0,2,1:T(8,128)(2,1)S(1)} collective-permute-done((bf16[2,2,2,2,80,192]{5,4,3,0,2,1:T(8,128)(2,1)S(1)}, bf16[2,2,2,2,80,192]{5,4,3,0,2,1:T(8,128)(2,1)S(1)}, u32[]{:S(2)}, u32[]{:S(2)}) %collective-permute-start.8) | collective-permute-done | bytes 491552 | tf_op jit(solution)/shard_map/ppermute | solution.py:1129
  104.5 16.2 %collective-permute-done.10.refs_3_ = bf16[544,768]{1,0:T(8,128)(2,1)} collective-permute-done((bf16[544,768]{1,0:T(8,128)(2,1)}, bf16[544,768]{1,0:T(8,128)(2,1)}, u32[]{:S(2)}, u32[]{:S(2)}) %collective-permute-start.10) | collective-permute-done | bytes 835616 | tf_op jit(solution)/shard_map/ppermute | solution.py:1129
  129.4 17.5 %qkv.1 = (bf16[3,4096,128]{2,1,0:T(8,128)(2,1)}, bf16[3,4096,128]{2,1,0:T(8,128)(2,1)}, bf16[6,64,4096]{2,1,0:T(8,128)(2,1)}, bf16[4096,768]{1,0:T(8,128)(2,1)}) custom-call(s32[128]{0:T(128)} %pad_add_fusion.1.meta, bf16[544,768]{1,0:T(8,128)(2,1)} %collective-permute-done.5.refs_0_, bf16[544,768]{1,0:T(8,128)(2,1)} %collective-permute-done.6.refs_1_, ...), custom_call_target="tpu_custom_call" | custom-call | flops 3623878656 | bytes 20000000 | tf_op jit(solution)/shard_map/qkv/pallas_call | solution.py:517
  147.0 44.3 %attend.1 = (bf16[32,128,192]{2,1,0:T(8,128)(2,1)}, f32[8,4096]{1,0:T(8,128)}) custom-call(s32[128]{0:T(128)} %pad_add_fusion.1.meta, bf16[3,4096,128]{2,1,0:T(8,128)(2,1)} %get-tuple-element.84.q_ref, bf16[3,4096,128]{2,1,0:T(8,128)(2,1)} %get-tuple-element.85.kv_ref, bf16[6,64,4096]{2,1,0:T(8,128)(2,1)} %get-tuple-element.86.tr_ref), custom_call_target="tpu_custom_call" | custom-call | flops 20000000000 | bytes 10000000 | tf_op jit(solution)/shard_map/attend/pallas_call | solution.py:618
  197.8 16.0 %collective-permute-done.18 = bf16[512,768]{1,0:T(8,128)(2,1)S(1)} collective-permute-done((bf16[512,768]{1,0:T(8,128)(2,1)S(1)}, bf16[512,768]{1,0:T(8,128)(2,1)S(1)}, u32[]{:S(2)}, u32[]{:S(2)}) %collective-permute-start.18) | collective-permute-done | bytes 786464 | tf_op jit(solution)/shard_map/ppermute | solution.py:1129
  220.1 4.8 slice.588
  224.9 5.9 fusion.19
  235.2 20.0 %middle.1 = (f32[1024,768]{1,0:T(8,128)}, f32[1024,768]{1,0:T(8,128)}, bf16[1024,768]{1,0:T(8,128)(2,1)}, bf16[1024,768]{1,0:T(8,128)(2,1)}, bf16[1024,768]{1,0:...) custom-call(s32[128]{0:T(128)} %pad_add_fusion.1.meta, ...), custom_call_target="tpu_custom_call" | custom-call | flops 8000000000 | bytes 25000000 | tf_op jit(solution)/shard_map/middle/pallas_call | solution.py:851
  255.2 43.0 %feed.1 = (bf16[1024,768]{1,0:T(8,128)(2,1)}, f32[1024,768]{1,0:T(8,128)}, bf16[4,768,768]{2,1,0:T(8,128)(2,1)}, bf16[4,768,768]{2,1,0:T(8,128)(2,1)}, f32[32,768]{1,0:T(8,128)}, /*index=5*/f32[8,768]{1,0:T(8,128)}) custom-call(bf16[1024,768]{1,0:T(8,128)(2,1)} %get-tuple-element.90.n3_ref, bf16[1024,768]{1,0:T(8,128)(2,1)} %constant_dynamic-update-slice_fusion.20.og_ref, ...), custom_call_target="tpu_custom_call" | custom-call | flops 28991029248 | bytes 35000000 | tf_op jit(solution)/shard_map/feed/pallas_call | solution.py:931
  298.3 34.7 %middle_back.1 = (f32[1024,768]{1,0:T(8,128)}, bf16[1024,192]{1,0:T(8,128)(2,1)}, bf16[1024,192]{1,0:T(8,128)(2,1)}, bf16[1024,192]{1,0:T(8,128)(2,1)}, bf16[102...) custom-call(s32[128]{0:T(128)} %pad_add_fusion.1.meta, ...), custom_call_target="tpu_custom_call" | custom-call | flops 22000001024 | bytes 35000000 | tf_op jit(solution)/shard_map/middle_back/pallas_call | solution.py:1051
  363.9 7.4 %collective-permute-start.23 = (bf16[512,768]{1,0:T(8,128)(2,1)S(1)}, bf16[512,768]{1,0:T(8,128)(2,1)}, u32[]{:S(2)}, u32[]{:S(2)}) collective-permute-start(bf16[512,768]{1,0:T(8,128)(2,1)S(1)} %get-tuple-element.170), channel_id=1, source_target_pairs={{0,0},{1,1},{2,2},{3,3},{8,4},{9,5},{10,6},{11,7},{4,8},{5,9},{6,1... | collective-permute-start | bytes 2359304 | tf_op jit(solution)/shard_map/ppermute | solution.py:1129
  375.5 70.7 %attend_back.1 = (bf16[4096,576]{1,0:T(8,128)(2,1)}, bf16[1024,768]{1,0:T(8,128)(2,1)}, bf16[1024,768]{1,0:T(8,128)(2,1)}, bf16[1024,768]{1,0:T(8,128)(2,1)}, bf16[1024,768]{1,0:T(8,128)(2,1)}) custom-call(s32[128]{0:T(128)} %pad_add_fusion.1.meta, bf16[3,4096,128]{2,1,0:T(8,128)(2,1)} %get-tuple-element.84.q_ref, ...), custom_call_target="tpu_custom_call" | custom-call | flops 49999998976 | bytes 15000000 | tf_op jit(solution)/shard_map/attend_back/pallas_call | solution.py:723
  451.7 9.2 %win.1 = (bf16[768,576]{1,0:T(8,128)(2,1)}, f32[8,576]{1,0:T(8,128)}) custom-call(bf16[4096,768]{1,0:T(8,128)(2,1)} %get-tuple-element.121.n_ref, bf16[4096,576]{1,0:T(8,128)(2,1)} %get-tuple-element.122.d_ref), custom_call_target="tpu_custom_call" | custom-call | flops 3623878656 | bytes 12000000 | tf_op jit(solution)/shard_map/win/pallas_call | solution.py:764
  467.4 9.9 %collective-permute-start.30 = (bf16[1,2,4,2,24,576]{5,4,3,2,1,0:T(8,128)(2,1)S(1)}, bf16[1,2,4,2,24,576]{5,4,3,2,1,0:T(8,128)(2,1)S(1)}, u32[]{:S(2)}, u32[]{:S(2)}) collective-permute-start(bf16[1,2,4,2,24,576]{5,4,3,2,1,0:T(8,128)(2,1)S(1)} %dynamic-slice_bitcast_fusion), channel_id=1, source_target_pairs={{0,16},{1,17},{2,18},{3,19},{4,20},{5,21},{6,22},{7,23},{8,24},{9,... | collective-permute-start | bytes 1327112 | tf_op jit(solution)/shard_map/ppermute | solution.py:1129
  491.4 4.9 collective-permute-done.46
  498.0 6.7 %collective-permute-done.35.c_ref = bf16[512,768]{1,0:T(8,128)(2,1)} collective-permute-done((bf16[512,768]{1,0:T(8,128)(2,1)S(1)}, bf16[512,768]{1,0:T(8,128)(2,1)}, u32[]{:S(2)}, u32[]{:S(2)}) %collective-permute-start.35) | collective-permute-done | bytes 786464 | tf_op jit(solution)/shard_map/ppermute | solution.py:1129
  508.9 11.5 %collective-permute-done.33.c_ref = bf16[512,768]{1,0:T(8,128)(2,1)} collective-permute-done((bf16[512,768]{1,0:T(8,128)(2,1)}, bf16[512,768]{1,0:T(8,128)(2,1)}, u32[]{:S(2)}, u32[]{:S(2)}) %collective-permute-start.33) | collective-permute-done | bytes 786464 | tf_op jit(solution)/shard_map/ppermute | solution.py:1129
  549.8 16.4 %collective-permute-done.34 = bf16[512,768]{1,0:T(8,128)(2,1)S(1)} collective-permute-done((bf16[512,768]{1,0:T(8,128)(2,1)}, bf16[512,768]{1,0:T(8,128)(2,1)S(1)}, u32[]{:S(2)}, u32[]{:S(2)}) %collective-permute-start.34) | collective-permute-done | bytes 786464 | tf_op jit(solution)/shard_map/ppermute | solution.py:1129
  566.2 9.4 %collective-permute-done.36 = bf16[512,768]{1,0:T(8,128)(2,1)S(1)} collective-permute-done((bf16[512,768]{1,0:T(8,128)(2,1)S(1)}, bf16[512,768]{1,0:T(8,128)(2,1)S(1)}, u32[]{:S(2)}, u32[]{:S(2)}) %collective-permute-start.36) | collective-permute-done | bytes 786464 | tf_op jit(solution)/shard_map/ppermute | solution.py:1129
  (319 shorter events, 163.7 us)
Async XLA Ops:
  7.2 212.9 %all-gather.3.cloned.1.call-start = ((), (), s32[]{:S(2)}) async-start(), calls=%async_computation.2 | async-start | bytes 15814656 | tf_op jit(solution)/shard_map/all_gather | solution.py:1207
  17.0 36.9 %collective-permute-start.5 = (bf16[544,768]{1,0:T(8,128)(2,1)S(1)}, bf16[544,768]{1,0:T(8,128)(2,1)}, u32[]{:S(2)}, u32[]{:S(2)}) collective-permute-start(bf16[544,768]{1,0:T(8,128)(2,1)S(1)} %get-tuple-element.162), channel_id=1, source_target_pairs={{0,0},{1,1},{2,2},{3,3},{4,8},{5,9},{6,10},{7,11},{8,4},{9,5},{10,... | collective-permute-start | bytes 2506760 | tf_op jit(solution)/shard_map/ppermute | solution.py:1129
  90.9 486.9 %reduce-scatter.2.cloned.1.call-start = ((), (), s32[]{:S(2)}) async-start(), calls=%async_computation.1 | async-start | bytes 15814656 | tf_op jit(solution)/shard_map/reduce_scatter | solution.py:1249
  94.4 27.8 %collective-permute-start.11 = (bf16[544,768]{1,0:T(8,128)(2,1)}, bf16[544,768]{1,0:T(8,128)(2,1)}, u32[]{:S(2)}, u32[]{:S(2)}) collective-permute-start(bf16[544,768]{1,0:T(8,128)(2,1)} %collective-permute-done.5.refs_0_), channel_id=1, source_target_pairs={{0,8},{1,9},{2,10},{3,11},{4,12},{5,13},{6,14},{7,15},{8,0},{9,1},... | collective-permute-start | bytes 2506760 | tf_op jit(solution)/shard_map/ppermute | solution.py:1129
  95.9 27.2 %collective-permute-start.12 = (bf16[544,768]{1,0:T(8,128)(2,1)}, bf16[544,768]{1,0:T(8,128)(2,1)}, u32[]{:S(2)}, u32[]{:S(2)}) collective-permute-start(bf16[544,768]{1,0:T(8,128)(2,1)} %collective-permute-done.6.refs_1_), channel_id=1, source_target_pairs={{0,8},{1,9},{2,10},{3,11},{4,12},{5,13},{6,14},{7,15},{8,0},{9,1},... | collective-permute-start | bytes 2506760 | tf_op jit(solution)/shard_map/ppermute | solution.py:1129
  96.3 24.4 %collective-permute-start.10 = (bf16[544,768]{1,0:T(8,128)(2,1)}, bf16[544,768]{1,0:T(8,128)(2,1)}, u32[]{:S(2)}, u32[]{:S(2)}) collective-permute-start(bf16[544,768]{1,0:T(8,128)(2,1)} %collective-permute-done.6.refs_1_), channel_id=1, source_target_pairs={{0,1},{1,0},{2,3},{3,2},{4,5},{5,4},{6,7},{7,6},{8,9},{9,8},{10,11... | collective-permute-start | bytes 2506760 | tf_op jit(solution)/shard_map/ppermute | solution.py:1129
  104.5 25.0 %collective-permute-start.13 = (bf16[544,768]{1,0:T(8,128)(2,1)}, bf16[544,768]{1,0:T(8,128)(2,1)}, u32[]{:S(2)}, u32[]{:S(2)}) collective-permute-start(bf16[544,768]{1,0:T(8,128)(2,1)} %collective-permute-done.9.refs_2_), channel_id=1, source_target_pairs={{0,8},{1,9},{2,10},{3,11},{4,12},{5,13},{6,14},{7,15},{8,0},{9,1},... | collective-permute-start | bytes 2506760 | tf_op jit(solution)/shard_map/ppermute | solution.py:1129
  124.0 90.7 %collective-permute-start.19 = (bf16[512,768]{1,0:T(8,128)(2,1)S(1)}, bf16[512,768]{1,0:T(8,128)(2,1)S(1)}, u32[]{:S(2)}, u32[]{:S(2)}) collective-permute-start(bf16[512,768]{1,0:T(8,128)(2,1)S(1)} %get-tuple-element.171), channel_id=1, source_target_pairs={{0,2},{1,3},{2,0},{3,1},{4,10},{5,11},{6,8},{7,9},{8,6},{9,7},{10,... | collective-permute-start | bytes 2359304 | tf_op jit(solution)/shard_map/ppermute | solution.py:1129
  126.8 87.0 %collective-permute-start.18 = (bf16[512,768]{1,0:T(8,128)(2,1)S(1)}, bf16[512,768]{1,0:T(8,128)(2,1)S(1)}, u32[]{:S(2)}, u32[]{:S(2)}) collective-permute-start(bf16[512,768]{1,0:T(8,128)(2,1)S(1)} %get-tuple-element.172), channel_id=1, source_target_pairs={{0,0},{1,1},{2,2},{3,3},{4,8},{5,9},{6,10},{7,11},{8,4},{9,5},{10,... | collective-permute-start | bytes 2359304 | tf_op jit(solution)/shard_map/ppermute | solution.py:1129
  194.0 41.2 %collective-permute-start.16 = (bf16[1024,192]{1,0:T(8,128)(2,1)}, bf16[1024,192]{1,0:T(8,128)(2,1)}, u32[]{:S(2)}, u32[]{:S(2)}) collective-permute-start(bf16[1024,192]{1,0:T(8,128)(2,1)} %bitcast.36), channel_id=1, source_target_pairs={{0,8},{1,9},{2,10},{3,11},{4,12},{5,13},{6,14},{7,15},{8,0},{9,1},... | collective-permute-start | bytes 1179656 | tf_op jit(solution)/shard_map/ppermute | solution.py:1129
  194.0 41.2 %collective-permute-start.17 = (bf16[1024,192]{1,0:T(8,128)(2,1)}, bf16[1024,192]{1,0:T(8,128)(2,1)}, u32[]{:S(2)}, u32[]{:S(2)}) collective-permute-start(bf16[1024,192]{1,0:T(8,128)(2,1)} %bitcast.37), channel_id=1, source_target_pairs={{0,9},{1,8},{2,11},{3,10},{4,13},{5,12},{6,15},{7,14},{8,1},{9,0},... | collective-permute-start | bytes 1179656 | tf_op jit(solution)/shard_map/ppermute | solution.py:1129
  195.7 39.5 %collective-permute-start.15 = (bf16[1024,192]{1,0:T(8,128)(2,1)S(1)}, bf16[1024,192]{1,0:T(8,128)(2,1)}, u32[]{:S(2)}, u32[]{:S(2)}) collective-permute-start(bf16[1024,192]{1,0:T(8,128)(2,1)S(1)} %bitcast.220), channel_id=1, source_target_pairs={{0,1},{1,0},{2,3},{3,2},{4,5},{5,4},{6,7},{7,6},{8,9},{9,8},{10,11... | collective-permute-start | bytes 1179656 | tf_op jit(solution)/shard_map/ppermute | solution.py:1129
  333.9 23.0 %collective-permute-start.22 = (bf16[1024,192]{1,0:T(8,128)(2,1)}, bf16[1024,192]{1,0:T(8,128)(2,1)S(1)}, u32[]{:S(2)}, u32[]{:S(2)}) collective-permute-start(bf16[1024,192]{1,0:T(8,128)(2,1)} %get-tuple-element.109), channel_id=1, source_target_pairs={{0,9},{1,8},{2,11},{3,10},{4,13},{5,12},{6,15},{7,14},{8,1},{9,0},... | collective-permute-start | bytes 1179656 | tf_op jit(solution)/shard_map/ppermute | solution.py:1129
  362.2 84.1 %collective-permute-start.24 = (bf16[512,768]{1,0:T(8,128)(2,1)S(1)}, bf16[512,768]{1,0:T(8,128)(2,1)S(1)}, u32[]{:S(2)}, u32[]{:S(2)}) collective-permute-start(bf16[512,768]{1,0:T(8,128)(2,1)S(1)} %get-tuple-element.169), channel_id=1, source_target_pairs={{2,0},{3,1},{0,2},{1,3},{10,4},{11,5},{8,6},{9,7},{6,8},{7,9},{4,1... | collective-permute-start | bytes 2359304 | tf_op jit(solution)/shard_map/ppermute | solution.py:1129
  363.9 82.4 %collective-permute-start.23 = (bf16[512,768]{1,0:T(8,128)(2,1)S(1)}, bf16[512,768]{1,0:T(8,128)(2,1)}, u32[]{:S(2)}, u32[]{:S(2)}) collective-permute-start(bf16[512,768]{1,0:T(8,128)(2,1)S(1)} %get-tuple-element.170), channel_id=1, source_target_pairs={{0,0},{1,1},{2,2},{3,3},{8,4},{9,5},{10,6},{11,7},{4,8},{5,9},{6,1... | collective-permute-start | bytes 2359304 | tf_op jit(solution)/shard_map/ppermute | solution.py:1129
  371.4 74.8 %collective-permute-start.28 = (bf16[32,768]{1,0:T(8,128)(2,1)S(1)}, bf16[32,768]{1,0:T(8,128)(2,1)S(1)}, u32[]{:S(2)}, u32[]{:S(2)}) collective-permute-start(bf16[32,768]{1,0:T(8,128)(2,1)S(1)} %get-tuple-element.212), channel_id=1, source_target_pairs={{2,0},{3,1},{0,2},{1,3},{10,4},{11,5},{8,6},{9,7},{6,8},{7,9},{4,1... | collective-permute-start | bytes 147464 | tf_op jit(solution)/shard_map/ppermute | solution.py:1129
  372.6 73.7 %collective-permute-start.27 = (bf16[32,768]{1,0:T(8,128)(2,1)S(1)}, bf16[32,768]{1,0:T(8,128)(2,1)S(1)}, u32[]{:S(2)}, u32[]{:S(2)}) collective-permute-start(bf16[32,768]{1,0:T(8,128)(2,1)S(1)} %get-tuple-element.213), channel_id=1, source_target_pairs={{0,0},{1,1},{2,2},{3,3},{8,4},{9,5},{10,6},{11,7},{4,8},{5,9},{6,1... | collective-permute-start | bytes 147464 | tf_op jit(solution)/shard_map/ppermute | solution.py:1129
  449.7 48.4 %collective-permute-start.32 = (bf16[1024,768]{1,0:T(8,128)(2,1)}, bf16[1024,768]{1,0:T(8,128)(2,1)S(1)}, u32[]{:S(2)}, u32[]{:S(2)}) collective-permute-start(bf16[1024,768]{1,0:T(8,128)(2,1)} %get-tuple-element.125), channel_id=1, source_target_pairs={{0,8},{1,9},{2,10},{3,11},{4,12},{5,13},{6,14},{7,15},{8,0},{9,1},... | collective-permute-start | bytes 4718600 | tf_op jit(solution)/shard_map/ppermute | solution.py:1129
  467.4 28.9 %collective-permute-start.30 = (bf16[1,2,4,2,24,576]{5,4,3,2,1,0:T(8,128)(2,1)S(1)}, bf16[1,2,4,2,24,576]{5,4,3,2,1,0:T(8,128)(2,1)S(1)}, u32[]{:S(2)}, u32[]{:S(2)}) collective-permute-start(bf16[1,2,4,2,24,576]{5,4,3,2,1,0:T(8,128)(2,1)S(1)} %dynamic-slice_bitcast_fusion), channel_id=1, source_target_pairs={{0,16},{1,17},{2,18},{3,19},{4,20},{5,21},{6,22},{7,23},{8,24},{9,... | collective-permute-start | bytes 1327112 | tf_op jit(solution)/shard_map/ppermute | solution.py:1129
  477.3 27.4 %collective-permute-start.35 = (bf16[512,768]{1,0:T(8,128)(2,1)S(1)}, bf16[512,768]{1,0:T(8,128)(2,1)}, u32[]{:S(2)}, u32[]{:S(2)}) collective-permute-start(bf16[512,768]{1,0:T(8,128)(2,1)S(1)} %get-tuple-element.165), channel_id=1, source_target_pairs={{0,1},{1,0},{2,3},{3,2},{4,5},{5,4},{6,7},{7,6},{8,9},{9,8},{10,11... | collective-permute-start | bytes 2359304 | tf_op jit(solution)/shard_map/ppermute | solution.py:1129
  478.2 42.3 %collective-permute-start.33 = (bf16[512,768]{1,0:T(8,128)(2,1)}, bf16[512,768]{1,0:T(8,128)(2,1)}, u32[]{:S(2)}, u32[]{:S(2)}) collective-permute-start(bf16[512,768]{1,0:T(8,128)(2,1)} %get-tuple-element.166), channel_id=1, source_target_pairs={{0,1},{1,0},{2,3},{3,2},{4,5},{5,4},{6,7},{7,6},{8,9},{9,8},{10,11... | collective-permute-start | bytes 2359304 | tf_op jit(solution)/shard_map/ppermute | solution.py:1129
  496.5 32.8 %collective-permute-start.31 = (bf16[2,2,2,24,576]{4,3,2,1,0:T(8,128)(2,1)S(1)}, bf16[2,2,2,24,576]{4,3,2,1,0:T(8,128)(2,1)S(1)}, u32[]{:S(2)}, u32[]{:S(2)}) collective-permute-start(bf16[2,2,2,24,576]{4,3,2,1,0:T(8,128)(2,1)S(1)} %dynamic-slice_bitcast_fusion.1), channel_id=1, source_target_pairs={{0,2},{1,3},{2,0},{3,1},{4,6},{5,7},{6,4},{7,5},{8,10},{9,11},{10,... | collective-permute-start | bytes 663560 | tf_op jit(solution)/shard_map/ppermute | solution.py:1129
  537.7 28.5 %collective-permute-start.34 = (bf16[512,768]{1,0:T(8,128)(2,1)}, bf16[512,768]{1,0:T(8,128)(2,1)S(1)}, u32[]{:S(2)}, u32[]{:S(2)}) collective-permute-start(bf16[512,768]{1,0:T(8,128)(2,1)} %get-tuple-element.129), channel_id=1, source_target_pairs={{0,0},{1,1},{2,2},{3,3},{8,4},{9,5},{10,6},{11,7},{4,8},{5,9},{6,1... | collective-permute-start | bytes 2359304 | tf_op jit(solution)/shard_map/ppermute | solution.py:1129
  539.6 36.1 %collective-permute-start.36 = (bf16[512,768]{1,0:T(8,128)(2,1)S(1)}, bf16[512,768]{1,0:T(8,128)(2,1)S(1)}, u32[]{:S(2)}, u32[]{:S(2)}) collective-permute-start(bf16[512,768]{1,0:T(8,128)(2,1)S(1)} %copy-done.20), channel_id=1, source_target_pairs={{2,0},{3,1},{0,2},{1,3},{10,4},{11,5},{8,6},{9,7},{6,8},{7,9},{4,1... | collective-permute-start | bytes 2359304 | tf_op jit(solution)/shard_map/ppermute | solution.py:1129
  (55 other events, 521.5 us)
Sparse Core Ops, SparseCore 0:
  91.0 129.0 all-gather.2
  357.8 182.2 reduce-scatter.1
